TPU v7x, 32 devices: a whole 2x2x4 slice. The times are simulated.
32 devices in a mesh: tm: 4 (over x, core), space: 8 (over z, y).
Axes of the slice: x: 2, y: 2, z: 4, core: 2. Of those that a mesh axis runs over, the one named last changes fastest.
Arguments:
- video_in: bfloat16 [16, 8, 16, 3072], P('tm', 'space'), may hold values from -6 to 6
- neighbours: int32 [8, 8], replicated, may hold values from 0 to 8, as said below
- valid_frames: int32 [8], replicated, may hold values from 0 to 16, as said below
- norm1_gain: float32 [192], replicated, may hold values from 0.1 to 1.9
- conv1_weight: bfloat16 [9, 576, 192], replicated, may hold values from -0.078125 to 0.078125
- conv1_bias: float32 [192], replicated, may hold values from -3 to 3
- norm2_gain: float32 [192], replicated, may hold values from 0.1 to 1.9
- conv2_weight: bfloat16 [9, 576, 192], replicated, may hold values from -0.078125 to 0.078125
- conv2_bias: float32 [192], replicated, may hold values from -3 to 3
Outputs:
- block_out: bfloat16 [16, 8, 16, 3072], P('tm', 'space')
Inputs may be any that keep to these rules, and one draw needn't show every extreme that they name: `neighbours`: entry k of a tile's row names the tile beside it in direction k of one placement of all tiles on a grid of 1 row by 8 columns, directions ordered (row, column) = (-1,-1), (-1,0), (-1,1), (0,-1), (0,1), (1,-1), (1,0), (1,1); 8 where that place lies outside the grid. `valid_frames`: frames from this number on are padding in that tile's track.
All inputs are finite; a program needn't handle non-finite values.
Results may differ from a plain program's by a relative error of at most 0.0037.
Values may be sent and summed in bfloat16 or wider, within the bound.
No kernel may reach another device: no remote copies, remote signals or barrier semaphores. Data moves between devices by JAX's collectives and lax.ppermute only.
A program may use at most 64 MiB of HBM per device.

v0:
```python
from functools import partial

import jax
import jax.numpy as jnp
from jax import lax
from jax.sharding import PartitionSpec as P

epsilon = 1e-06


def shifted(value, axis, steps):
    count = lax.axis_size(axis)
    first, last = (max(0, -steps), min(count, count - steps))
    return lax.ppermute(value, axis, [(source, source + steps) for source in range(first, last)])


def norm_silu(values, scale_gain):
    square = jnp.mean(values * values, axis=-1, keepdims=True)
    return jax.nn.silu(values * lax.rsqrt(square + epsilon) * scale_gain)


def conv_tile(framed, weight):
    frames_out = framed.shape[0] - 2
    side_len = framed.shape[1] - 2
    channels = framed.shape[-1]
    widened = jnp.concatenate(
        [framed[:, :, col_off : col_off + side_len] for col_off in range(3)], axis=-1
    )
    summed = jnp.zeros((frames_out * side_len * side_len, channels), jnp.float32)
    for time_off in range(3):
        for row_off in range(3):
            window = widened[
                time_off : time_off + frames_out, row_off : row_off + side_len
            ].reshape(-1, 3 * channels)
            summed = summed + jnp.dot(
                window, weight[time_off * 3 + row_off], preferred_element_type=jnp.float32
            )
    return summed.reshape(frames_out, side_len, side_len, channels)


def edge_pack(activation):
    return jnp.stack(
        [
            activation[:, :, -1],
            activation[:, :, :, -1],
            activation[:, :, :, 0],
            activation[:, :, 0],
        ],
        axis=2,
    )


def fold_edges(totals, portion, offset, nearby):
    amount = portion.shape[1]
    tile_ids = jnp.arange(amount, dtype=jnp.int32)
    choose = (nearby[:, :, None] == tile_ids[None, None, :]).astype(jnp.bfloat16)
    side_choose = jnp.stack([choose[:, 1], choose[:, 3], choose[:, 4], choose[:, 6]], axis=1)
    corner_choose = jnp.stack([choose[:, 0], choose[:, 2], choose[:, 5], choose[:, 7]], axis=1)
    corner_source = jnp.stack(
        [portion[:, :, 0, -1], portion[:, :, 0, 0], portion[:, :, 3, -1], portion[:, :, 3, 0]],
        axis=2,
    )
    new_sides = jnp.einsum(
        "djn,fnjxc->fdjxc", side_choose, portion, preferred_element_type=jnp.float32
    )
    new_corners = jnp.einsum(
        "djn,fnjc->fdjc", corner_choose, corner_source, preferred_element_type=jnp.float32
    )
    return (new_sides.astype(jnp.bfloat16), new_corners.astype(jnp.bfloat16))


def empty_rims(frame_count, activation):
    tiles_dev, side_len, channels = (activation.shape[1], activation.shape[2], activation.shape[4])
    return (
        jnp.zeros((frame_count, tiles_dev, 4, side_len, channels), jnp.bfloat16),
        jnp.zeros((frame_count, tiles_dev, 4, channels), jnp.bfloat16),
    )


def assemble(longer, side_rims, corners):
    top_row = jnp.concatenate([corners[:, :, 0:1], side_rims[:, :, 0], corners[:, :, 1:2]], axis=2)
    bottom_row = jnp.concatenate(
        [corners[:, :, 2:3], side_rims[:, :, 3], corners[:, :, 3:4]], axis=2
    )
    middle = jnp.concatenate(
        [side_rims[:, :, 1][:, :, :, None], longer, side_rims[:, :, 2][:, :, :, None]], axis=3
    )
    return jnp.concatenate([top_row[:, :, None], middle, bottom_row[:, :, None]], axis=2)


def extend(activation, nearby):
    frames_dev = activation.shape[0]
    folder = partial(fold_edges, nearby=nearby)
    side_rims, corners = folder(
        empty_rims(frames_dev, activation),
        lax.all_gather(edge_pack(activation), "space", axis=1, tiled=True),
        jnp.int32(0),
    )
    prev_act, prev_sides, prev_corners = shifted(
        (activation[frames_dev - 2 :], side_rims[frames_dev - 2 :], corners[frames_dev - 2 :]),
        "tm",
        1,
    )
    longer = jnp.concatenate([prev_act, activation], axis=0)
    side_rims = jnp.concatenate([prev_sides, side_rims], axis=0)
    corners = jnp.concatenate([prev_corners, corners], axis=0)
    return assemble(longer, side_rims, corners)


def blank_tile(pieces, tile_valid):
    framed = pieces[0]
    return jnp.zeros(
        (framed.shape[0] - 2, framed.shape[1] - 2, framed.shape[2] - 2, framed.shape[3]),
        jnp.bfloat16,
    )


def home_tiles(inputs, home_valid, first_frame, worker):
    pieces = tuple((stacked[:, 0] for stacked in inputs))
    results = [lax.cond(home_valid[0] > first_frame, worker, blank_tile, pieces, home_valid[0])]
    return jnp.stack(results, axis=1)


def on_device(
    video_in,
    neighbours,
    valid_frames,
    norm1_gain,
    conv1_weight,
    conv1_bias,
    norm2_gain,
    conv2_weight,
    conv2_bias,
):
    frames_dev, tiles_dev, side_len, merged = video_in.shape
    channels = norm1_gain.shape[0]
    voxels = video_in.reshape(frames_dev, tiles_dev, side_len, side_len, channels)
    first_frame = lax.axis_index("tm") * frames_dev
    home_ids = lax.axis_index("space") * tiles_dev + jnp.arange(tiles_dev, dtype=jnp.int32)
    home_valid = jnp.take(valid_frames, home_ids)
    nearby = jnp.take(neighbours, home_ids, axis=0)
    frame_pos = first_frame + jnp.arange(frames_dev, dtype=jnp.int32)
    present = (frame_pos[:, None] < home_valid[None, :]).astype(jnp.bfloat16)
    masked = voxels * present[:, :, None, None, None]
    activation = norm_silu(masked.astype(jnp.float32), norm1_gain).astype(jnp.bfloat16)

    def frame_weights(tile_valid):
        return (frame_pos < tile_valid).astype(jnp.float32)[:, None, None, None]

    def first_worker(pieces, tile_valid):
        summed = conv_tile(pieces[0], conv1_weight)
        return norm_silu((summed + conv1_bias) * frame_weights(tile_valid), norm2_gain).astype(
            jnp.bfloat16
        )

    def second_worker(pieces, tile_valid):
        summed = conv_tile(pieces[0], conv2_weight)
        return (
            (summed + conv2_bias) * frame_weights(tile_valid) + pieces[1].astype(jnp.float32)
        ).astype(jnp.bfloat16)

    padded = extend(activation, nearby)
    hidden = home_tiles((padded,), home_valid, first_frame, first_worker)
    padded = extend(hidden, nearby)
    block_out = home_tiles((padded, masked), home_valid, first_frame, second_worker)
    return block_out.reshape(frames_dev, tiles_dev, side_len, side_len * channels)


def solution(mesh):
    in_specs = (P("tm", "space", None, None), P(), P(), P(), P(), P(), P(), P(), P())
    out_specs = P("tm", "space", None, None)
    return jax.shard_map(
        on_device, mesh=mesh, in_specs=in_specs, out_specs=out_specs, check_vma=False
    )
```

profile of v0, /device:TPU:0, one launch (start us, length us, event | category | flops | bytes accessed | tf_op | source)
XLA Modules:
  0.0 147.2 jit_solution(2349354967583737358)
XLA Ops:
  0.0 1.6 %reshape.252 = bf16[4,1,16,16,192]{4,3,2,0,1:T(8,128)(2,1)S(1)} reshape(bf16[4,1,16,3072]{3,2,1,0:T(8,128)(2,1)} %param.13) | data formatting | bytes 786432 | tf_op jit(solution)/shard_map/reshape | solution.py:137
  1.6 1.2 dynamic-slice.5
  3.7 0.4 fusion.9
  4.4 34.6 %all_gather.6 = bf16[4,8,4,16,192]{4,3,2,0,1:T(8,128)(2,1)S(1)} all-gather(bf16[4,1,4,16,192]{4,3,2,0,1:T(8,128)(2,1)S(1)} %pad_maximum_fusion.4), channel_id=1, replica_groups=mesh['tm'=4,'space'=8] {'space'}, dimensions={1}, use_global_device_ids=true | all-gather | bytes 884736 | tf_op jit(solution)/shard_map/all_gather | solution.py:96
  39.1 0.7 fusion.69
  40.1 1.3 collective-permute-start
  41.4 0.7 fusion.12
  42.2 4.1 %collective-permute-start.1 = (bf16[2,1,4,16,192]{4,3,0,2,1:T(8,128)(2,1)S(1)}, bf16[2,1,4,16,192]{4,3,0,2,1:T(8,128)(2,1)S(1)}, u32[]{:S(2)}, u32[]{:S(2)}) collective-permute-start(bf16[2,1,4,16,192]{4,3,0,2,1:T(8,128)(2,1)S(1)} %slice.385), channel_id=1, source_target_pairs={{0,8},{8,16},{16,24},{1,9},{9,17},{17,25},{2,10},{10,18},{18,26},{... | collective-permute-start | bytes 147464 | tf_op jit(solution)/shard_map/ppermute | solution.py:14
  46.4 1.9 %collective-permute-start.2 = (bf16[2,1,16,16,192]{4,3,2,0,1:T(8,128)(2,1)S(1)}, bf16[2,1,16,16,192]{4,3,2,0,1:T(8,128)(2,1)S(1)}, u32[]{:S(2)}, u32[]{:S(2)}) collective-permute-start(bf16[2,1,16,16,192]{4,3,2,0,1:T(8,128)(2,1)S(1)} %slice.392), channel_id=1, source_target_pairs={{0,8},{8,16},{16,24},{1,9},{9,17},{17,25},{2,10},{10,18},{18,26},{... | collective-permute-start | bytes 589832 | tf_op jit(solution)/shard_map/ppermute | solution.py:14
  48.7 0.7 collective-permute-done.2
  49.5 0.9 pad_maximum_fusion.2
  50.3 24.7 %conditional.2 = (bf16[4,16,16,192]{3,2,1,0:T(8,128)(2,1)S(1)}) conditional(s32[]{:T(128)} %convert_element_type.107, () %tuple.20, (bf16[6,1,18,18,192]{4,3,2,0,1:T(8,128)(2,1)S(1)}, bf16[9,576,192]{1,2,0:T(8,128)(2,1)}, f32[192]{0:T(256)S(1)}, s32[]{:T(128)}, s32[4]{0:T(128)S(1)}, /*index=5*/f32[192]{0:T(256)S(1)}) %tuple.102), branch_computations={%region_1.2_spmd, %region_2.4_spmd} | conditional | flops 2048533504 | bytes 96561936 | solution.py:120
  50.4 0.7 fusion.73
  51.1 0.9 pad_maximum_fusion
  51.9 4.4 %fusion.72 = (bf16[4,16,16,576]{3,2,1,0:T(8,128)(2,1)}, bf16[4,16,16,576]{3,2,1,0:T(8,128)(2,1)}, bf16[4,16,16,576]{3,2,1,0:T(8,128)(2,1)}, bf16[4,16,16,576]{3,...) fusion(bf16[6,18,16,576]{3,2,1,0:T(8,128)(2,1)S(1)} %pad_maximu, ...), kind=kLoop, calls=%fused_computation.174 | loop fusion | bytes 21233664 | tf_op jit(solution)/shard_map/cond/branch_1_fun/slice | solution.py:32
  56.3 4.1 %copy.179 = bf16[9,576,192]{2,1,0:T(8,128)(2,1)S(1)} copy(bf16[9,576,192]{1,2,0:T(8,128)(2,1)} %get-tuple-element.168) | data formatting | bytes 3981312 | tf_op jit(solution)/shard_map
  60.4 2.0 %fusion = f32[1024,192]{0,1:T(8,128)S(1)} fusion(bf16[1024,576]{1,0:T(8,128)(2,1)} %bitcast.249, bf16[9,576,192]{2,1,0:T(8,128)(2,1)S(1)} %copy.179), kind=kOutput, calls=%fused_computation.20 | convolution fusion | flops 226492416 | bytes 2260992 | tf_op jit(solution)/shard_map/cond/branch_1_fun/dot_general | solution.py:35
  62.5 0.6 convolution_add_fusion.7
  63.1 0.7 copy-done.11
  63.8 0.6 convolution_add_fusion.6
  64.4 0.7 copy-done.9
  65.1 0.6 convolution_add_fusion.5
  65.7 0.7 copy-done.7
  66.4 0.6 convolution_add_fusion.4
  67.1 0.7 copy-done.5
  67.8 0.6 convolution_add_fusion.3
  68.4 0.7 copy-done.3
  69.1 0.6 convolution_add_fusion.2
  69.7 0.7 copy-done.1
  70.4 1.5 %convolution_add_fusion.1 = f32[1024,192]{0,1:T(8,128)} fusion(f32[1024,192]{0,1:T(8,128)S(1)} %convolution_add_fusion.2, bf16[1024,576]{1,0:T(8,128)(2,1)S(1)} %bitcast.235, bf16[9,576,192]{2,1,0:T(8,128)(2,1)S(1)} %copy.179), kind=kOutput, calls=%fused_computation.2 | convolution fusion | flops 226689024 | bytes 3178496 | tf_op jit(solution)/shard_map/cond/branch_1_fun/dot_general | solution.py:35
  72.0 2.2 %multiply_reduce_fusion = (f32[1024]{0:T(1024)S(1)}, f32[1024,192]{0,1:T(8,128)S(1)}) fusion(f32[1024]{0:T(1024)S(1)} %mul.124, f32[192]{0:T(256)S(1)} %get-tuple-element.60, f32[1024,192]{0,1:T(8,128)} %convolution_add_fusion.1, bf16[1024,576]{1,0:T(8,128)(2,1)} %bitcast.233, bf16[9,576,192]{2,1,0:T(8,128)(2,1)S(1)} %copy.179), kind=kOutput, calls=%fused_computation.10 | convolution fusion | flops 227474432 | bytes 3056640 | tf_op jit(solution)/shard_map/cond/branch_1_fun/dot_general | solution.py:35
  74.2 0.3 copy.167
  74.7 0.4 multiply_convert_fusion
  75.3 34.3 %all_gather.7 = bf16[4,8,4,16,192]{4,3,2,0,1:T(8,128)(2,1)S(1)} all-gather(bf16[4,1,4,16,192]{4,3,2,0,1:T(8,128)(2,1)S(1)} %pad_maximum_fusion.5), channel_id=1, replica_groups=mesh['tm'=4,'space'=8] {'space'}, dimensions={1}, use_global_device_ids=true | all-gather | bytes 884736 | tf_op jit(solution)/shard_map/all_gather | solution.py:96
  109.7 0.7 fusion.10
  110.7 1.3 collective-permute-start.3
  112.0 6.9 %collective-permute-start.4 = (bf16[2,1,4,16,192]{4,3,0,2,1:T(8,128)(2,1)S(1)}, bf16[2,1,4,16,192]{4,3,0,2,1:T(8,128)(2,1)S(1)}, u32[]{:S(2)}, u32[]{:S(2)}) collective-permute-start(bf16[2,1,4,16,192]{4,3,0,2,1:T(8,128)(2,1)S(1)} %slice.408), channel_id=1, source_target_pairs={{0,8},{8,16},{16,24},{1,9},{9,17},{17,25},{2,10},{10,18},{18,26},{... | collective-permute-start | bytes 147464 | tf_op jit(solution)/shard_map/ppermute | solution.py:14
  119.0 1.9 %collective-permute-start.5 = (bf16[2,1,16,16,192]{4,3,2,0,1:T(8,128)(2,1)S(1)}, bf16[2,1,16,16,192]{4,3,2,0,1:T(8,128)(2,1)S(1)}, u32[]{:S(2)}, u32[]{:S(2)}) collective-permute-start(bf16[2,1,16,16,192]{4,3,2,0,1:T(8,128)(2,1)S(1)} %slice_bitcast_fusion.36), channel_id=1, source_target_pairs={{0,8},{8,16},{16,24},{1,9},{9,17},{17,25},{2,10},{10,18},{18,26},{... | collective-permute-start | bytes 589832 | tf_op jit(solution)/shard_map/ppermute | solution.py:14
  121.3 0.7 collective-permute-done.5
  122.0 0.9 pad_maximum_fusion.3
  122.9 24.3 %conditional.3 = (bf16[4,1,16,3072]{3,2,0,1:T(8,128)(2,1)}) conditional(s32[]{:T(128)} %convert_element_type.107, () %tuple.19, (bf16[6,1,18,18,192]{4,3,2,0,1:T(8,128)(2,1)S(1)}, bf16[9,576,192]{1,2,0:T(8,128)(2,1)}, f32[192]{0:T(256)S(1)}, s32[]{:T(128)}, s32[4]{0:T(128)S(1)}, /*index=5*/bf16[4]{0:T(256)(128)(2,1)S(1)}, ...), branch_computations={%region_4.5_spmd, %region_5.6_spmd} | conditional | flops 2047156224 | bytes 104957008 | solution.py:120
  122.9 0.7 fusion.75
  123.6 0.9 pad_maximum_fusion.1
  124.5 4.4 %fusion.74 = (bf16[4,16,16,576]{3,2,1,0:T(8,128)(2,1)}, bf16[4,16,16,576]{3,2,1,0:T(8,128)(2,1)}, bf16[4,16,16,576]{3,2,1,0:T(8,128)(2,1)}, bf16[4,16,16,576]{3,...) fusion(bf16[6,18,16,576]{3,2,1,0:T(8,128)(2,1)S(1)} %pad_maximu, ...), kind=kLoop, calls=%fused_computation.176 | loop fusion | bytes 21233664 | tf_op jit(solution)/shard_map/cond/branch_1_fun/slice | solution.py:32
  128.9 4.1 %copy.190 = bf16[9,576,192]{2,1,0:T(8,128)(2,1)S(1)} copy(bf16[9,576,192]{1,2,0:T(8,128)(2,1)} %get-tuple-element.174) | data formatting | bytes 3981312 | tf_op jit(solution)/shard_map
  133.0 2.0 %fusion.1 = f32[1024,192]{0,1:T(8,128)S(1)} fusion(bf16[1024,576]{1,0:T(8,128)(2,1)} %bitcast.250, bf16[9,576,192]{2,1,0:T(8,128)(2,1)S(1)} %copy.190), kind=kOutput, calls=%fused_computation.43 | convolution fusion | flops 226492416 | bytes 2260992 | tf_op jit(solution)/shard_map/cond/branch_1_fun/dot_general | solution.py:35
  135.1 0.6 convolution_add_fusion.15
  135.7 0.7 copy-done.12
  136.4 0.6 convolution_add_fusion.14
  137.0 0.7 copy-done.10
  137.7 0.6 convolution_add_fusion.13
  138.3 0.7 copy-done.8
  139.0 0.6 convolution_add_fusion.12
  139.6 0.7 copy-done.6
  140.3 0.6 convolution_add_fusion.11
  140.9 0.7 copy-done.4
  141.6 0.6 convolution_add_fusion.10
  142.3 0.7 copy-done.2
  143.0 0.6 convolution_add_fusion.9
  143.6 0.7 copy-done
  144.3 0.6 convolution_add_fusion.8
  145.2 0.4 reshape.248
  145.7 0.5 copy-done.15
  146.2 0.9 add_convert_fusion
  (91 shorter events, 2.8 us)
Async XLA Ops:
  0.0 3.7 %copy-start.17 = (f32[192]{0:T(256)S(1)}, f32[192]{0:T(256)}, u32[]{:S(2)}) copy-start(f32[192]{0:T(256)} %param.16) | copy-start | bytes 2308
  40.1 8.2 %collective-permute-start = (bf16[2,1,4,192]{3,2,0,1:T(4,128)(2,1)S(1)}, bf16[2,1,4,192]{3,2,0,1:T(4,128)(2,1)S(1)}, u32[]{:S(2)}, u32[]{:S(2)}) collective-permute-start(bf16[2,1,4,192]{3,2,0,1:T(4,128)(2,1)S(1)} %slice.382), channel_id=1, source_target_pairs={{0,8},{8,16},{16,24},{1,9},{9,17},{17,25},{2,10},{10,18},{18,26},{... | collective-permute-start | bytes 9224 | tf_op jit(solution)/shard_map/ppermute | solution.py:14
  42.2 6.2 %collective-permute-start.1 = (bf16[2,1,4,16,192]{4,3,0,2,1:T(8,128)(2,1)S(1)}, bf16[2,1,4,16,192]{4,3,0,2,1:T(8,128)(2,1)S(1)}, u32[]{:S(2)}, u32[]{:S(2)}) collective-permute-start(bf16[2,1,4,16,192]{4,3,0,2,1:T(8,128)(2,1)S(1)} %slice.385), channel_id=1, source_target_pairs={{0,8},{8,16},{16,24},{1,9},{9,17},{17,25},{2,10},{10,18},{18,26},{... | collective-permute-start | bytes 147464 | tf_op jit(solution)/shard_map/ppermute | solution.py:14
  46.4 3.1 %collective-permute-start.2 = (bf16[2,1,16,16,192]{4,3,2,0,1:T(8,128)(2,1)S(1)}, bf16[2,1,16,16,192]{4,3,2,0,1:T(8,128)(2,1)S(1)}, u32[]{:S(2)}, u32[]{:S(2)}) collective-permute-start(bf16[2,1,16,16,192]{4,3,2,0,1:T(8,128)(2,1)S(1)} %slice.392), channel_id=1, source_target_pairs={{0,8},{8,16},{16,24},{1,9},{9,17},{17,25},{2,10},{10,18},{18,26},{... | collective-permute-start | bytes 589832 | tf_op jit(solution)/shard_map/ppermute | solution.py:14
  48.7 1.7 %copy-start.16 = (f32[192]{0:T(256)S(1)}, f32[192]{0:T(256)}, u32[]{:S(2)}) copy-start(f32[192]{0:T(256)} %param.18) | copy-start | bytes 2308
  48.7 1.7 %copy-start.19 = (f32[192]{0:T(256)S(1)}, f32[192]{0:T(256)}, u32[]{:S(2)}) copy-start(f32[192]{0:T(256)} %param.19) | copy-start | bytes 2308
  60.4 2.0 %copy-start.13 = (bf16[4,16,16,576]{3,2,1,0:T(8,128)(2,1)S(1)}, bf16[4,16,16,576]{3,2,1,0:T(8,128)(2,1)}, u32[]{:S(2)}) copy-start(bf16[4,16,16,576]{3,2,1,0:T(8,128)(2,1)} %get-tuple-element.187) | copy-start | bytes 3538948 | tf_op jit(solution)/shard_map/cond
  62.5 1.3 copy-start.11
  63.8 1.3 copy-start.9
  65.1 1.3 copy-start.7
  66.4 1.3 copy-start.5
  67.8 1.3 copy-start.3
  69.1 1.3 copy-start.1
  110.7 10.3 %collective-permute-start.3 = (bf16[2,1,4,192]{3,2,0,1:T(4,128)(2,1)S(1)}, bf16[2,1,4,192]{3,2,0,1:T(4,128)(2,1)S(1)}, u32[]{:S(2)}, u32[]{:S(2)}) collective-permute-start(bf16[2,1,4,192]{3,2,0,1:T(4,128)(2,1)S(1)} %slice.405), channel_id=1, source_target_pairs={{0,8},{8,16},{16,24},{1,9},{9,17},{17,25},{2,10},{10,18},{18,26},{... | collective-permute-start | bytes 9224 | tf_op jit(solution)/shard_map/ppermute | solution.py:14
  112.0 8.9 %collective-permute-start.4 = (bf16[2,1,4,16,192]{4,3,0,2,1:T(8,128)(2,1)S(1)}, bf16[2,1,4,16,192]{4,3,0,2,1:T(8,128)(2,1)S(1)}, u32[]{:S(2)}, u32[]{:S(2)}) collective-permute-start(bf16[2,1,4,16,192]{4,3,0,2,1:T(8,128)(2,1)S(1)} %slice.408), channel_id=1, source_target_pairs={{0,8},{8,16},{16,24},{1,9},{9,17},{17,25},{2,10},{10,18},{18,26},{... | collective-permute-start | bytes 147464 | tf_op jit(solution)/shard_map/ppermute | solution.py:14
  119.0 3.1 %collective-permute-start.5 = (bf16[2,1,16,16,192]{4,3,2,0,1:T(8,128)(2,1)S(1)}, bf16[2,1,16,16,192]{4,3,2,0,1:T(8,128)(2,1)S(1)}, u32[]{:S(2)}, u32[]{:S(2)}) collective-permute-start(bf16[2,1,16,16,192]{4,3,2,0,1:T(8,128)(2,1)S(1)} %slice_bitcast_fusion.36), channel_id=1, source_target_pairs={{0,8},{8,16},{16,24},{1,9},{9,17},{17,25},{2,10},{10,18},{18,26},{... | collective-permute-start | bytes 589832 | tf_op jit(solution)/shard_map/ppermute | solution.py:14
  121.2 1.7 %copy-start.18 = (f32[192]{0:T(256)S(1)}, f32[192]{0:T(256)}, u32[]{:S(2)}) copy-start(f32[192]{0:T(256)} %param.21) | copy-start | bytes 2308
  133.0 2.0 %copy-start.14 = (bf16[4,16,16,576]{3,2,1,0:T(8,128)(2,1)S(1)}, bf16[4,16,16,576]{3,2,1,0:T(8,128)(2,1)}, u32[]{:S(2)}) copy-start(bf16[4,16,16,576]{3,2,1,0:T(8,128)(2,1)} %get-tuple-element.201) | copy-start | bytes 3538948 | tf_op jit(solution)/shard_map/cond
  135.0 1.3 copy-start.12
  136.4 1.3 copy-start.10
  137.7 1.3 copy-start.8
  139.0 1.3 copy-start.6
  140.3 1.3 copy-start.4
  141.6 1.3 copy-start.2
  142.9 1.3 copy-start
  145.2 1.0 copy-start.15
where the time goes:
time: 150 us; the launch traced here: 147 us
  blocking collectives  68.9 us (46%)
  local copies, waits for them, and re-layouts  33 us (22%)
  matrix products  18.2 us (12%)
  starting transfers between devices  17.5 us (12%)
  other arithmetic  6.69 us (4%)
    all_gather x2, blocking collectives, extend(): lax.all_gather(edge_pack(activation), 'space', axis=1, tiled=True)  68.9 us
    ppermute x6, starting transfers between devices, shifted(): lax.ppermute(value, axis, [(source, source + steps) for source in range(f...  17.5 us
    dot_general x18, matrix products, conv_tile(): jnp.dot(window, weight[time_off * 3 + row_off], preferred_element_type=jn...  16.4 us
    cond x32, local copies, waits for them, and re-layouts  9.47 us
    slice x2, local copies, waits for them, and re-layouts, conv_tile(): widened[time_off:time_off + frames_out, row_off:row_off + side_len]  8.86 us
    another operation x2, local copies, waits for them, and re-layouts  8.17 us
  transfers between devices with their start and end apart: 6, of which 2 were waited for; matrix products, arithmetic and copies ran while one was open for 1% of the time, Pallas kernels for 0%

commit v1 on v0

--- a/solution.py
+++ b/solution.py
@@ -1,8 +1,11 @@
+import functools
 from functools import partial
 
 import jax
 import jax.numpy as jnp
 from jax import lax
+from jax.experimental import pallas as pl
+from jax.experimental.pallas import tpu as pltpu
 from jax.sharding import PartitionSpec as P
 
 epsilon = 1e-06
@@ -121,7 +124,7 @@
     return jnp.stack(results, axis=1)
 
 
-def on_device(
+def general_path(
     video_in,
     neighbours,
     valid_frames,
@@ -166,6 +169,208 @@
     return block_out.reshape(frames_dev, tiles_dev, side_len, side_len * channels)
 
 
+def silu(a):
+    return a*(0.5+0.5*jnp.tanh(0.5*a))
+def normsilu(v,g):
+    ss=jnp.mean(v*v,axis=-1,keepdims=True)
+    return silu(v*lax.rsqrt(ss+epsilon)*g)
+LANE=256
+def put(B,idx,h,C):
+    S=h.shape[0]
+    row=lax.broadcasted_iota(jnp.int32,h.shape,0)
+    down=jnp.where(row==0,0.0,pltpu.roll(h,1,0))
+    up=jnp.where(row==S-1,0.0,pltpu.roll(h,S-1,0))
+    B[idx+(slice(None),slice(0,C))]=down.astype(jnp.bfloat16)
+    B[idx+(slice(None),slice(LANE,LANE+C))]=h.astype(jnp.bfloat16)
+    B[idx+(slice(None),slice(2*LANE,2*LANE+C))]=up.astype(jnp.bfloat16)
+def zero_pads(B,C):
+    X,Fr,S,L=B.shape
+    z=jnp.zeros((Fr,S,LANE-C),B.dtype)
+    def body(x,_):
+        for q in range(3):
+            B[x,:,:,q*LANE+C:(q+1)*LANE]=z
+        return 0
+    lax.fori_loop(0,X,body,0)
+def conv(B,x0,G,nf,w,C):
+    S=B.shape[2]
+    acc=None
+    for p in range(3):
+        for r in range(3):
+            lhs=B[pl.ds(x0+r,G),p:p+nf].reshape(G*nf*S,3*LANE)
+            d=jnp.dot(lhs,w[p*3+r],preferred_element_type=jnp.float32)
+            acc=d if acc is None else acc+d
+    return acc.reshape(G,nf,S,C)
+def spread_weights(wt,w,C):
+    z=jnp.zeros((LANE-C,C),w.dtype)
+    def body(p,_):
+        for q in range(3):
+            t=wt[3*p+q].T
+            for r in range(3):
+                w[p*3+r,q*LANE:q*LANE+C]=t[r*C:(r+1)*C]
+                w[p*3+r,q*LANE+C:(q+1)*LANE]=z
+        return 0
+    lax.fori_loop(0,3,body,0)
+def whole(nb,vf,own,prev,rim,prim,g1,w1h,b1,g2,w2h,b2,out,B1,B2,w1,w2,wt1,wt2,sem1,sem2,*,G1,G2):
+    Fd,S,M=own.shape; C=g1.shape[0]; X=M//C
+    c1=pltpu.make_async_copy(w1h,wt1,sem1.at[0]); c2=pltpu.make_async_copy(w2h,wt2,sem2.at[0])
+    c1.start(); c2.start()
+    first=lax.axis_index("tm")*Fd; vs,vl,vr=tracks(nb,vf)
+    zero_pads(B1,C); zero_pads(B2,C)
+    gv1=g1[...].reshape(1,C); gv2=g2[...].reshape(1,C); bv1=b1[...].reshape(1,C); bv2=b2[...].reshape(1,C)
+    def there(f,v):
+        return ((f>=0)&(f<v)).astype(jnp.float32)
+    def act(pair,f,v,x,fi):
+        m=there(f,v)
+        vv=pair.astype(jnp.float32)*m
+        for j in range(2):
+            put(B1,(x+j,fi),normsilu(vv[:,j*C:(j+1)*C],gv1),C)
+    for f in range(Fd):
+        act(prim[0,f],first-Fd+f,vl,0,f); act(rim[0,f],first+f,vl,0,Fd+f)
+        act(prim[1,f],first-Fd+f,vr,X+2,f); act(rim[1,f],first+f,vr,X+2,Fd+f)
+    def actloop(k,_):
+        ds=pl.ds(pl.multiple_of(k*2*C,128),2*C)
+        for f in range(Fd):
+            act(prev[f,:,ds],first-Fd+f,vs,2+2*k,f)
+            act(own[f,:,ds],first+f,vs,2+2*k,Fd+f)
+        return 0
+    lax.fori_loop(0,X//2,actloop,0)
+    c1.wait(); spread_weights(wt1,w1,C)
+    nf1=Fd+2
+    def c1loop(i,_):
+        x0=i*G1
+        a=conv(B1,x0,G1,nf1,w1,C)
+        for g in range(G1):
+            x=x0+g-1
+            v=jnp.where(x<0,vl,jnp.where(x>=X,vr,vs))
+            for f in range(nf1):
+                m=there(first-2+f,v)
+                put(B2,(x0+g,f),normsilu((a[g,f]+bv1)*m,gv2),C)
+        return 0
+    lax.fori_loop(0,(X+2)//G1,c1loop,0)
+    c2.wait(); spread_weights(wt2,w2,C)
+    def c2loop(i,_):
+        x0=i*G2
+        a=conv(B2,x0,G2,Fd,w2,C)
+        for f in range(Fd):
+            m=there(first+f,vs)
+            for g in range(0,G2,2):
+                ds=pl.ds(pl.multiple_of((x0+g)*C,128),2*C)
+                res=own[f,:,ds].astype(jnp.float32)*m
+                o=jnp.concatenate([(a[g,f]+bv2)*m,(a[g+1,f]+bv2)*m],-1)+res
+                out[f,:,ds]=o.astype(jnp.bfloat16)
+        return 0
+    lax.fori_loop(0,X//G2,c2loop,0)
+def call_whole(nb,vf,own,prev,rim,prim,g1,w1,b1,g2,w2,b2,G1=6,G2=8):
+    Fd,S,M=own.shape; C=g1.shape[0]; X=M//C
+    V=pl.BlockSpec(memory_space=pltpu.VMEM); A=pl.BlockSpec(memory_space=pl.ANY); SM=pl.BlockSpec(memory_space=pltpu.SMEM)
+    return pl.pallas_call(functools.partial(whole,G1=G1,G2=G2),
+        out_shape=jax.ShapeDtypeStruct(own.shape,own.dtype),
+        in_specs=[SM,SM,V,V,V,V,V,A,V,V,A,V],out_specs=V,
+        scratch_shapes=[pltpu.VMEM((X+4,2*Fd,S,3*LANE),jnp.bfloat16),pltpu.VMEM((X+2,Fd+2,S,3*LANE),jnp.bfloat16),
+            pltpu.VMEM((9,3*LANE,C),jnp.bfloat16),pltpu.VMEM((9,3*LANE,C),jnp.bfloat16),pltpu.VMEM((9,C,3*C),jnp.bfloat16),pltpu.VMEM((9,C,3*C),jnp.bfloat16),pltpu.SemaphoreType.DMA((1,)),pltpu.SemaphoreType.DMA((1,))],
+        compiler_params=pltpu.CompilerParams(vmem_limit_bytes=60*2**20),
+    )(nb,vf,own,prev,rim,prim,g1,jnp.swapaxes(w1,1,2),b1,g2,jnp.swapaxes(w2,1,2),b2)
+
+
+LEFT, RIGHT = 3, 4
+
+
+def tracks(nb, vf):
+    me = lax.axis_index("space")
+    tiles = nb.shape[0]
+
+    def of(tile):
+        return jnp.where(tile < tiles, vf[jnp.minimum(tile, tiles - 1)], 0)
+
+    return vf[me], of(nb[me, LEFT]), of(nb[me, RIGHT])
+
+
+def pick_kernel(nb, mine, pair, *outs):
+    tiles = nb.shape[0]
+    me = lax.axis_index("space")
+    for step, out in enumerate(outs):
+        there = lax.rem(me + 2 * (step + 1), tiles)
+        for side, column in ((0, LEFT), (1, RIGHT)):
+            source = nb[there, column]
+
+            @pl.when(source == me)
+            def _():
+                out[side] = mine[1 - side]
+
+            @pl.when(source != me)
+            def _():
+                out[side] = pair[1 - side]
+
+
+def rims_kernel(nb, mine, pair, *rest):
+    received, out = rest[:-1], rest[-1]
+    tiles = nb.shape[0]
+    half = tiles // 2
+    me = lax.axis_index("space")
+    for side, column in ((0, LEFT), (1, RIGHT)):
+        source = nb[me, column]
+        step = lax.rem(me // 2 - source // 2 + tiles, half)
+        at_home = (step == 0) | (source >= tiles)
+
+        @pl.when(at_home & (source == me ^ 1))
+        def _():
+            out[side] = pair[1 - side]
+
+        @pl.when(at_home & (source != me ^ 1))
+        def _():
+            out[side] = mine[1 - side]
+
+        for s, arrived in enumerate(received):
+
+            @pl.when((step == s + 1) & (source < tiles))
+            def _():
+                out[side] = arrived[side]
+
+
+def exchange(own, neighbours, channels):
+    count = lax.axis_size("space")
+    vmem = pl.BlockSpec(memory_space=pltpu.VMEM)
+    smem = pl.BlockSpec(memory_space=pltpu.SMEM)
+    mine = jnp.stack([own[:, :, : 2 * channels], own[:, :, -2 * channels :]])
+    pair = lax.ppermute(mine, "space", [(i, i ^ 1) for i in range(count)])
+    piece = jax.ShapeDtypeStruct(mine.shape, mine.dtype)
+    steps = count // 2 - 1
+    sent = pl.pallas_call(
+        pick_kernel,
+        out_shape=[piece] * steps,
+        in_specs=[smem, vmem, vmem],
+        out_specs=[vmem] * steps,
+    )(neighbours, mine, pair)
+    received = [
+        lax.ppermute(value, "space", [(i, (i + 2 * (s + 1)) % count) for i in range(count)])
+        for s, value in enumerate(sent)
+    ]
+    return pl.pallas_call(
+        rims_kernel,
+        out_shape=piece,
+        in_specs=[smem] + [vmem] * (2 + steps),
+        out_specs=vmem,
+    )(neighbours, mine, pair, *received)
+
+
+def row_path(video_in, neighbours, valid_frames, gain1, weight1, bias1, gain2, weight2, bias2):
+    own = video_in[:, 0]
+    prev = shifted(own, "tm", 1)
+    rim = exchange(own, neighbours, gain1.shape[0])
+    prev_rim = shifted(rim, "tm", 1)
+    out = call_whole(neighbours, valid_frames, own, prev, rim, prev_rim, gain1, weight1, bias1, gain2, weight2, bias2)
+    return out[:, None]
+
+
+def on_device(video_in, neighbours, *rest):
+    frames_dev, tiles_dev = video_in.shape[:2]
+    tiles = neighbours.shape[0]
+    if tiles_dev != 1 or tiles % 2 or frames_dev < 4:
+        return general_path(video_in, neighbours, *rest)
+    beyond = jnp.concatenate([neighbours[:, :LEFT], neighbours[:, RIGHT + 1 :]], axis=1)
+    return lax.cond(jnp.any(beyond < tiles), general_path, row_path, video_in, neighbours, *rest)
+
+
 def solution(mesh):
     in_specs = (P("tm", "space", None, None), P(), P(), P(), P(), P(), P(), P(), P())
     out_specs = P("tm", "space", None, None)

time: 150 us -> 59.2 us (0.39); the launches traced: 147 us -> 58.4 us
  blocking collectives: 68.9 us -> 0 us
  Pallas kernels: 0 us -> 29.1 us
  local copies, waits for them, and re-layouts: 33 us -> 4.38 us
  matrix products: 18.2 us -> 0 us
  waiting for transfers between devices: 1.48 us -> 9.88 us
  other arithmetic: 6.69 us -> 0.72 us
  starting transfers between devices: 17.5 us -> 13.1 us
    all_gather x2 -> x0, blocking collectives: 68.9 us -> none  [extend(): lax.all_gather(edge_pack(activation), 'space', axis=1, tiled=True)]
    pallas_call x0 -> x3, Pallas kernels: none -> 29.1 us  [the longest x1 25.5 us: call_whole(): pl.pallas_call(functools.partial(whole, G1=G1, G2=G2), out_shape=jax.Shap...]
    dot_general x22 -> x0, matrix products: 18.2 us -> none  [the longest x18 16.4 us: conv_tile(): jnp.dot(window, weight[time_off * 3 + row_off], preferred_element_type=jn...]
    ppermute x6 -> x2, starting transfers between devices: 17.5 us -> 4.45 us  [shifted(): lax.ppermute(value, axis, [(source, source + steps) for source in range(f...]
    slice x18 -> x1, local copies, waits for them, and re-layouts: 10.7 us -> 0.83 us  [on_device(): neighbours[:, :LEFT]]
    ppermute x0 -> x4, waiting for transfers between devices: none -> 8.75 us  [the longest x3 6.15 us: exchange(): lax.ppermute(value, 'space', [(i, (i + 2 * (s + 1)) % count) for i in ran...]
    ppermute x0 -> x4, starting transfers between devices: none -> 8.66 us  [the longest x3 6.26 us: exchange(): lax.ppermute(value, 'space', [(i, (i + 2 * (s + 1)) % count) for i in ran...]
    another operation x7 -> x1, local copies, waits for them, and re-layouts: 8.49 us -> 0.84 us  [exchange(): mine = jnp.stack([own[:, :, :2 * channels], own[:, :, -2 * channels:]])]
  transfers between devices with their start and end apart: 6 -> 6, of which waited for: 2 -> 4; matrix products, arithmetic and copies ran while one was open for 1% -> 1% of each run, Pallas kernels for 0% -> 6%
where the time goes in v1:
time: 59.2 us; the launch traced here: 58.4 us
  Pallas kernels  29.1 us (49%)
  starting transfers between devices  13.1 us (22%)
  waiting for transfers between devices  9.88 us (17%)
  local copies, waits for them, and re-layouts  4.38 us (7%)
  between operations  0.83 us (1%)
  other arithmetic  0.72 us (1%)
    pallas_call x1, Pallas kernels, call_whole(): pl.pallas_call(functools.partial(whole, G1=G1, G2=G2), out_shape=jax.Shap...  25.5 us
    ppermute x3, starting transfers between devices, exchange(): lax.ppermute(value, 'space', [(i, (i + 2 * (s + 1)) % count) for i in ran...  6.26 us
    ppermute x3, waiting for transfers between devices, exchange(): lax.ppermute(value, 'space', [(i, (i + 2 * (s + 1)) % count) for i in ran...  6.15 us
    ppermute x2, starting transfers between devices, shifted(): lax.ppermute(value, axis, [(source, source + steps) for source in range(f...  4.45 us
    cond x16, local copies, waits for them, and re-layouts  2.71 us
    ppermute x1, waiting for transfers between devices, exchange(): pair = lax.ppermute(mine, 'space', [(i, i ^ 1) for i in range(count)])  2.6 us
    ppermute x1, starting transfers between devices, exchange(): pair = lax.ppermute(mine, 'space', [(i, i ^ 1) for i in range(count)])  2.4 us
    pallas_call x1, Pallas kernels, exchange(): pl.pallas_call(rims_kernel, out_shape=piece, in_specs=[smem] + [vmem] * (...  1.83 us
  transfers between devices with their start and end apart: 6, of which 4 were waited for; matrix products, arithmetic and copies ran while one was open for 1% of the time, Pallas kernels for 6%

profile of v1, /device:TPU:0, one launch (start us, length us, event | category | flops | bytes accessed | tf_op | source)
XLA Modules:
  0.0 58.4 jit_solution(5390163076993463551)
XLA Ops:
  0.0 0.8 %fusion.84 = (s32[8,3]{1,0:T(8,128)S(1)}, s32[8,3]{1,0:T(8,128)S(1)}) fusion(s32[8,8]{1,0:T(8,128)} %param.16), kind=kLoop, calls=%fused_computation.189 | loop fusion | bytes 384 | tf_op jit(solution)/shard_map/slice | solution.py:370
  0.8 0.7 %fusion.72 = pred[]{:T(512)} fusion(s32[8,3]{1,0:T(8,128)S(1)} %get-tuple-element.413, s32[8,3]{1,0:T(8,128)S(1)} %get-tuple-element.412), kind=kLoop, calls=%fused_computation.177 | loop fusion | flops 143 | bytes 193 | tf_op jit(solution)/shard_map/reduce_or | solution.py:371
  2.2 56.0 %conditional.3 = ((bf16[4,1,16,3072]{3,2,0,1:T(8,128)(2,1)})) conditional(s32[]{:T(128)} %convert_element_type.108, (bf16[4,1,16,3072]{3,2,1,0:T(8,128)(2,1)}, s32[8,8]{1,0:T(8,128)}, bf16[9,576,192]{1,2,0:T(8,128)(2,1)}, bf16[9,576,192]{1,2,0:T(8,128)(2,1)}, s32[8]{0:T(128)}, /*index=5*/f32[192]{0:T(256)}, f32[192]{0:T(256)}, f32[192]{0:T(256)}, ...), branch_computations={%region_1.0_spmd, %region_2.9_spmd} | conditional | flops 4110178304 | bytes 216145120 | solution.py:371
  2.2 0.0 copy-start.15
  2.2 2.6 %collective-permute-start = (bf16[4,16,3072]{2,1,0:T(8,128)(2,1)}, bf16[4,16,3072]{2,1,0:T(8,128)(2,1)S(1)}, u32[]{:S(2)}, u32[]{:S(2)}) collective-permute-start(bf16[4,16,3072]{2,1,0:T(8,128)(2,1)} %bitcast.273), channel_id=1, source_target_pairs={{0,8},{8,16},{16,24},{1,9},{9,17},{17,25},{2,10},{10,18},{18,26},{... | collective-permute-start | bytes 1179656 | tf_op jit(solution)/shard_map/cond/branch_0_fun/ppermute | solution.py:17
  4.8 0.8 %slice_bitcast_fusion.1 = (bf16[1,4,16,384]{3,2,1,0:T(8,128)(2,1)S(1)}, bf16[1,4,16,384]{3,2,1,0:T(8,128)(2,1)S(1)}) fusion(bf16[4,16,3072]{2,1,0:T(8,128)(2,1)} %bitcast.274), kind=kLoop, calls=%fused_computation.2 | loop fusion | bytes 196608 | tf_op jit(solution)/shard_map/cond/branch_0_fun/stack | solution.py:334
  5.6 0.0 copy-start.17
  5.7 2.4 %collective-permute-start.1 = (bf16[2,4,16,384]{3,2,1,0:T(8,128)(2,1)S(1)}, bf16[2,4,16,384]{3,2,1,0:T(8,128)(2,1)S(1)}, u32[]{:S(2)}, u32[]{:S(2)}) collective-permute-start(bf16[2,4,16,384]{3,2,1,0:T(8,128)(2,1)S(1)} %pad_maximum_fusion.mine), channel_id=1, source_target_pairs={{0,1},{1,0},{2,3},{3,2},{4,5},{5,4},{6,7},{7,6},{8,9},{9,8},{10,11... | collective-permute-start | bytes 294920 | tf_op jit(solution)/shard_map/cond/branch_0_fun/ppermute | solution.py:335
  8.1 2.6 %collective-permute-done.1.pair = bf16[2,4,16,384]{3,2,1,0:T(8,128)(2,1)S(1)} collective-permute-done((bf16[2,4,16,384]{3,2,1,0:T(8,128)(2,1)S(1)}, bf16[2,4,16,384]{3,2,1,0:T(8,128)(2,1)S(1)}, u32[]{:S(2)}, u32[]{:S(2)}) %collective-permute-start.1) | collective-permute-done | bytes 98336 | tf_op jit(solution)/shard_map/cond/branch_0_fun/ppermute | solution.py:335
  10.7 0.0 copy-start.19
  10.7 0.0 copy-done.17
  10.7 0.6 %copy-done.19 = bf16[2,4,16,384]{3,2,1,0:T(8,128)(2,1)} copy-done((bf16[2,4,16,384]{3,2,1,0:T(8,128)(2,1)}, bf16[2,4,16,384]{3,2,1,0:T(8,128)(2,1)S(1)}, u32[]{:S(2)}) %copy-start.19) | copy-done | bytes 98328 | tf_op jit(solution)/shard_map/cond
  11.3 1.8 %branch_0_fun.3 = (bf16[2,4,16,384]{3,2,1,0:T(8,128)(2,1)}, bf16[2,4,16,384]{3,2,1,0:T(8,128)(2,1)}, bf16[2,4,16,384]{3,2,1,0:T(8,128)(2,1)}) custom-call(s32[8,8]{1,0:T(8,128)} %get-tuple-element.81.nb, bf16[2,4,16,384]{3,2,1,0:T(8,128)(2,1)} %copy-done.17, bf16[2,4,16,384]{3,2,1,0:T(8,128)(2,1)} %copy-done.19), custom_call_target="tpu_custom_call" | custom-call | tf_op jit(solution)/shard_map/cond/branch_0_fun/pallas_call | solution.py:338
  13.1 2.3 %collective-permute-start.2 = (bf16[2,4,16,384]{3,2,1,0:T(8,128)(2,1)}, bf16[2,4,16,384]{3,2,1,0:T(8,128)(2,1)S(1)}, u32[]{:S(2)}, u32[]{:S(2)}) collective-permute-start(bf16[2,4,16,384]{3,2,1,0:T(8,128)(2,1)} %get-tuple-element.84), channel_id=1, source_target_pairs={{0,2},{1,3},{2,4},{3,5},{4,6},{5,7},{6,0},{7,1},{8,10},{9,11},{10,... | collective-permute-start | bytes 294920 | tf_op jit(solution)/shard_map/cond/branch_0_fun/ppermute | solution.py:345
  15.4 2.6 %collective-permute-start.3 = (bf16[2,4,16,384]{3,2,1,0:T(8,128)(2,1)}, bf16[2,4,16,384]{3,2,1,0:T(8,128)(2,1)S(1)}, u32[]{:S(2)}, u32[]{:S(2)}) collective-permute-start(bf16[2,4,16,384]{3,2,1,0:T(8,128)(2,1)} %get-tuple-element.85), channel_id=1, source_target_pairs={{0,4},{1,5},{2,6},{3,7},{4,0},{5,1},{6,2},{7,3},{8,12},{9,13},{10,... | collective-permute-start | bytes 294920 | tf_op jit(solution)/shard_map/cond/branch_0_fun/ppermute | solution.py:345
  18.0 1.3 %collective-permute-start.4 = (bf16[2,4,16,384]{3,2,1,0:T(8,128)(2,1)}, bf16[2,4,16,384]{3,2,1,0:T(8,128)(2,1)S(1)}, u32[]{:S(2)}, u32[]{:S(2)}) collective-permute-start(bf16[2,4,16,384]{3,2,1,0:T(8,128)(2,1)} %get-tuple-element.86), channel_id=1, source_target_pairs={{0,6},{1,7},{2,0},{3,1},{4,2},{5,3},{6,4},{7,5},{8,14},{9,15},{10,... | collective-permute-start | bytes 294920 | tf_op jit(solution)/shard_map/cond/branch_0_fun/ppermute | solution.py:345
  19.3 2.0 %collective-permute-done.2.rest_0_ = bf16[2,4,16,384]{3,2,1,0:T(8,128)(2,1)S(1)} collective-permute-done((bf16[2,4,16,384]{3,2,1,0:T(8,128)(2,1)}, bf16[2,4,16,384]{3,2,1,0:T(8,128)(2,1)S(1)}, u32[]{:S(2)}, u32[]{:S(2)}) %collective-permute-start.2) | collective-permute-done | bytes 98336 | tf_op jit(solution)/shard_map/cond/branch_0_fun/ppermute | solution.py:345
  21.4 0.0 copy-start.20
  21.4 4.1 %collective-permute-done.3.rest_1_ = bf16[2,4,16,384]{3,2,1,0:T(8,128)(2,1)S(1)} collective-permute-done((bf16[2,4,16,384]{3,2,1,0:T(8,128)(2,1)}, bf16[2,4,16,384]{3,2,1,0:T(8,128)(2,1)S(1)}, u32[]{:S(2)}, u32[]{:S(2)}) %collective-permute-start.3) | collective-permute-done | bytes 98336 | tf_op jit(solution)/shard_map/cond/branch_0_fun/ppermute | solution.py:345
  25.5 0.0 copy-start.21
  25.5 0.0 collective-permute-done.4.rest_2_
  25.5 0.0 copy-done.20
  25.5 0.6 %copy-done.21 = bf16[2,4,16,384]{3,2,1,0:T(8,128)(2,1)} copy-done((bf16[2,4,16,384]{3,2,1,0:T(8,128)(2,1)}, bf16[2,4,16,384]{3,2,1,0:T(8,128)(2,1)S(1)}, u32[]{:S(2)}) %copy-start.21) | copy-done | bytes 98328 | tf_op jit(solution)/shard_map/cond
  26.1 0.0 copy-start.22
  26.1 0.6 %copy-done.22 = bf16[2,4,16,384]{3,2,1,0:T(8,128)(2,1)} copy-done((bf16[2,4,16,384]{3,2,1,0:T(8,128)(2,1)}, bf16[2,4,16,384]{3,2,1,0:T(8,128)(2,1)S(1)}, u32[]{:S(2)}) %copy-start.22) | copy-done | bytes 98328 | tf_op jit(solution)/shard_map/cond
  26.8 1.8 %branch_0_fun.4.rim = bf16[2,4,16,384]{3,2,1,0:T(8,128)(2,1)} custom-call(s32[8,8]{1,0:T(8,128)} %get-tuple-element.81.nb, bf16[2,4,16,384]{3,2,1,0:T(8,128)(2,1)} %copy-done.17, bf16[2,4,16,384]{3,2,1,0:T(8,128)(2,1)} %copy-done.19, bf16[2,4,16,384]{3,2,1,0:T(8,128)(2,1)} %copy-done.20, bf16[2,4,16,384]{3,2,1,0:T(8,128)(2,1)} %copy-done.21, ...), custom_call_target="tpu_custom_call" | custom-call | tf_op jit(solution)/shard_map/cond/branch_0_fun/pallas_call | solution.py:348
  28.6 1.9 %collective-permute-start.5 = (bf16[2,4,16,384]{3,2,1,0:T(8,128)(2,1)}, bf16[2,4,16,384]{3,2,1,0:T(8,128)(2,1)S(1)}, u32[]{:S(2)}, u32[]{:S(2)}) collective-permute-start(bf16[2,4,16,384]{3,2,1,0:T(8,128)(2,1)} %branch_0_fun.4.rim), channel_id=1, source_target_pairs={{0,8},{8,16},{16,24},{1,9},{9,17},{17,25},{2,10},{10,18},{18,26},{... | collective-permute-start | bytes 294920 | tf_op jit(solution)/shard_map/cond/branch_0_fun/ppermute | solution.py:17
  30.5 1.1 %collective-permute-done.5.prim = bf16[2,4,16,384]{3,2,1,0:T(8,128)(2,1)S(1)} collective-permute-done((bf16[2,4,16,384]{3,2,1,0:T(8,128)(2,1)}, bf16[2,4,16,384]{3,2,1,0:T(8,128)(2,1)S(1)}, u32[]{:S(2)}, u32[]{:S(2)}) %collective-permute-start.5) | collective-permute-done | bytes 98336 | tf_op jit(solution)/shard_map/cond/branch_0_fun/ppermute | solution.py:17
  31.6 0.0 copy-start.23
  31.6 0.0 collective-permute-done.prev
  31.6 0.0 copy-start.18
  31.6 0.6 %copy-done.23 = bf16[2,4,16,384]{3,2,1,0:T(8,128)(2,1)} copy-done((bf16[2,4,16,384]{3,2,1,0:T(8,128)(2,1)}, bf16[2,4,16,384]{3,2,1,0:T(8,128)(2,1)S(1)}, u32[]{:S(2)}) %copy-start.23) | copy-done | bytes 98328 | tf_op jit(solution)/shard_map/cond
  32.3 0.1 copy-done.18
  32.4 0.0 copy-done.15
  32.4 25.5 %branch_0_fun.5 = bf16[4,16,3072]{2,1,0:T(8,128)(2,1)} custom-call(s32[8,8]{1,0:T(8,128)} %get-tuple-element.81.nb, s32[8]{0:T(128)} %get-tuple-element.82.vf, bf16[4,16,3072]{2,1,0:T(8,128)(2,1)S(1)} %bitcast.275, bf16[4,16,3072]{2,1,0:T(8,128)(2,1)} %copy-done.18, bf16[2,4,16,384]{3,2,1,0:T(8,128)(2,1)} %branch_0_fun.4.rim, ...), custom_call_target="tpu_custom_call" | custom-call | tf_op jit(solution)/shard_map/cond/branch_0_fun/pallas_call | solution.py:266
  (1 shorter events, 0.0 us)
Async XLA Ops:
  2.2 30.2 %copy-start.15 = (bf16[4,1,16,3072]{3,2,1,0:T(8,128)(2,1)S(1)}, bf16[4,1,16,3072]{3,2,1,0:T(8,128)(2,1)}, u32[]{:S(2)}) copy-start(bf16[4,1,16,3072]{3,2,1,0:T(8,128)(2,1)} %get-tuple-element.326) | copy-start | bytes 1179652 | tf_op jit(solution)/shard_map/cond
  2.2 29.4 %collective-permute-start = (bf16[4,16,3072]{2,1,0:T(8,128)(2,1)}, bf16[4,16,3072]{2,1,0:T(8,128)(2,1)S(1)}, u32[]{:S(2)}, u32[]{:S(2)}) collective-permute-start(bf16[4,16,3072]{2,1,0:T(8,128)(2,1)} %bitcast.273), channel_id=1, source_target_pairs={{0,8},{8,16},{16,24},{1,9},{9,17},{17,25},{2,10},{10,18},{18,26},{... | collective-permute-start | bytes 1179656 | tf_op jit(solution)/shard_map/cond/branch_0_fun/ppermute | solution.py:17
  5.6 5.0 %copy-start.17 = (bf16[2,4,16,384]{3,2,1,0:T(8,128)(2,1)}, bf16[2,4,16,384]{3,2,1,0:T(8,128)(2,1)S(1)}, u32[]{:S(2)}) copy-start(bf16[2,4,16,384]{3,2,1,0:T(8,128)(2,1)S(1)} %pad_maximum_fusion.mine) | copy-start | bytes 294916 | tf_op jit(solution)/shard_map/cond
  5.7 5.0 %collective-permute-start.1 = (bf16[2,4,16,384]{3,2,1,0:T(8,128)(2,1)S(1)}, bf16[2,4,16,384]{3,2,1,0:T(8,128)(2,1)S(1)}, u32[]{:S(2)}, u32[]{:S(2)}) collective-permute-start(bf16[2,4,16,384]{3,2,1,0:T(8,128)(2,1)S(1)} %pad_maximum_fusion.mine), channel_id=1, source_target_pairs={{0,1},{1,0},{2,3},{3,2},{4,5},{5,4},{6,7},{7,6},{8,9},{9,8},{10,11... | collective-permute-start | bytes 294920 | tf_op jit(solution)/shard_map/cond/branch_0_fun/ppermute | solution.py:335
  10.7 0.7 %copy-start.19 = (bf16[2,4,16,384]{3,2,1,0:T(8,128)(2,1)}, bf16[2,4,16,384]{3,2,1,0:T(8,128)(2,1)S(1)}, u32[]{:S(2)}) copy-start(bf16[2,4,16,384]{3,2,1,0:T(8,128)(2,1)S(1)} %collective-permute-done.1.pair) | copy-start | bytes 294916 | tf_op jit(solution)/shard_map/cond
  13.1 8.3 %collective-permute-start.2 = (bf16[2,4,16,384]{3,2,1,0:T(8,128)(2,1)}, bf16[2,4,16,384]{3,2,1,0:T(8,128)(2,1)S(1)}, u32[]{:S(2)}, u32[]{:S(2)}) collective-permute-start(bf16[2,4,16,384]{3,2,1,0:T(8,128)(2,1)} %get-tuple-element.84), channel_id=1, source_target_pairs={{0,2},{1,3},{2,4},{3,5},{4,6},{5,7},{6,0},{7,1},{8,10},{9,11},{10,... | collective-permute-start | bytes 294920 | tf_op jit(solution)/shard_map/cond/branch_0_fun/ppermute | solution.py:345
  15.4 10.1 %collective-permute-start.3 = (bf16[2,4,16,384]{3,2,1,0:T(8,128)(2,1)}, bf16[2,4,16,384]{3,2,1,0:T(8,128)(2,1)S(1)}, u32[]{:S(2)}, u32[]{:S(2)}) collective-permute-start(bf16[2,4,16,384]{3,2,1,0:T(8,128)(2,1)} %get-tuple-element.85), channel_id=1, source_target_pairs={{0,4},{1,5},{2,6},{3,7},{4,0},{5,1},{6,2},{7,3},{8,12},{9,13},{10,... | collective-permute-start | bytes 294920 | tf_op jit(solution)/shard_map/cond/branch_0_fun/ppermute | solution.py:345
  18.0 7.5 %collective-permute-start.4 = (bf16[2,4,16,384]{3,2,1,0:T(8,128)(2,1)}, bf16[2,4,16,384]{3,2,1,0:T(8,128)(2,1)S(1)}, u32[]{:S(2)}, u32[]{:S(2)}) collective-permute-start(bf16[2,4,16,384]{3,2,1,0:T(8,128)(2,1)} %get-tuple-element.86), channel_id=1, source_target_pairs={{0,6},{1,7},{2,0},{3,1},{4,2},{5,3},{6,4},{7,5},{8,14},{9,15},{10,... | collective-permute-start | bytes 294920 | tf_op jit(solution)/shard_map/cond/branch_0_fun/ppermute | solution.py:345
  21.4 4.1 %copy-start.20 = (bf16[2,4,16,384]{3,2,1,0:T(8,128)(2,1)}, bf16[2,4,16,384]{3,2,1,0:T(8,128)(2,1)S(1)}, u32[]{:S(2)}) copy-start(bf16[2,4,16,384]{3,2,1,0:T(8,128)(2,1)S(1)} %collective-permute-done.2.rest_0_) | copy-start | bytes 294916 | tf_op jit(solution)/shard_map/cond
  25.5 0.6 %copy-start.21 = (bf16[2,4,16,384]{3,2,1,0:T(8,128)(2,1)}, bf16[2,4,16,384]{3,2,1,0:T(8,128)(2,1)S(1)}, u32[]{:S(2)}) copy-start(bf16[2,4,16,384]{3,2,1,0:T(8,128)(2,1)S(1)} %collective-permute-done.3.rest_1_) | copy-start | bytes 294916 | tf_op jit(solution)/shard_map/cond
  26.1 0.6 %copy-start.22 = (bf16[2,4,16,384]{3,2,1,0:T(8,128)(2,1)}, bf16[2,4,16,384]{3,2,1,0:T(8,128)(2,1)S(1)}, u32[]{:S(2)}) copy-start(bf16[2,4,16,384]{3,2,1,0:T(8,128)(2,1)S(1)} %collective-permute-done.4.rest_2_) | copy-start | bytes 294916 | tf_op jit(solution)/shard_map/cond
  28.6 3.0 %collective-permute-start.5 = (bf16[2,4,16,384]{3,2,1,0:T(8,128)(2,1)}, bf16[2,4,16,384]{3,2,1,0:T(8,128)(2,1)S(1)}, u32[]{:S(2)}, u32[]{:S(2)}) collective-permute-start(bf16[2,4,16,384]{3,2,1,0:T(8,128)(2,1)} %branch_0_fun.4.rim), channel_id=1, source_target_pairs={{0,8},{8,16},{16,24},{1,9},{9,17},{17,25},{2,10},{10,18},{18,26},{... | collective-permute-start | bytes 294920 | tf_op jit(solution)/shard_map/cond/branch_0_fun/ppermute | solution.py:17
  31.6 0.6 %copy-start.23 = (bf16[2,4,16,384]{3,2,1,0:T(8,128)(2,1)}, bf16[2,4,16,384]{3,2,1,0:T(8,128)(2,1)S(1)}, u32[]{:S(2)}) copy-start(bf16[2,4,16,384]{3,2,1,0:T(8,128)(2,1)S(1)} %collective-permute-done.5.prim) | copy-start | bytes 294916 | tf_op jit(solution)/shard_map/cond
  31.6 0.8 %copy-start.18 = (bf16[4,16,3072]{2,1,0:T(8,128)(2,1)}, bf16[4,16,3072]{2,1,0:T(8,128)(2,1)S(1)}, u32[]{:S(2)}) copy-start(bf16[4,16,3072]{2,1,0:T(8,128)(2,1)S(1)} %collective-permute-done.prev) | copy-start | bytes 1179652 | tf_op jit(solution)/shard_map/cond

commit v2 on v0

--- a/solution.py
+++ b/solution.py
@@ -1,8 +1,11 @@
+import functools
 from functools import partial
 
 import jax
 import jax.numpy as jnp
 from jax import lax
+from jax.experimental import pallas as pl
+from jax.experimental.pallas import tpu as pltpu
 from jax.sharding import PartitionSpec as P
 
 epsilon = 1e-06
@@ -121,7 +124,7 @@
     return jnp.stack(results, axis=1)
 
 
-def on_device(
+def general_path(
     video_in,
     neighbours,
     valid_frames,
@@ -166,6 +169,373 @@
     return block_out.reshape(frames_dev, tiles_dev, side_len, side_len * channels)
 
 
+LANE = 256
+
+
+def silu(a):
+    return a * (0.5 + 0.5 * jnp.tanh(0.5 * a))
+
+
+def normed(v, gain):
+    square = jnp.mean(v * v, axis=-1, keepdims=True)
+    return silu(v * lax.rsqrt(square + epsilon) * gain)
+
+
+def put(buf, x, f0, h):
+    n, side, channels = h.shape
+    row = lax.broadcasted_iota(jnp.int32, h.shape, 1)
+    down = jnp.where(row == 0, 0.0, pltpu.roll(h, 1, 1))
+    up = jnp.where(row == side - 1, 0.0, pltpu.roll(h, side - 1, 1))
+    for q, t in enumerate((down, h, up)):
+        buf[x, f0 : f0 + n, :, q * LANE : q * LANE + channels] = t.astype(jnp.bfloat16)
+
+
+def zero_pads(buf, channels):
+    columns, frames, side, _ = buf.shape
+    zero = jnp.zeros((frames, side, LANE - channels), buf.dtype)
+
+    def body(x, _):
+        for q in range(3):
+            buf[x, :, :, q * LANE + channels : (q + 1) * LANE] = zero
+        return 0
+
+    lax.fori_loop(0, columns, body, 0)
+
+
+def spread(flat, weight):
+    channels = weight.shape[2]
+    zero = jnp.zeros((LANE - channels, channels), weight.dtype)
+
+    def body(p, _):
+        for q in range(3):
+            turned = flat[3 * p + q].T
+            for r in range(3):
+                weight[p * 3 + r, q * LANE : q * LANE + channels] = turned[r * channels : (r + 1) * channels]
+                weight[p * 3 + r, q * LANE + channels : (q + 1) * LANE] = zero
+        return 0
+
+    lax.fori_loop(0, 3, body, 0)
+
+
+def conv(buf, starts, width, f0, frames, weight):
+    side = buf.shape[2]
+    total = None
+    for p in range(3):
+        for r in range(3):
+            parts = [buf[pl.ds(x0 + r, width), f0 + p : f0 + p + frames] for x0 in starts]
+            rows = parts[0] if len(parts) == 1 else jnp.concatenate(parts, axis=0)
+            term = jnp.dot(rows.reshape(-1, 3 * LANE), weight[p * 3 + r], preferred_element_type=jnp.float32)
+            total = term if total is None else total + term
+    return total.reshape(len(starts) * width, frames, side, weight.shape[2])
+
+
+def there(f0, frames, valid):
+    frame = f0 + lax.broadcasted_iota(jnp.int32, (frames, 1, 1), 0)
+    return ((frame >= 0) & (frame < valid)).astype(jnp.float32)
+
+
+def act(buf, pair, f0, valid, x, at, gain):
+    channels = gain.shape[1]
+    values = pair.astype(jnp.float32) * there(f0, pair.shape[0], valid)
+    for j in range(2):
+        put(buf, x + j, at, normed(values[:, :, j * channels : (j + 1) * channels], gain))
+
+
+def act_tile(buf, tile, f0, valid, at, gain):
+    channels = gain.shape[1]
+
+    def body(k, _):
+        lanes = pl.ds(pl.multiple_of(k * 2 * channels, 128), 2 * channels)
+        act(buf, tile[:, :, lanes], f0, valid, 2 + 2 * k, at, gain)
+        return 0
+
+    lax.fori_loop(0, tile.shape[2] // (2 * channels), body, 0)
+
+
+def row_of(ref):
+    return ref[...].reshape(1, -1)
+
+
+def hide(total, buf, places, f0, at, bias, gain, valids):
+    for g, (x, valid) in enumerate(zip(places, valids)):
+        put(buf, x, at, normed((total[g] + bias) * there(f0, total.shape[1], valid), gain))
+
+
+def finish(total, out, own, places, bias, f0, valid):
+    channels = bias.shape[1]
+    mask = there(f0, total.shape[1], valid)
+    for g in range(0, len(places), 2):
+        x = places[g]
+        lanes = pl.ds(x * channels if isinstance(x, int) else pl.multiple_of(x * channels, 128), 2 * channels)
+        both = jnp.concatenate([(total[g] + bias) * mask, (total[g + 1] + bias) * mask], axis=-1)
+        out[:, :, lanes] = (both + own[:, :, lanes].astype(jnp.float32) * mask).astype(jnp.bfloat16)
+
+
+def prepare_kernel(nb, vf, own, gain1, flat1, flat2, buf1, buf2, weight1, weight2, held1, held2, sem):
+    first = lax.axis_index("tm") * own.shape[0]
+    copy1 = pltpu.make_async_copy(flat1, held1, sem.at[0])
+    copy2 = pltpu.make_async_copy(flat2, held2, sem.at[1])
+    copy1.start()
+    copy2.start()
+    channels = gain1.shape[0]
+    zero_pads(buf1, channels)
+    zero_pads(buf2, channels)
+    act_tile(buf1, own, first, tracks(nb, vf)[0], own.shape[0], row_of(gain1))
+    copy1.wait()
+    spread(held1, weight1)
+    copy2.wait()
+    spread(held2, weight2)
+
+
+def late_kernel(nb, vf, buf1, weight1, bias1, gain2, _, buf2):
+    frames = buf1.shape[1] // 2
+    inner = buf2.shape[0] - 4
+    f0 = lax.axis_index("tm") * frames + 2
+    valid = tracks(nb, vf)[0]
+    total = conv(buf1, (2,), inner, frames, frames - 2, weight1)
+    hide(total, buf2, range(2, 2 + inner), f0, 4, row_of(bias1), row_of(gain2), [valid] * inner)
+
+
+def early_kernel(nb, vf, prev, gain1, weight1, bias1, gain2, old1, old2, buf1, buf2):
+    frames = prev.shape[0]
+    inner = buf2.shape[0] - 4
+    first = lax.axis_index("tm") * frames
+    valid = tracks(nb, vf)[0]
+    act_tile(buf1, prev, first - frames, valid, 0, row_of(gain1))
+    half = inner // 2
+
+    def body(i, _):
+        x0 = 2 + i * half
+        total = conv(buf1, (x0,), half, frames - 4, 4, weight1)
+        hide(total, buf2, [x0 + g for g in range(half)], first - 2, 0, row_of(bias1), row_of(gain2), [valid] * half)
+        return 0
+
+    lax.fori_loop(0, 2, body, 0)
+
+
+def inner_kernel(nb, vf, own, buf2, weight2, bias2, out):
+    frames = own.shape[0]
+    inner = buf2.shape[0] - 6
+    first = lax.axis_index("tm") * frames
+    valid = tracks(nb, vf)[0]
+    half = inner // 2
+
+    def body(i, _):
+        x0 = 2 + i * half
+        total = conv(buf2, (x0,), half, 0, frames, weight2)
+        finish(total, out, own, [x0 + g for g in range(half)], row_of(bias2), first, valid)
+        return 0
+
+    lax.fori_loop(0, 2, body, 0)
+
+
+def rim_kernel(nb, vf, own, rim, prev_rim, gain1, weight1, bias1, gain2, weight2, bias2, old1, old2, inner, buf1, buf2, out, staged, sem):
+    frames, _, merged = own.shape
+    columns = buf2.shape[0] - 2
+    first = lax.axis_index("tm") * frames
+    valid, left, right = tracks(nb, vf)
+    for side, (x, v) in enumerate(((0, left), (columns + 2, right))):
+        act(buf1, prev_rim[side], first - frames, v, x, 0, row_of(gain1))
+        act(buf1, rim[side], first, v, x, frames, row_of(gain1))
+    total = conv(buf1, (0, columns), 2, frames - 4, frames + 2, weight1)
+    places = (0, 1, columns, columns + 1)
+    hide(total, buf2, places, first - 2, 0, row_of(bias1), row_of(gain2), (left, valid, valid, right))
+    total = conv(buf2, (0, columns - 2), 2, 0, frames, weight2)
+    ends = (0, merged - staged.shape[3])
+    for side, lane in enumerate(ends):
+        lanes = pl.ds(lane, staged.shape[3])
+        mask = there(first, frames, valid)
+        both = jnp.concatenate([(total[2 * side + g] + row_of(bias2)) * mask for g in range(2)], axis=-1)
+        staged[side] = (both + own[:, :, lanes].astype(jnp.float32) * mask).astype(jnp.bfloat16)
+    copies = [pltpu.make_async_copy(staged.at[k], out.at[:, :, pl.ds(lane, staged.shape[3])], sem.at[k]) for k, lane in enumerate(ends)]
+    for copy in copies:
+        copy.start()
+    for copy in copies:
+        copy.wait()
+
+
+LEFT, RIGHT = 3, 4
+
+
+def tracks(nb, vf):
+    me = lax.axis_index("space")
+    tiles = nb.shape[0]
+
+    def of(tile):
+        return jnp.where(tile < tiles, vf[jnp.minimum(tile, tiles - 1)], 0)
+
+    return vf[me], of(nb[me, LEFT]), of(nb[me, RIGHT])
+
+
+def pick_kernel(nb, mine, pair, *outs):
+    tiles = nb.shape[0]
+    me = lax.axis_index("space")
+    for step, out in enumerate(outs):
+        there = lax.rem(me + 2 * (step + 1), tiles)
+        for side, column in ((0, LEFT), (1, RIGHT)):
+            source = nb[there, column]
+
+            @pl.when(source == me)
+            def _():
+                out[side] = mine[1 - side]
+
+            @pl.when(source != me)
+            def _():
+                out[side] = pair[1 - side]
+
+
+def rims_kernel(nb, mine, pair, *rest):
+    received, out = rest[:-1], rest[-1]
+    tiles = nb.shape[0]
+    half = tiles // 2
+    me = lax.axis_index("space")
+    for side, column in ((0, LEFT), (1, RIGHT)):
+        source = nb[me, column]
+        step = lax.rem(me // 2 - source // 2 + tiles, half)
+        at_home = (step == 0) | (source >= tiles)
+
+        @pl.when(at_home & (source == me ^ 1))
+        def _():
+            out[side] = pair[1 - side]
+
+        @pl.when(at_home & (source != me ^ 1))
+        def _():
+            out[side] = mine[1 - side]
+
+        for s, arrived in enumerate(received):
+
+            @pl.when((step == s + 1) & (source < tiles))
+            def _():
+                out[side] = arrived[side]
+
+
+def exchange(own, neighbours, channels):
+    count = lax.axis_size("space")
+    vmem = pl.BlockSpec(memory_space=pltpu.VMEM)
+    smem = pl.BlockSpec(memory_space=pltpu.SMEM)
+    mine = jnp.stack([own[:, :, : 2 * channels], own[:, :, -2 * channels :]])
+    pair = lax.ppermute(mine, "space", [(i, i ^ 1) for i in range(count)])
+    piece = jax.ShapeDtypeStruct(mine.shape, mine.dtype)
+    steps = count // 2 - 1
+    sent = pl.pallas_call(
+        pick_kernel,
+        out_shape=[piece] * steps,
+        in_specs=[smem, vmem, vmem],
+        out_specs=[vmem] * steps,
+        compiler_params=pltpu.CompilerParams(vmem_limit_bytes=8 * 2**20),
+    )(neighbours, mine, pair)
+    received = [
+        lax.ppermute(value, "space", [(i, (i + 2 * (s + 1)) % count) for i in range(count)])
+        for s, value in enumerate(sent)
+    ]
+    return pl.pallas_call(
+        rims_kernel,
+        out_shape=piece,
+        in_specs=[smem] + [vmem] * (2 + steps),
+        out_specs=vmem,
+        compiler_params=pltpu.CompilerParams(vmem_limit_bytes=8 * 2**20),
+    )(neighbours, mine, pair, *received)
+
+
+def call(kernel, cost, outs, ins, args, places=None, **more):
+    flops, moved = cost
+    return pl.pallas_call(
+        kernel,
+        out_shape=outs,
+        in_specs=ins,
+        out_specs=[VM] * len(outs) if places is None else places,
+        cost_estimate=pl.CostEstimate(flops=flops, bytes_accessed=moved, transcendentals=0),
+        compiler_params=pltpu.CompilerParams(vmem_limit_bytes=24 * 2**20),
+        **more,
+    )(*args)
+
+
+VM = pl.BlockSpec(memory_space=pltpu.VMEM)
+SM = pl.BlockSpec(memory_space=pltpu.SMEM)
+HB = pl.BlockSpec(memory_space=pl.ANY)
+
+
+def row_path(video_in, neighbours, valid_frames, gain1, weight1, bias1, gain2, weight2, bias2):
+    own = video_in[:, 0]
+    frames, side, merged = own.shape
+    channels = gain1.shape[0]
+    columns = merged // channels
+    tables = (neighbours, valid_frames)
+    prev = shifted(own, "tm", 1)
+    rim = exchange(own, neighbours, channels)
+    prev_rim = shifted(rim, "tm", 1)
+    one = 2 * 27 * channels * channels * side
+    space1 = pltpu.VMEM((columns + 4, 2 * frames, side, 3 * LANE), jnp.bfloat16)
+    space2 = pltpu.VMEM((columns + 2, frames + 2, side, 3 * LANE), jnp.bfloat16)
+    spaced = pltpu.VMEM((9, 3 * LANE, channels), jnp.bfloat16)
+    flat = pltpu.VMEM((9, channels, 3 * channels), jnp.bfloat16)
+    buf1, buf2, wide1, wide2 = call(
+        prepare_kernel,
+        (one, 4 * weight1.size),
+        [space1, space2, spaced, spaced],
+        [SM, SM, VM, VM, HB, HB],
+        (*tables, own, gain1, jnp.swapaxes(weight1, 1, 2), jnp.swapaxes(weight2, 1, 2)),
+        scratch_shapes=[flat, flat, pltpu.SemaphoreType.DMA((2,))],
+    )
+    (buf2,) = call(
+        late_kernel,
+        (one * 2 * columns, own.size),
+        [space2],
+        [SM, SM, VM, VM, VM, VM, VM],
+        (*tables, buf1, wide1, bias1, gain2, buf2),
+        input_output_aliases={6: 0},
+    )
+    buf1, buf2 = call(
+        early_kernel,
+        (one * 4 * columns, own.size),
+        [space1, space2],
+        [SM, SM, VM, VM, VM, VM, VM, VM, VM],
+        (*tables, prev, gain1, wide1, bias1, gain2, buf1, buf2),
+        input_output_aliases={7: 0, 8: 1},
+    )
+    (inner,) = call(
+        inner_kernel,
+        (one * 4 * columns, own.size),
+        [jax.ShapeDtypeStruct(own.shape, own.dtype)],
+        [SM, SM, VM, VM, VM, VM],
+        (*tables, own, buf2, wide2, bias2),
+    )
+    return own, rim, prev_rim, wide1, wide2, buf1, buf2, inner
+
+
+def row_end(state, tables, gain1, bias1, gain2, bias2):
+    own, rim, prev_rim, wide1, wide2, buf1, buf2, inner = state
+    space1, space2 = pltpu.VMEM(buf1.shape, buf1.dtype), pltpu.VMEM(buf2.shape, buf2.dtype)
+    _, _, out = call(
+        rim_kernel,
+        (own.size * 1000, own.size),
+        [space1, space2, jax.ShapeDtypeStruct(own.shape, own.dtype)],
+        [SM, SM] + [VM] * 11 + [HB],
+        (*tables, own, rim, prev_rim, gain1, wide1, bias1, gain2, wide2, bias2, buf1, buf2, inner),
+        places=[VM, VM, HB],
+        input_output_aliases={11: 0, 12: 1, 13: 2},
+        scratch_shapes=[pltpu.VMEM(rim.shape, rim.dtype), pltpu.SemaphoreType.DMA((2,))],
+    )
+    return out[:, None]
+
+
+def on_device(*args):
+    video_in, neighbours, valid_frames, gain1, weight1, bias1, gain2, weight2, bias2 = args
+    frames_dev, tiles_dev = video_in.shape[:2]
+    tiles = neighbours.shape[0]
+    if tiles_dev != 1 or tiles % 2 or frames_dev != 4:
+        return general_path(*args)
+    state = row_path(*args)
+    beyond = jnp.concatenate([neighbours[:, :LEFT], neighbours[:, RIGHT + 1 :]], axis=1)
+    return lax.cond(
+        jnp.any(beyond < tiles),
+        lambda state, args: general_path(*args),
+        lambda state, args: row_end(state, args[1:3], gain1, bias1, gain2, bias2),
+        state,
+        args,
+    )
+
+
 def solution(mesh):
     in_specs = (P("tm", "space", None, None), P(), P(), P(), P(), P(), P(), P(), P())
     out_specs = P("tm", "space", None, None)

time: 150 us -> 46.3 us (0.31); the launches traced: 147 us -> 45.8 us
  blocking collectives: 68.9 us -> 0 us
  local copies, waits for them, and re-layouts: 33 us -> 1.73 us
  Pallas kernels: 0 us -> 27.6 us
  matrix products: 18.2 us -> 0 us
  other arithmetic: 6.69 us -> 0.75 us
  starting transfers between devices: 17.5 us -> 13.5 us
    all_gather x2 -> x0, blocking collectives: 68.9 us -> none  [extend(): lax.all_gather(edge_pack(activation), 'space', axis=1, tiled=True)]
    pallas_call x0 -> x7, Pallas kernels: none -> 27.6 us  [the longest x5 26.1 us: call(): pl.pallas_call(kernel, out_shape=outs, in_specs=ins, out_specs=[VM] * len...]
    dot_general x22 -> x0, matrix products: 18.2 us -> none  [the longest x18 16.4 us: conv_tile(): jnp.dot(window, weight[time_off * 3 + row_off], preferred_element_type=jn...]
    ppermute x6 -> x2, starting transfers between devices: 17.5 us -> 4.58 us  [shifted(): lax.ppermute(value, axis, [(source, source + steps) for source in range(f...]
    slice x18 -> x1, local copies, waits for them, and re-layouts: 10.7 us -> 0.83 us  [on_device(): neighbours[:, :LEFT]]
    cond x32 -> x0, local copies, waits for them, and re-layouts: 9.47 us -> none
    ppermute x0 -> x4, starting transfers between devices: none -> 8.93 us  [the longest x3 6.53 us: exchange(): lax.ppermute(value, 'space', [(i, (i + 2 * (s + 1)) % count) for i in ran...]
    another operation x7 -> x1, local copies, waits for them, and re-layouts: 8.49 us -> 0.83 us  [exchange(): mine = jnp.stack([own[:, :, :2 * channels], own[:, :, -2 * channels:]])]
  transfers between devices with their start and end apart: 6 -> 6, of which waited for: 2 -> 1; matrix products, arithmetic and copies ran while one was open for 1% -> 5% of each run, Pallas kernels for 0% -> 47%
where the time goes in v2:
time: 46.3 us; the launch traced here: 45.8 us
  Pallas kernels  27.6 us (60%)
  starting transfers between devices  13.5 us (29%)
  local copies, waits for them, and re-layouts  1.73 us (4%)
  between operations  1.06 us (2%)
  waiting for transfers between devices  0.92 us (2%)
  other arithmetic  0.75 us (2%)
    pallas_call x5, Pallas kernels, call(): pl.pallas_call(kernel, out_shape=outs, in_specs=ins, out_specs=[VM] * len...  26.1 us
    ppermute x3, starting transfers between devices, exchange(): lax.ppermute(value, 'space', [(i, (i + 2 * (s + 1)) % count) for i in ran...  6.53 us
    ppermute x2, starting transfers between devices, shifted(): lax.ppermute(value, axis, [(source, source + steps) for source in range(f...  4.58 us
    ppermute x1, starting transfers between devices, exchange(): pair = lax.ppermute(mine, 'space', [(i, i ^ 1) for i in range(count)])  2.4 us
  transfers between devices with their start and end apart: 6, of which 1 were waited for; matrix products, arithmetic and copies ran while one was open for 5% of the time, Pallas kernels for 47%

profile of v2, /device:TPU:0, one launch (start us, length us, event | category | flops | bytes accessed | tf_op | source)
XLA Modules:
  0.0 45.8 jit_solution(12081230667322929496)
XLA Ops:
  0.0 3.2 %collective-permute-start.11 = (bf16[4,16,3072]{2,1,0:T(8,128)(2,1)}, bf16[4,16,3072]{2,1,0:T(8,128)(2,1)}, u32[]{:S(2)}, u32[]{:S(2)}) collective-permute-start(bf16[4,16,3072]{2,1,0:T(8,128)(2,1)} %bitcast.249), channel_id=1, source_target_pairs={{0,8},{8,16},{16,24},{1,9},{9,17},{17,25},{2,10},{10,18},{18,26},{... | collective-permute-start | bytes 1179656 | tf_op jit(solution)/shard_map/ppermute | solution.py:17
  3.2 0.8 %slice_bitcast_fusion.38 = (bf16[1,4,16,384]{3,2,1,0:T(8,128)(2,1)S(1)}, bf16[1,4,16,384]{3,2,1,0:T(8,128)(2,1)S(1)}) fusion(bf16[4,16,3072]{2,1,0:T(8,128)(2,1)} %bitcast.250), kind=kLoop, calls=%fused_computation.175 | loop fusion | bytes 196608 | tf_op jit(solution)/shard_map/stack | solution.py:416
  4.0 0.0 copy-start
  4.0 2.4 %collective-permute-start.6 = (bf16[2,4,16,384]{3,2,1,0:T(8,128)(2,1)S(1)}, bf16[2,4,16,384]{3,2,1,0:T(8,128)(2,1)S(1)}, u32[]{:S(2)}, u32[]{:S(2)}) collective-permute-start(bf16[2,4,16,384]{3,2,1,0:T(8,128)(2,1)S(1)} %pad_maximum_fusion.8.mine), channel_id=1, source_target_pairs={{0,1},{1,0},{2,3},{3,2},{4,5},{5,4},{6,7},{7,6},{8,9},{9,8},{10,11... | collective-permute-start | bytes 294920 | tf_op jit(solution)/shard_map/ppermute | solution.py:417
  6.4 0.8 %fusion.84 = (s32[8,3]{1,0:T(8,128)S(1)}, s32[8,3]{1,0:T(8,128)S(1)}) fusion(s32[8,8]{1,0:T(8,128)} %nb.11), kind=kLoop, calls=%fused_computation.189 | loop fusion | bytes 384 | tf_op jit(solution)/shard_map/slice | solution.py:529
  7.3 0.7 %fusion.72 = pred[]{:T(512)} fusion(s32[8,3]{1,0:T(8,128)S(1)} %get-tuple-element.381, s32[8,3]{1,0:T(8,128)S(1)} %get-tuple-element.380), kind=kLoop, calls=%fused_computation.177 | loop fusion | flops 143 | bytes 193 | tf_op jit(solution)/shard_map/reduce_or | solution.py:531
  8.6 0.9 %collective-permute-done.6.pair = bf16[2,4,16,384]{3,2,1,0:T(8,128)(2,1)S(1)} collective-permute-done((bf16[2,4,16,384]{3,2,1,0:T(8,128)(2,1)S(1)}, bf16[2,4,16,384]{3,2,1,0:T(8,128)(2,1)S(1)}, u32[]{:S(2)}, u32[]{:S(2)}) %collective-permute-start.6) | collective-permute-done | bytes 98336 | tf_op jit(solution)/shard_map/ppermute | solution.py:417
  9.5 0.0 copy-start.2
  9.5 0.8 %shard_map.93 = (bf16[2,4,16,384]{3,2,1,0:T(8,128)(2,1)S(1)}, bf16[2,4,16,384]{3,2,1,0:T(8,128)(2,1)S(1)}, bf16[2,4,16,384]{3,2,1,0:T(8,128)(2,1)S(1)}) custom-call(s32[8,8]{1,0:T(8,128)} %nb.11, bf16[2,4,16,384]{3,2,1,0:T(8,128)(2,1)S(1)} %pad_maximum_fusion.8.mine, bf16[2,4,16,384]{3,2,1,0:T(8,128)(2,1)S(1)} %collective-permute-done.6.pair), custom_call_target="tpu_custom_call" | custom-call | tf_op jit(solution)/shard_map/pallas_call | solution.py:420
  10.4 2.6 %collective-permute-start.7 = (bf16[2,4,16,384]{3,2,1,0:T(8,128)(2,1)S(1)}, bf16[2,4,16,384]{3,2,1,0:T(8,128)(2,1)S(1)}, u32[]{:S(2)}, u32[]{:S(2)}) collective-permute-start(bf16[2,4,16,384]{3,2,1,0:T(8,128)(2,1)S(1)} %get-tuple-element.137), channel_id=1, source_target_pairs={{0,2},{1,3},{2,4},{3,5},{4,6},{5,7},{6,0},{7,1},{8,10},{9,11},{10,... | collective-permute-start | bytes 294920 | tf_op jit(solution)/shard_map/ppermute | solution.py:428
  13.0 2.6 %collective-permute-start.8 = (bf16[2,4,16,384]{3,2,1,0:T(8,128)(2,1)S(1)}, bf16[2,4,16,384]{3,2,1,0:T(8,128)(2,1)S(1)}, u32[]{:S(2)}, u32[]{:S(2)}) collective-permute-start(bf16[2,4,16,384]{3,2,1,0:T(8,128)(2,1)S(1)} %get-tuple-element.138), channel_id=1, source_target_pairs={{0,4},{1,5},{2,6},{3,7},{4,0},{5,1},{6,2},{7,3},{8,12},{9,13},{10,... | collective-permute-start | bytes 294920 | tf_op jit(solution)/shard_map/ppermute | solution.py:428
  15.6 1.3 %collective-permute-start.9 = (bf16[2,4,16,384]{3,2,1,0:T(8,128)(2,1)S(1)}, bf16[2,4,16,384]{3,2,1,0:T(8,128)(2,1)S(1)}, u32[]{:S(2)}, u32[]{:S(2)}) collective-permute-start(bf16[2,4,16,384]{3,2,1,0:T(8,128)(2,1)S(1)} %get-tuple-element.139), channel_id=1, source_target_pairs={{0,6},{1,7},{2,0},{3,1},{4,2},{5,3},{6,4},{7,5},{8,14},{9,15},{10,... | collective-permute-start | bytes 294920 | tf_op jit(solution)/shard_map/ppermute | solution.py:428
  16.9 0.0 copy-done
  16.9 0.0 copy-done.2
  16.9 0.0 copy-start.20
  16.9 0.0 copy-start.21
  16.9 0.0 copy-start.23
  16.9 0.0 copy-start.24
  16.9 5.5 %shard_map.95 = (bf16[20,8,16,768]{3,2,1,0:T(8,128)(2,1)S(1)}, bf16[18,6,16,768]{3,2,1,0:T(8,128)(2,1)S(1)}, bf16[9,768,192]{2,1,0:T(8,128)(2,1)S(1)}, bf16[9,768,192]{2,1,0:T(8,128)(2,1)S(1)}) custom-call(s32[8,8]{1,0:T(8,128)} %nb.11, s32[8]{0:T(128)} %vf.7, bf16[4,16,3072]{2,1,0:T(8,128)(2,1)} %bitcast.251, f32[192]{0:T(256)} %gain1.3, ...), custom_call_target="tpu_custom_call" | custom-call | flops 31850496 | bytes 3981312 | tf_op jit(solution)/shard_map/pallas_call | solution.py:442
  22.5 0.0 copy-done.20
  22.5 0.0 copy-done.21
  22.5 0.0 copy-done.23
  22.5 0.0 copy-done.24
  22.5 0.0 copy-start.1
  22.5 0.0 copy-start.3
  22.6 0.0 copy-start.22
  22.6 2.6 %shard_map.96.old2 = bf16[18,6,16,768]{3,2,1,0:T(8,128)(2,1)S(1)} custom-call(s32[8,8]{1,0:T(8,128)S(1)} %copy-done.20, s32[8]{0:T(128)S(1)} %copy-done.24, bf16[20,8,16,768]{3,2,1,0:T(8,128)(2,1)S(1)} %get-tuple-element.142.buf1.old1, bf16[9,768,192]{2,1,0:T(8,128)(2,1)S(1)} %get-tuple-element.392.weight1, ...), custom_call_target="tpu_custom_call", output_to_operand_aliasing={{}: (6, {})} | custom-call | flops 1019215872 | bytes 196608 | tf_op jit(solution)/shard_map/pallas_call | solution.py:442
  25.2 0.0 collective-permute-done.7.rest_0_
  25.2 0.0 collective-permute-done.8.rest_1_
  25.2 0.0 collective-permute-done.9.rest_2_
  25.2 0.0 copy-done.1
  25.2 0.0 copy-done.3
  25.2 0.7 %shard_map.94 = bf16[2,4,16,384]{3,2,1,0:T(8,128)(2,1)S(1)} custom-call(s32[8,8]{1,0:T(8,128)S(1)} %copy-done.20, bf16[2,4,16,384]{3,2,1,0:T(8,128)(2,1)S(1)} %copy-done.1, bf16[2,4,16,384]{3,2,1,0:T(8,128)(2,1)S(1)} %copy-done.3, bf16[2,4,16,384]{3,2,1,0:T(8,128)(2,1)S(1)} %collective-permute-done.7.rest_0_, ...), custom_call_target="tpu_custom_call" | custom-call | tf_op jit(solution)/shard_map/pallas_call | solution.py:431
  25.9 0.0 copy-start.4
  25.9 0.0 copy-start.25
  25.9 1.4 %collective-permute-start.10 = (bf16[2,4,16,384]{3,2,1,0:T(8,128)(2,1)S(1)}, bf16[2,4,16,384]{3,2,1,0:T(8,128)(2,1)S(1)}, u32[]{:S(2)}, u32[]{:S(2)}) collective-permute-start(bf16[2,4,16,384]{3,2,1,0:T(8,128)(2,1)S(1)} %shard_map.94), channel_id=1, source_target_pairs={{0,8},{8,16},{16,24},{1,9},{9,17},{17,25},{2,10},{10,18},{18,26},{... | collective-permute-start | bytes 294920 | tf_op jit(solution)/shard_map/ppermute | solution.py:17
  27.4 0.0 collective-permute-done.11.prev
  27.4 0.0 copy-done.22
  27.4 7.2 %shard_map.97 = (bf16[20,8,16,768]{3,2,1,0:T(8,128)(2,1)S(1)}, bf16[18,6,16,768]{3,2,1,0:T(8,128)(2,1)S(1)}) custom-call(s32[8,8]{1,0:T(8,128)S(1)} %copy-done.20, s32[8]{0:T(128)S(1)} %copy-done.24, bf16[4,16,3072]{2,1,0:T(8,128)(2,1)} %collective-permute-done.11.prev, f32[192]{0:T(256)S(1)} %copy-done.22, ...), custom_call_target="tpu_custom_call", output_to_operand_aliasing={{0}: (7, {}), {1}: (8, {})} | custom-call | flops 2038431744 | bytes 196608 | tf_op jit(solution)/shard_map/pallas_call | solution.py:442
  34.6 0.0 copy-done.4
  34.6 0.0 copy-done.25
  34.6 4.6 %shard_map.98 = bf16[4,16,3072]{2,1,0:T(8,128)(2,1)} custom-call(s32[8,8]{1,0:T(8,128)S(1)} %copy-done.20, s32[8]{0:T(128)S(1)} %copy-done.24, bf16[4,16,3072]{2,1,0:T(8,128)(2,1)S(1)} %bitcast.252, bf16[18,6,16,768]{3,2,1,0:T(8,128)(2,1)S(1)} %get-tuple-element.398.buf2, bf16[9,768,192]{2,1,0:T(8,128)(2,1)S(1)} %get-tuple-element.395.weight2, f32[192]{0:T(256)S(1)} %copy-done.25), custom_call_target="tpu_custom_call" | custom-call | flops 2038431744 | bytes 196608 | tf_op jit(solution)/shard_map/pallas_call | solution.py:442
  39.2 0.0 collective-permute-done.10
  39.2 6.4 %conditional.3 = ((bf16[4,1,16,3072]{3,2,0,1:T(8,128)(2,1)})) conditional(s32[]{:T(128)} %convert_element_type.108, (s32[8,8]{1,0:T(8,128)S(1)}, s32[8]{0:T(128)S(1)}, bf16[4,16,3072]{2,1,0:T(8,128)(2,1)S(1)}, bf16[2,4,16,384]{3,2,1,0:T(8,128)(2,1)S(1)}, bf16[2,4,16,384]{3,2,1,0:T(8,128)(2,1)S(1)}, /*index=5*/f32[192]{0:T(256)S(1)}, ...), branch_computations={%region_1.0_spmd, %region_2.9_spmd} | conditional | flops 4110178304 | bytes 214559840 | solution.py:530
  39.2 6.2 %branch_0_fun.1 = (bf16[20,8,16,768]{3,2,1,0:T(8,128)(2,1)S(1)}, bf16[18,6,16,768]{3,2,1,0:T(8,128)(2,1)S(1)}, bf16[4,16,3072]{2,1,0:T(8,128)(2,1)}) custom-call(s32[8,8]{1,0:T(8,128)S(1)} %get-tuple-element.91.nb, s32[8]{0:T(128)S(1)} %get-tuple-element.92.vf, ...), custom_call_target="tpu_custom_call", output_to_operand_aliasing={{0}: (11, {}), {1}: (12, {}), {2}: (13, {})} | custom-call | flops 196608000 | bytes 196608 | tf_op jit(solution)/shard_map/cond/branch_0_fun/pallas_call | solution.py:442
  (1 shorter events, 0.0 us)
Async XLA Ops:
  0.0 27.4 %collective-permute-start.11 = (bf16[4,16,3072]{2,1,0:T(8,128)(2,1)}, bf16[4,16,3072]{2,1,0:T(8,128)(2,1)}, u32[]{:S(2)}, u32[]{:S(2)}) collective-permute-start(bf16[4,16,3072]{2,1,0:T(8,128)(2,1)} %bitcast.249), channel_id=1, source_target_pairs={{0,8},{8,16},{16,24},{1,9},{9,17},{17,25},{2,10},{10,18},{18,26},{... | collective-permute-start | bytes 1179656 | tf_op jit(solution)/shard_map/ppermute | solution.py:17
  4.0 12.9 %copy-start = (bf16[2,4,16,384]{3,2,1,0:T(8,128)(2,1)}, bf16[2,4,16,384]{3,2,1,0:T(8,128)(2,1)S(1)}, u32[]{:S(2)}) copy-start(bf16[2,4,16,384]{3,2,1,0:T(8,128)(2,1)S(1)} %pad_maximum_fusion.8.mine) | copy-start | bytes 294916
  4.0 5.5 %collective-permute-start.6 = (bf16[2,4,16,384]{3,2,1,0:T(8,128)(2,1)S(1)}, bf16[2,4,16,384]{3,2,1,0:T(8,128)(2,1)S(1)}, u32[]{:S(2)}, u32[]{:S(2)}) collective-permute-start(bf16[2,4,16,384]{3,2,1,0:T(8,128)(2,1)S(1)} %pad_maximum_fusion.8.mine), channel_id=1, source_target_pairs={{0,1},{1,0},{2,3},{3,2},{4,5},{5,4},{6,7},{7,6},{8,9},{9,8},{10,11... | collective-permute-start | bytes 294920 | tf_op jit(solution)/shard_map/ppermute | solution.py:417
  9.5 7.4 %copy-start.2 = (bf16[2,4,16,384]{3,2,1,0:T(8,128)(2,1)}, bf16[2,4,16,384]{3,2,1,0:T(8,128)(2,1)S(1)}, u32[]{:S(2)}) copy-start(bf16[2,4,16,384]{3,2,1,0:T(8,128)(2,1)S(1)} %collective-permute-done.6.pair) | copy-start | bytes 294916
  10.4 14.8 %collective-permute-start.7 = (bf16[2,4,16,384]{3,2,1,0:T(8,128)(2,1)S(1)}, bf16[2,4,16,384]{3,2,1,0:T(8,128)(2,1)S(1)}, u32[]{:S(2)}, u32[]{:S(2)}) collective-permute-start(bf16[2,4,16,384]{3,2,1,0:T(8,128)(2,1)S(1)} %get-tuple-element.137), channel_id=1, source_target_pairs={{0,2},{1,3},{2,4},{3,5},{4,6},{5,7},{6,0},{7,1},{8,10},{9,11},{10,... | collective-permute-start | bytes 294920 | tf_op jit(solution)/shard_map/ppermute | solution.py:428
  13.0 12.2 %collective-permute-start.8 = (bf16[2,4,16,384]{3,2,1,0:T(8,128)(2,1)S(1)}, bf16[2,4,16,384]{3,2,1,0:T(8,128)(2,1)S(1)}, u32[]{:S(2)}, u32[]{:S(2)}) collective-permute-start(bf16[2,4,16,384]{3,2,1,0:T(8,128)(2,1)S(1)} %get-tuple-element.138), channel_id=1, source_target_pairs={{0,4},{1,5},{2,6},{3,7},{4,0},{5,1},{6,2},{7,3},{8,12},{9,13},{10,... | collective-permute-start | bytes 294920 | tf_op jit(solution)/shard_map/ppermute | solution.py:428
  15.6 9.6 %collective-permute-start.9 = (bf16[2,4,16,384]{3,2,1,0:T(8,128)(2,1)S(1)}, bf16[2,4,16,384]{3,2,1,0:T(8,128)(2,1)S(1)}, u32[]{:S(2)}, u32[]{:S(2)}) collective-permute-start(bf16[2,4,16,384]{3,2,1,0:T(8,128)(2,1)S(1)} %get-tuple-element.139), channel_id=1, source_target_pairs={{0,6},{1,7},{2,0},{3,1},{4,2},{5,3},{6,4},{7,5},{8,14},{9,15},{10,... | collective-permute-start | bytes 294920 | tf_op jit(solution)/shard_map/ppermute | solution.py:428
  16.9 5.6 %copy-start.20 = (s32[8,8]{1,0:T(8,128)S(1)}, s32[8,8]{1,0:T(8,128)}, u32[]{:S(2)}) copy-start(s32[8,8]{1,0:T(8,128)} %nb.11) | copy-start | bytes 772
  16.9 5.6 %copy-start.21 = (f32[192]{0:T(256)S(1)}, f32[192]{0:T(256)}, u32[]{:S(2)}) copy-start(f32[192]{0:T(256)} %bias1.3) | copy-start | bytes 2308
  16.9 5.6 %copy-start.23 = (f32[192]{0:T(256)S(1)}, f32[192]{0:T(256)}, u32[]{:S(2)}) copy-start(f32[192]{0:T(256)} %gain2.3) | copy-start | bytes 2308
  16.9 5.6 %copy-start.24 = (s32[8]{0:T(128)S(1)}, s32[8]{0:T(128)}, u32[]{:S(2)}) copy-start(s32[8]{0:T(128)} %vf.7) | copy-start | bytes 100
  22.5 2.7 %copy-start.1 = (bf16[2,4,16,384]{3,2,1,0:T(8,128)(2,1)S(1)}, bf16[2,4,16,384]{3,2,1,0:T(8,128)(2,1)}, u32[]{:S(2)}) copy-start(bf16[2,4,16,384]{3,2,1,0:T(8,128)(2,1)} %copy-done) | copy-start | bytes 294916
  22.5 2.7 %copy-start.3 = (bf16[2,4,16,384]{3,2,1,0:T(8,128)(2,1)S(1)}, bf16[2,4,16,384]{3,2,1,0:T(8,128)(2,1)}, u32[]{:S(2)}) copy-start(bf16[2,4,16,384]{3,2,1,0:T(8,128)(2,1)} %copy-done.2) | copy-start | bytes 294916
  22.6 4.8 %copy-start.22 = (f32[192]{0:T(256)S(1)}, f32[192]{0:T(256)}, u32[]{:S(2)}) copy-start(f32[192]{0:T(256)} %gain1.3) | copy-start | bytes 2308
  25.9 8.7 %copy-start.4 = (bf16[4,1,16,3072]{3,2,1,0:T(8,128)(2,1)S(1)}, bf16[4,1,16,3072]{3,2,1,0:T(8,128)(2,1)}, u32[]{:S(2)}) copy-start(bf16[4,1,16,3072]{3,2,1,0:T(8,128)(2,1)} %param.15) | copy-start | bytes 1179652
  25.9 8.7 %copy-start.25 = (f32[192]{0:T(256)S(1)}, f32[192]{0:T(256)}, u32[]{:S(2)}) copy-start(f32[192]{0:T(256)} %bias2.1) | copy-start | bytes 2308
  25.9 13.2 %collective-permute-start.10 = (bf16[2,4,16,384]{3,2,1,0:T(8,128)(2,1)S(1)}, bf16[2,4,16,384]{3,2,1,0:T(8,128)(2,1)S(1)}, u32[]{:S(2)}, u32[]{:S(2)}) collective-permute-start(bf16[2,4,16,384]{3,2,1,0:T(8,128)(2,1)S(1)} %shard_map.94), channel_id=1, source_target_pairs={{0,8},{8,16},{16,24},{1,9},{9,17},{17,25},{2,10},{10,18},{18,26},{... | collective-permute-start | bytes 294920 | tf_op jit(solution)/shard_map/ppermute | solution.py:17

commit v3 on v2

--- a/solution.py
+++ b/solution.py
@@ -202,31 +202,37 @@
     lax.fori_loop(0, columns, body, 0)
 
 
-def spread(flat, weight):
+def spread_one(flat, weight, p, q):
     channels = weight.shape[2]
     zero = jnp.zeros((LANE - channels, channels), weight.dtype)
-
-    def body(p, _):
-        for q in range(3):
-            turned = flat[3 * p + q].T
-            for r in range(3):
-                weight[p * 3 + r, q * LANE : q * LANE + channels] = turned[r * channels : (r + 1) * channels]
-                weight[p * 3 + r, q * LANE + channels : (q + 1) * LANE] = zero
-        return 0
-
-    lax.fori_loop(0, 3, body, 0)
-
-
-def conv(buf, starts, width, f0, frames, weight):
-    side = buf.shape[2]
-    total = None
-    for p in range(3):
-        for r in range(3):
-            parts = [buf[pl.ds(x0 + r, width), f0 + p : f0 + p + frames] for x0 in starts]
-            rows = parts[0] if len(parts) == 1 else jnp.concatenate(parts, axis=0)
-            term = jnp.dot(rows.reshape(-1, 3 * LANE), weight[p * 3 + r], preferred_element_type=jnp.float32)
-            total = term if total is None else total + term
-    return total.reshape(len(starts) * width, frames, side, weight.shape[2])
+    turned = flat[3 * p + q].T
+    for r in range(3):
+        weight[p * 3 + r, q * LANE : q * LANE + channels] = turned[r * channels : (r + 1) * channels]
+        weight[p * 3 + r, q * LANE + channels : (q + 1) * LANE] = zero
+
+
+def spreads(flat, weight):
+    return [partial(spread_one, flat, weight, p, q) for p in range(3) for q in range(3)]
+
+
+def conv(buf, starts, width, f0, frames, weight, accs, beside=()):
+    side, channels = buf.shape[2], weight.shape[2]
+    totals = [None] * len(starts)
+    done = 0
+    for tap in range(9):
+        p, r = divmod(tap, 3)
+        for k, x0 in enumerate(starts):
+            rows = buf[x0 + r : x0 + r + width, f0 + p : f0 + p + frames].reshape(-1, 3 * LANE)
+            term = jnp.dot(rows, weight[tap], preferred_element_type=jnp.float32)
+            totals[k] = term if totals[k] is None else totals[k] + term
+        while done * 9 < len(beside) * (tap + 1):
+            beside[done]()
+            done += 1
+    views = []
+    for total, acc in zip(totals, accs):
+        acc[0:width, 0:frames] = total.reshape(width, frames, side, channels)
+        views += [acc.at[g, 0:frames] for g in range(width)]
+    return views
 
 
 def there(f0, frames, valid):
@@ -241,95 +247,97 @@
         put(buf, x + j, at, normed(values[:, :, j * channels : (j + 1) * channels], gain))
 
 
-def act_tile(buf, tile, f0, valid, at, gain):
-    channels = gain.shape[1]
-
-    def body(k, _):
-        lanes = pl.ds(pl.multiple_of(k * 2 * channels, 128), 2 * channels)
-        act(buf, tile[:, :, lanes], f0, valid, 2 + 2 * k, at, gain)
-        return 0
-
-    lax.fori_loop(0, tile.shape[2] // (2 * channels), body, 0)
+def acts(buf, tile, f0, valid, at, gain):
+    lanes = 2 * gain.shape[1]
+
+    def one(k):
+        act(buf, tile[:, :, k * lanes : (k + 1) * lanes], f0, valid, 2 + 2 * k, at, gain)
+
+    return [partial(one, k) for k in range(tile.shape[2] // lanes)]
 
 
 def row_of(ref):
     return ref[...].reshape(1, -1)
 
 
-def hide(total, buf, places, f0, at, bias, gain, valids):
-    for g, (x, valid) in enumerate(zip(places, valids)):
-        put(buf, x, at, normed((total[g] + bias) * there(f0, total.shape[1], valid), gain))
-
-
-def finish(total, out, own, places, bias, f0, valid):
+def hides(totals, buf, places, f0, at, bias, gain, valids):
+    def one(g):
+        total = totals[g][...]
+        put(buf, places[g], at, normed((total + bias) * there(f0, total.shape[0], valids[g]), gain))
+
+    return [partial(one, g) for g in range(len(places))]
+
+
+def ended(totals, own, lanes, bias, f0, valid):
+    parts = [total[...] + bias for total in totals]
+    mask = there(f0, parts[0].shape[0], valid)
+    both = jnp.concatenate([part * mask for part in parts], axis=-1)
+    return (both + own[:, :, lanes].astype(jnp.float32) * mask).astype(jnp.bfloat16)
+
+
+def finishes(totals, out, own, x0, bias, f0, valid):
     channels = bias.shape[1]
-    mask = there(f0, total.shape[1], valid)
-    for g in range(0, len(places), 2):
-        x = places[g]
-        lanes = pl.ds(x * channels if isinstance(x, int) else pl.multiple_of(x * channels, 128), 2 * channels)
-        both = jnp.concatenate([(total[g] + bias) * mask, (total[g + 1] + bias) * mask], axis=-1)
-        out[:, :, lanes] = (both + own[:, :, lanes].astype(jnp.float32) * mask).astype(jnp.bfloat16)
-
-
-def prepare_kernel(nb, vf, own, gain1, flat1, flat2, buf1, buf2, weight1, weight2, held1, held2, sem):
-    first = lax.axis_index("tm") * own.shape[0]
-    copy1 = pltpu.make_async_copy(flat1, held1, sem.at[0])
-    copy2 = pltpu.make_async_copy(flat2, held2, sem.at[1])
-    copy1.start()
-    copy2.start()
+
+    def one(g):
+        lanes = pl.ds((x0 + g) * channels, 2 * channels)
+        out[:, :, lanes] = ended(totals[g : g + 2], own, lanes, bias, f0, valid)
+
+    return [partial(one, g) for g in range(0, len(totals), 2)]
+
+
+def run(works):
+    for work in works:
+        work()
+
+
+def tile_kernel(nb, vf, own, gain1, buf1, buf2, flag):
+    frames = own.shape[0]
     channels = gain1.shape[0]
+    tiles = nb.shape[0]
+    beyond = jnp.int32(0)
+    for tile in range(tiles):
+        for k in range(nb.shape[1]):
+            if k not in (LEFT, RIGHT):
+                beyond = jnp.maximum(beyond, tiles - nb[tile, k])
+    flag[0] = beyond
     zero_pads(buf1, channels)
     zero_pads(buf2, channels)
-    act_tile(buf1, own, first, tracks(nb, vf)[0], own.shape[0], row_of(gain1))
-    copy1.wait()
-    spread(held1, weight1)
-    copy2.wait()
-    spread(held2, weight2)
-
-
-def late_kernel(nb, vf, buf1, weight1, bias1, gain2, _, buf2):
+    run(acts(buf1, own, lax.axis_index("tm") * frames, tracks(nb, vf)[0], frames, row_of(gain1)))
+
+
+def late_kernel(nb, vf, buf1, flat1, flat2, bias1, gain2, _, weight1, weight2, buf2, acc):
     frames = buf1.shape[1] // 2
     inner = buf2.shape[0] - 4
     f0 = lax.axis_index("tm") * frames + 2
     valid = tracks(nb, vf)[0]
-    total = conv(buf1, (2,), inner, frames, frames - 2, weight1)
-    hide(total, buf2, range(2, 2 + inner), f0, 4, row_of(bias1), row_of(gain2), [valid] * inner)
-
-
-def early_kernel(nb, vf, prev, gain1, weight1, bias1, gain2, old1, old2, buf1, buf2):
+    run(spreads(flat1, weight1))
+    totals = conv(buf1, (2,), inner, frames, frames - 2, weight1, (acc,), spreads(flat2, weight2))
+    run(hides(totals, buf2, range(2, 2 + inner), f0, 4, row_of(bias1), row_of(gain2), [valid] * inner))
+
+
+def main_kernel(nb, vf, own, prev, gain1, weight1, bias1, gain2, weight2, bias2, old1, old2, buf1, buf2, out, *accs):
     frames = prev.shape[0]
-    inner = buf2.shape[0] - 4
+    columns = buf2.shape[0] - 2
     first = lax.axis_index("tm") * frames
     valid = tracks(nb, vf)[0]
-    act_tile(buf1, prev, first - frames, valid, 0, row_of(gain1))
-    half = inner // 2
-
-    def body(i, _):
-        x0 = 2 + i * half
-        total = conv(buf1, (x0,), half, frames - 4, 4, weight1)
-        hide(total, buf2, [x0 + g for g in range(half)], first - 2, 0, row_of(bias1), row_of(gain2), [valid] * half)
-        return 0
-
-    lax.fori_loop(0, 2, body, 0)
-
-
-def inner_kernel(nb, vf, own, buf2, weight2, bias2, out):
-    frames = own.shape[0]
-    inner = buf2.shape[0] - 6
-    first = lax.axis_index("tm") * frames
-    valid = tracks(nb, vf)[0]
-    half = inner // 2
-
-    def body(i, _):
-        x0 = 2 + i * half
-        total = conv(buf2, (x0,), half, 0, frames, weight2)
-        finish(total, out, own, [x0 + g for g in range(half)], row_of(bias2), first, valid)
-        return 0
-
-    lax.fori_loop(0, 2, body, 0)
-
-
-def rim_kernel(nb, vf, own, rim, prev_rim, gain1, weight1, bias1, gain2, weight2, bias2, old1, old2, inner, buf1, buf2, out, staged, sem):
+    half = (columns - 4) // 2
+    wide, rest = half + 2, columns - 4 - half
+    before = acts(buf1, prev, first - frames, valid, 0, row_of(gain1))
+    needed = (wide + 3) // 2
+    norm = (first - 2, 0, row_of(bias1), row_of(gain2), [valid] * columns)
+    run(before[:needed])
+    totals = conv(buf1, (2,), wide, frames - 4, 4, weight1, accs[0:1], before[needed:])
+    works = hides(totals, buf2, range(2, 2 + wide), *norm)
+    totals = conv(buf1, (2 + wide,), rest, frames - 4, 4, weight1, accs[1:2], works)
+    works = hides(totals, buf2, range(2 + wide, columns), *norm)
+    totals = conv(buf2, (2,), half, 0, frames, weight2, accs[2:3], works)
+    works = finishes(totals, out, own, 2, row_of(bias2), first, valid)
+    totals = conv(buf2, (2 + half,), rest, 0, frames, weight2, accs[3:4], works)
+    run(finishes(totals, out, own, 2 + half, row_of(bias2), first, valid))
+
+
+def rim_kernel(nb, vf, own, rim, prev_rim, gain1, weight1, bias1, gain2, weight2, bias2, old1, old2, inner, buf1, buf2, out, *scratch):
+    *accs, staged, sem = scratch
     frames, _, merged = own.shape
     columns = buf2.shape[0] - 2
     first = lax.axis_index("tm") * frames
@@ -337,19 +345,16 @@
     for side, (x, v) in enumerate(((0, left), (columns + 2, right))):
         act(buf1, prev_rim[side], first - frames, v, x, 0, row_of(gain1))
         act(buf1, rim[side], first, v, x, frames, row_of(gain1))
-    total = conv(buf1, (0, columns), 2, frames - 4, frames + 2, weight1)
+    totals = conv(buf1, (0, columns), 2, frames - 4, frames + 2, weight1, accs[0:2])
     places = (0, 1, columns, columns + 1)
-    hide(total, buf2, places, first - 2, 0, row_of(bias1), row_of(gain2), (left, valid, valid, right))
-    total = conv(buf2, (0, columns - 2), 2, 0, frames, weight2)
-    ends = (0, merged - staged.shape[3])
-    for side, lane in enumerate(ends):
+    run(hides(totals, buf2, places, first - 2, 0, row_of(bias1), row_of(gain2), (left, valid, valid, right)))
+    totals = conv(buf2, (0, columns - 2), 2, 0, frames, weight2, accs[2:4])
+    copies = []
+    for side, lane in enumerate((0, merged - staged.shape[3])):
         lanes = pl.ds(lane, staged.shape[3])
-        mask = there(first, frames, valid)
-        both = jnp.concatenate([(total[2 * side + g] + row_of(bias2)) * mask for g in range(2)], axis=-1)
-        staged[side] = (both + own[:, :, lanes].astype(jnp.float32) * mask).astype(jnp.bfloat16)
-    copies = [pltpu.make_async_copy(staged.at[k], out.at[:, :, pl.ds(lane, staged.shape[3])], sem.at[k]) for k, lane in enumerate(ends)]
-    for copy in copies:
-        copy.start()
+        staged[side] = ended(totals[2 * side : 2 * side + 2], own, lanes, row_of(bias2), first, valid)
+        copies.append(pltpu.make_async_copy(staged.at[side], out.at[:, :, lanes], sem.at[side]))
+        copies[-1].start()
     for copy in copies:
         copy.wait()
 
@@ -455,6 +460,13 @@
 HB = pl.BlockSpec(memory_space=pl.ANY)
 
 
+def rooms(side, channels):
+    def room(width, frames):
+        return pltpu.VMEM((width, frames, side, channels), jnp.float32)
+
+    return room
+
+
 def row_path(video_in, neighbours, valid_frames, gain1, weight1, bias1, gain2, weight2, bias2):
     own = video_in[:, 0]
     frames, side, merged = own.shape
@@ -464,48 +476,44 @@
     prev = shifted(own, "tm", 1)
     rim = exchange(own, neighbours, channels)
     prev_rim = shifted(rim, "tm", 1)
+    room = rooms(side, channels)
     one = 2 * 27 * channels * channels * side
     space1 = pltpu.VMEM((columns + 4, 2 * frames, side, 3 * LANE), jnp.bfloat16)
     space2 = pltpu.VMEM((columns + 2, frames + 2, side, 3 * LANE), jnp.bfloat16)
     spaced = pltpu.VMEM((9, 3 * LANE, channels), jnp.bfloat16)
-    flat = pltpu.VMEM((9, channels, 3 * channels), jnp.bfloat16)
-    buf1, buf2, wide1, wide2 = call(
-        prepare_kernel,
-        (one, 4 * weight1.size),
-        [space1, space2, spaced, spaced],
-        [SM, SM, VM, VM, HB, HB],
-        (*tables, own, gain1, jnp.swapaxes(weight1, 1, 2), jnp.swapaxes(weight2, 1, 2)),
-        scratch_shapes=[flat, flat, pltpu.SemaphoreType.DMA((2,))],
-    )
-    (buf2,) = call(
+    buf1, buf2, flag = call(
+        tile_kernel,
+        (one * 2 * columns, own.size),
+        [space1, space2, jax.ShapeDtypeStruct((1,), jnp.int32)],
+        [SM, SM, VM, VM],
+        (*tables, own, gain1),
+        places=[VM, VM, SM],
+    )
+    wide1, wide2, buf2 = call(
         late_kernel,
-        (one * 2 * columns, own.size),
-        [space2],
-        [SM, SM, VM, VM, VM, VM, VM],
-        (*tables, buf1, wide1, bias1, gain2, buf2),
-        input_output_aliases={6: 0},
-    )
-    buf1, buf2 = call(
-        early_kernel,
         (one * 4 * columns, own.size),
-        [space1, space2],
-        [SM, SM, VM, VM, VM, VM, VM, VM, VM],
-        (*tables, prev, gain1, wide1, bias1, gain2, buf1, buf2),
-        input_output_aliases={7: 0, 8: 1},
-    )
-    (inner,) = call(
-        inner_kernel,
-        (one * 4 * columns, own.size),
-        [jax.ShapeDtypeStruct(own.shape, own.dtype)],
-        [SM, SM, VM, VM, VM, VM],
-        (*tables, own, buf2, wide2, bias2),
-    )
-    return own, rim, prev_rim, wide1, wide2, buf1, buf2, inner
+        [spaced, spaced, space2],
+        [SM, SM] + [VM] * 6,
+        (*tables, buf1, jnp.swapaxes(weight1, 1, 2), jnp.swapaxes(weight2, 1, 2), bias1, gain2, buf2),
+        input_output_aliases={7: 2},
+        scratch_shapes=[room(columns - 2, frames - 2)],
+    )
+    buf1, buf2, inner = call(
+        main_kernel,
+        (one * 8 * columns, own.size),
+        [space1, space2, jax.ShapeDtypeStruct(own.shape, own.dtype)],
+        [SM, SM] + [VM] * 10,
+        (*tables, own, prev, gain1, wide1, bias1, gain2, wide2, bias2, buf1, buf2),
+        input_output_aliases={10: 0, 11: 1},
+        scratch_shapes=[room(columns // 2, 4)] * 2 + [room(columns // 2, frames)] * 2,
+    )
+    return flag, (own, rim, prev_rim, wide1, wide2, buf1, buf2, inner)
 
 
 def row_end(state, tables, gain1, bias1, gain2, bias2):
     own, rim, prev_rim, wide1, wide2, buf1, buf2, inner = state
     space1, space2 = pltpu.VMEM(buf1.shape, buf1.dtype), pltpu.VMEM(buf2.shape, buf2.dtype)
+    room = rooms(own.shape[1], gain1.shape[0])
     _, _, out = call(
         rim_kernel,
         (own.size * 1000, own.size),
@@ -514,7 +522,7 @@
         (*tables, own, rim, prev_rim, gain1, wide1, bias1, gain2, wide2, bias2, buf1, buf2, inner),
         places=[VM, VM, HB],
         input_output_aliases={11: 0, 12: 1, 13: 2},
-        scratch_shapes=[pltpu.VMEM(rim.shape, rim.dtype), pltpu.SemaphoreType.DMA((2,))],
+        scratch_shapes=[room(2, own.shape[0] + 2)] * 4 + [pltpu.VMEM(rim.shape, rim.dtype), pltpu.SemaphoreType.DMA((2,))],
     )
     return out[:, None]
 
@@ -525,10 +533,9 @@
     tiles = neighbours.shape[0]
     if tiles_dev != 1 or tiles % 2 or frames_dev != 4:
         return general_path(*args)
-    state = row_path(*args)
-    beyond = jnp.concatenate([neighbours[:, :LEFT], neighbours[:, RIGHT + 1 :]], axis=1)
+    flag, state = row_path(*args)
     return lax.cond(
-        jnp.any(beyond < tiles),
+        flag[0] > 0,
         lambda state, args: general_path(*args),
         lambda state, args: row_end(state, args[1:3], gain1, bias1, gain2, bias2),
         state,

time: 46.3 us -> 39.7 us (0.86)
  Pallas kernels: 27.6 us -> 23.1 us
  starting transfers between devices: 13.5 us -> 12.4 us
  local copies, waits for them, and re-layouts: 1.73 us -> 0.88 us
  waiting for transfers between devices: 0.92 us -> 1.77 us
  other arithmetic: 0.75 us -> 0.02 us
    pallas_call x5 -> x4, Pallas kernels: 26.1 us -> 21.7 us  [call(): pl.pallas_call(kernel, out_shape=outs, in_specs=ins, out_specs=[VM] * len...]
    ppermute x3, waiting for transfers between devices: 0.01 us -> 1.76 us  [exchange(): lax.ppermute(value, 'space', [(i, (i + 2 * (s + 1)) % count) for i in ran...]
    ppermute x3, starting transfers between devices: 6.53 us -> 5.57 us  [exchange(): lax.ppermute(value, 'space', [(i, (i + 2 * (s + 1)) % count) for i in ran...]
    ppermute x1, waiting for transfers between devices: 0.91 us -> 0.01 us  [exchange(): pair = lax.ppermute(mine, 'space', [(i, i ^ 1) for i in range(count)])]
    slice x1 -> x0, local copies, waits for them, and re-layouts: 0.83 us -> none  [on_device(): neighbours[:, :LEFT]]
    reduce_or x1 -> x0, other arithmetic: 0.73 us -> none  [on_device(): jnp.any(beyond < tiles)]
  transfers between devices with their start and end apart: 6 -> 6, of which waited for: 1 -> 2; matrix products, arithmetic and copies ran while one was open for 5% -> 2% of each run, Pallas kernels for 47% -> 47%
where the time goes in v3:
time: 39.7 us; the launch traced here: 39.5 us
  Pallas kernels  23.1 us (58%)
  starting transfers between devices  12.4 us (31%)
  waiting for transfers between devices  1.77 us (4%)
  between operations  1.02 us (3%)
  local copies, waits for them, and re-layouts  0.88 us (2%)
    pallas_call x4, Pallas kernels, call(): pl.pallas_call(kernel, out_shape=outs, in_specs=ins, out_specs=[VM] * len...  21.7 us
    ppermute x3, starting transfers between devices, exchange(): lax.ppermute(value, 'space', [(i, (i + 2 * (s + 1)) % count) for i in ran...  5.57 us
    ppermute x2, starting transfers between devices, shifted(): lax.ppermute(value, axis, [(source, source + steps) for source in range(f...  4.41 us
    ppermute x1, starting transfers between devices, exchange(): pair = lax.ppermute(mine, 'space', [(i, i ^ 1) for i in range(count)])  2.4 us
    ppermute x3, waiting for transfers between devices, exchange(): lax.ppermute(value, 'space', [(i, (i + 2 * (s + 1)) % count) for i in ran...  1.76 us
    another operation x1, local copies, waits for them, and re-layouts, exchange(): mine = jnp.stack([own[:, :, :2 * channels], own[:, :, -2 * channels:]])  0.84 us
  transfers between devices with their start and end apart: 6, of which 2 were waited for; matrix products, arithmetic and copies ran while one was open for 2% of the time, Pallas kernels for 47%

profile of v3, /device:TPU:0, one launch (start us, length us, event | category | flops | bytes accessed | tf_op | source)
XLA Modules:
  0.0 39.5 jit_solution(9896637029110077109)
XLA Ops:
  0.0 2.4 %collective-permute-start.11 = (bf16[4,16,3072]{2,1,0:T(8,128)(2,1)}, bf16[4,16,3072]{2,1,0:T(8,128)(2,1)S(1)}, u32[]{:S(2)}, u32[]{:S(2)}) collective-permute-start(bf16[4,16,3072]{2,1,0:T(8,128)(2,1)} %bitcast.271), channel_id=1, source_target_pairs={{0,8},{8,16},{16,24},{1,9},{9,17},{17,25},{2,10},{10,18},{18,26},{... | collective-permute-start | bytes 1179656 | tf_op jit(solution)/shard_map/ppermute | solution.py:17
  2.4 0.8 %slice_bitcast_fusion.38 = (bf16[1,4,16,384]{3,2,1,0:T(8,128)(2,1)S(1)}, bf16[1,4,16,384]{3,2,1,0:T(8,128)(2,1)S(1)}) fusion(bf16[4,16,3072]{2,1,0:T(8,128)(2,1)} %bitcast.272), kind=kLoop, calls=%fused_computation.175 | loop fusion | bytes 196608 | tf_op jit(solution)/shard_map/stack | solution.py:421
  3.3 0.0 copy-start.16
  3.3 0.0 copy-start.17
  3.3 0.0 copy-start.18
  3.3 0.0 copy-start.21
  3.3 2.4 %collective-permute-start.6 = (bf16[2,4,16,384]{3,2,1,0:T(8,128)(2,1)S(1)}, bf16[2,4,16,384]{3,2,1,0:T(8,128)(2,1)S(1)}, u32[]{:S(2)}, u32[]{:S(2)}) collective-permute-start(bf16[2,4,16,384]{3,2,1,0:T(8,128)(2,1)S(1)} %pad_maximum_fusion.8.mine), channel_id=1, source_target_pairs={{0,1},{1,0},{2,3},{3,2},{4,5},{5,4},{6,7},{7,6},{8,9},{9,8},{10,11... | collective-permute-start | bytes 294920 | tf_op jit(solution)/shard_map/ppermute | solution.py:422
  5.7 3.7 %shard_map.93 = (bf16[20,8,16,768]{3,2,1,0:T(8,128)(2,1)S(1)}, bf16[18,6,16,768]{3,2,1,0:T(8,128)(2,1)S(1)}, s32[1]{0:T(128)}) custom-call(s32[8,8]{1,0:T(8,128)} %nb.9, s32[8]{0:T(128)} %vf.5, bf16[4,16,3072]{2,1,0:T(8,128)(2,1)} %bitcast.273, f32[192]{0:T(256)} %gain1.3), custom_call_target="tpu_custom_call" | custom-call | flops 1019215872 | bytes 196608 | tf_op jit(solution)/shard_map/pallas_call | solution.py:447
  10.1 0.0 collective-permute-done.6.pair
  10.1 0.0 copy-done.16
  10.1 0.7 %shard_map.94 = (bf16[2,4,16,384]{3,2,1,0:T(8,128)(2,1)S(1)}, bf16[2,4,16,384]{3,2,1,0:T(8,128)(2,1)S(1)}, bf16[2,4,16,384]{3,2,1,0:T(8,128)(2,1)S(1)}) custom-call(s32[8,8]{1,0:T(8,128)S(1)} %copy-done.16, bf16[2,4,16,384]{3,2,1,0:T(8,128)(2,1)S(1)} %pad_maximum_fusion.8.mine, bf16[2,4,16,384]{3,2,1,0:T(8,128)(2,1)S(1)} %collective-permute-done.6.pair), custom_call_target="tpu_custom_call" | custom-call | tf_op jit(solution)/shard_map/pallas_call | solution.py:425
  10.9 1.6 %collective-permute-start.7 = (bf16[2,4,16,384]{3,2,1,0:T(8,128)(2,1)S(1)}, bf16[2,4,16,384]{3,2,1,0:T(8,128)(2,1)S(1)}, u32[]{:S(2)}, u32[]{:S(2)}) collective-permute-start(bf16[2,4,16,384]{3,2,1,0:T(8,128)(2,1)S(1)} %get-tuple-element.141), channel_id=1, source_target_pairs={{0,2},{1,3},{2,4},{3,5},{4,6},{5,7},{6,0},{7,1},{8,10},{9,11},{10,... | collective-permute-start | bytes 294920 | tf_op jit(solution)/shard_map/ppermute | solution.py:433
  12.5 2.6 %collective-permute-start.8 = (bf16[2,4,16,384]{3,2,1,0:T(8,128)(2,1)S(1)}, bf16[2,4,16,384]{3,2,1,0:T(8,128)(2,1)S(1)}, u32[]{:S(2)}, u32[]{:S(2)}) collective-permute-start(bf16[2,4,16,384]{3,2,1,0:T(8,128)(2,1)S(1)} %get-tuple-element.142), channel_id=1, source_target_pairs={{0,4},{1,5},{2,6},{3,7},{4,0},{5,1},{6,2},{7,3},{8,12},{9,13},{10,... | collective-permute-start | bytes 294920 | tf_op jit(solution)/shard_map/ppermute | solution.py:433
  15.1 1.3 %collective-permute-start.9 = (bf16[2,4,16,384]{3,2,1,0:T(8,128)(2,1)S(1)}, bf16[2,4,16,384]{3,2,1,0:T(8,128)(2,1)S(1)}, u32[]{:S(2)}, u32[]{:S(2)}) collective-permute-start(bf16[2,4,16,384]{3,2,1,0:T(8,128)(2,1)S(1)} %get-tuple-element.143), channel_id=1, source_target_pairs={{0,6},{1,7},{2,0},{3,1},{4,2},{5,3},{6,4},{7,5},{8,14},{9,15},{10,... | collective-permute-start | bytes 294920 | tf_op jit(solution)/shard_map/ppermute | solution.py:433
  16.4 0.0 copy-done.17
  16.4 0.0 copy-done.18
  16.4 0.0 copy-done.21
  16.4 0.0 copy-start.15
  16.4 0.0 copy-start.19
  16.5 0.0 copy-start.20
  16.5 4.6 %shard_map.96 = (bf16[9,768,192]{2,1,0:T(8,128)(2,1)S(1)}, bf16[9,768,192]{2,1,0:T(8,128)(2,1)S(1)}, bf16[18,6,16,768]{3,2,1,0:T(8,128)(2,1)S(1)}) custom-call(s32[8,8]{1,0:T(8,128)S(1)} %copy-done.16, s32[8]{0:T(128)S(1)} %copy-done.21, bf16[20,8,16,768]{3,2,1,0:T(8,128)(2,1)S(1)} %get-tuple-element.144.buf1.old1, ...), custom_call_target="tpu_custom_call", output_to_operand_aliasing={{2}: (7, {})} | custom-call | flops 2038431744 | bytes 196608 | tf_op jit(solution)/shard_map/pallas_call | solution.py:447
  21.1 0.0 collective-permute-done.7.rest_0_
  21.1 1.6 %collective-permute-done.8.rest_1_ = bf16[2,4,16,384]{3,2,1,0:T(8,128)(2,1)S(1)} collective-permute-done((bf16[2,4,16,384]{3,2,1,0:T(8,128)(2,1)S(1)}, bf16[2,4,16,384]{3,2,1,0:T(8,128)(2,1)S(1)}, u32[]{:S(2)}, u32[]{:S(2)}) %collective-permute-start.8) | collective-permute-done | bytes 98336 | tf_op jit(solution)/shard_map/ppermute | solution.py:433
  22.7 0.2 collective-permute-done.9.rest_2_
  22.9 0.7 %shard_map.95 = bf16[2,4,16,384]{3,2,1,0:T(8,128)(2,1)S(1)} custom-call(s32[8,8]{1,0:T(8,128)S(1)} %copy-done.16, bf16[2,4,16,384]{3,2,1,0:T(8,128)(2,1)S(1)} %pad_maximum_fusion.8.mine, bf16[2,4,16,384]{3,2,1,0:T(8,128)(2,1)S(1)} %collective-permute-done.6.pair, bf16[2,4,16,384]{3,2,1,0:T(8,128)(2,1)S(1)} %collective-permute-done.7.rest_0_, ...), custom_call_target="tpu_custom_call" | custom-call | tf_op jit(solution)/shard_map/pallas_call | solution.py:436
  23.6 2.0 %collective-permute-start.10 = (bf16[2,4,16,384]{3,2,1,0:T(8,128)(2,1)S(1)}, bf16[2,4,16,384]{3,2,1,0:T(8,128)(2,1)S(1)}, u32[]{:S(2)}, u32[]{:S(2)}) collective-permute-start(bf16[2,4,16,384]{3,2,1,0:T(8,128)(2,1)S(1)} %shard_map.95), channel_id=1, source_target_pairs={{0,8},{8,16},{16,24},{1,9},{9,17},{17,25},{2,10},{10,18},{18,26},{... | collective-permute-start | bytes 294920 | tf_op jit(solution)/shard_map/ppermute | solution.py:17
  25.6 0.0 collective-permute-done.11.prev
  25.6 0.0 copy-done.15
  25.6 0.0 copy-done.19
  25.6 0.0 copy-done.20
  25.6 9.0 %shard_map.97 = (bf16[20,8,16,768]{3,2,1,0:T(8,128)(2,1)S(1)}, bf16[18,6,16,768]{3,2,1,0:T(8,128)(2,1)S(1)}, bf16[4,16,3072]{2,1,0:T(8,128)(2,1)}) custom-call(s32[8,8]{1,0:T(8,128)S(1)} %copy-done.16, s32[8]{0:T(128)S(1)} %copy-done.21, bf16[4,16,3072]{2,1,0:T(8,128)(2,1)S(1)} %bitcast.274, ...), custom_call_target="tpu_custom_call", output_to_operand_aliasing={{0}: (10, {}), {1}: (11, {})} | custom-call | flops 4076863488 | bytes 196608 | tf_op jit(solution)/shard_map/pallas_call | solution.py:447
  34.6 0.0 collective-permute-done.10
  34.6 4.7 %conditional.3 = ((bf16[4,1,16,3072]{3,2,0,1:T(8,128)(2,1)})) conditional(s32[]{:T(128)} %bitcast.94, (s32[8,8]{1,0:T(8,128)S(1)}, s32[8]{0:T(128)S(1)}, bf16[4,16,3072]{2,1,0:T(8,128)(2,1)S(1)}, bf16[2,4,16,384]{3,2,1,0:T(8,128)(2,1)S(1)}, bf16[2,4,16,384]{3,2,1,0:T(8,128)(2,1)S(1)}, /*index=5*/f32[192]{0:T(256)S(1)}, ...), branch_computations={%region_0.0_spmd, %region_1.8_spmd} | conditional | flops 4110178304 | bytes 214559840 | solution.py:537
  34.6 4.4 %branch_0_fun.1 = (bf16[20,8,16,768]{3,2,1,0:T(8,128)(2,1)S(1)}, bf16[18,6,16,768]{3,2,1,0:T(8,128)(2,1)S(1)}, bf16[4,16,3072]{2,1,0:T(8,128)(2,1)}) custom-call(s32[8,8]{1,0:T(8,128)S(1)} %get-tuple-element.91.nb, s32[8]{0:T(128)S(1)} %get-tuple-element.92.vf, ...), custom_call_target="tpu_custom_call", output_to_operand_aliasing={{0}: (11, {}), {1}: (12, {}), {2}: (13, {})} | custom-call | flops 196608000 | bytes 196608 | tf_op jit(solution)/shard_map/cond/branch_0_fun/pallas_call | solution.py:447
  (1 shorter events, 0.0 us)
Async XLA Ops:
  0.0 25.6 %collective-permute-start.11 = (bf16[4,16,3072]{2,1,0:T(8,128)(2,1)}, bf16[4,16,3072]{2,1,0:T(8,128)(2,1)S(1)}, u32[]{:S(2)}, u32[]{:S(2)}) collective-permute-start(bf16[4,16,3072]{2,1,0:T(8,128)(2,1)} %bitcast.271), channel_id=1, source_target_pairs={{0,8},{8,16},{16,24},{1,9},{9,17},{17,25},{2,10},{10,18},{18,26},{... | collective-permute-start | bytes 1179656 | tf_op jit(solution)/shard_map/ppermute | solution.py:17
  3.3 6.9 %copy-start.16 = (s32[8,8]{1,0:T(8,128)S(1)}, s32[8,8]{1,0:T(8,128)}, u32[]{:S(2)}) copy-start(s32[8,8]{1,0:T(8,128)} %nb.9) | copy-start | bytes 772
  3.3 13.1 %copy-start.17 = (f32[192]{0:T(256)S(1)}, f32[192]{0:T(256)}, u32[]{:S(2)}) copy-start(f32[192]{0:T(256)} %bias1.3) | copy-start | bytes 2308
  3.3 13.1 %copy-start.18 = (f32[192]{0:T(256)S(1)}, f32[192]{0:T(256)}, u32[]{:S(2)}) copy-start(f32[192]{0:T(256)} %gain2.3) | copy-start | bytes 2308
  3.3 13.1 %copy-start.21 = (s32[8]{0:T(128)S(1)}, s32[8]{0:T(128)}, u32[]{:S(2)}) copy-start(s32[8]{0:T(128)} %vf.5) | copy-start | bytes 100
  3.3 6.8 %collective-permute-start.6 = (bf16[2,4,16,384]{3,2,1,0:T(8,128)(2,1)S(1)}, bf16[2,4,16,384]{3,2,1,0:T(8,128)(2,1)S(1)}, u32[]{:S(2)}, u32[]{:S(2)}) collective-permute-start(bf16[2,4,16,384]{3,2,1,0:T(8,128)(2,1)S(1)} %pad_maximum_fusion.8.mine), channel_id=1, source_target_pairs={{0,1},{1,0},{2,3},{3,2},{4,5},{5,4},{6,7},{7,6},{8,9},{9,8},{10,11... | collective-permute-start | bytes 294920 | tf_op jit(solution)/shard_map/ppermute | solution.py:422
  10.9 10.2 %collective-permute-start.7 = (bf16[2,4,16,384]{3,2,1,0:T(8,128)(2,1)S(1)}, bf16[2,4,16,384]{3,2,1,0:T(8,128)(2,1)S(1)}, u32[]{:S(2)}, u32[]{:S(2)}) collective-permute-start(bf16[2,4,16,384]{3,2,1,0:T(8,128)(2,1)S(1)} %get-tuple-element.141), channel_id=1, source_target_pairs={{0,2},{1,3},{2,4},{3,5},{4,6},{5,7},{6,0},{7,1},{8,10},{9,11},{10,... | collective-permute-start | bytes 294920 | tf_op jit(solution)/shard_map/ppermute | solution.py:433
  12.5 10.2 %collective-permute-start.8 = (bf16[2,4,16,384]{3,2,1,0:T(8,128)(2,1)S(1)}, bf16[2,4,16,384]{3,2,1,0:T(8,128)(2,1)S(1)}, u32[]{:S(2)}, u32[]{:S(2)}) collective-permute-start(bf16[2,4,16,384]{3,2,1,0:T(8,128)(2,1)S(1)} %get-tuple-element.142), channel_id=1, source_target_pairs={{0,4},{1,5},{2,6},{3,7},{4,0},{5,1},{6,2},{7,3},{8,12},{9,13},{10,... | collective-permute-start | bytes 294920 | tf_op jit(solution)/shard_map/ppermute | solution.py:433
  15.1 7.8 %collective-permute-start.9 = (bf16[2,4,16,384]{3,2,1,0:T(8,128)(2,1)S(1)}, bf16[2,4,16,384]{3,2,1,0:T(8,128)(2,1)S(1)}, u32[]{:S(2)}, u32[]{:S(2)}) collective-permute-start(bf16[2,4,16,384]{3,2,1,0:T(8,128)(2,1)S(1)} %get-tuple-element.143), channel_id=1, source_target_pairs={{0,6},{1,7},{2,0},{3,1},{4,2},{5,3},{6,4},{7,5},{8,14},{9,15},{10,... | collective-permute-start | bytes 294920 | tf_op jit(solution)/shard_map/ppermute | solution.py:433
  16.4 9.1 %copy-start.15 = (bf16[4,1,16,3072]{3,2,1,0:T(8,128)(2,1)S(1)}, bf16[4,1,16,3072]{3,2,1,0:T(8,128)(2,1)}, u32[]{:S(2)}) copy-start(bf16[4,1,16,3072]{3,2,1,0:T(8,128)(2,1)} %param.15) | copy-start | bytes 1179652
  16.4 9.2 %copy-start.19 = (f32[192]{0:T(256)S(1)}, f32[192]{0:T(256)}, u32[]{:S(2)}) copy-start(f32[192]{0:T(256)} %bias2.1) | copy-start | bytes 2308
  16.5 9.1 %copy-start.20 = (f32[192]{0:T(256)S(1)}, f32[192]{0:T(256)}, u32[]{:S(2)}) copy-start(f32[192]{0:T(256)} %gain1.3) | copy-start | bytes 2308
  23.6 11.1 %collective-permute-start.10 = (bf16[2,4,16,384]{3,2,1,0:T(8,128)(2,1)S(1)}, bf16[2,4,16,384]{3,2,1,0:T(8,128)(2,1)S(1)}, u32[]{:S(2)}, u32[]{:S(2)}) collective-permute-start(bf16[2,4,16,384]{3,2,1,0:T(8,128)(2,1)S(1)} %shard_map.95), channel_id=1, source_target_pairs={{0,8},{8,16},{16,24},{1,9},{9,17},{17,25},{2,10},{10,18},{18,26},{... | collective-permute-start | bytes 294920 | tf_op jit(solution)/shard_map/ppermute | solution.py:17

commit v4 on v3

--- a/solution.py
+++ b/solution.py
@@ -1,4 +1,3 @@
-import functools
 from functools import partial
 
 import jax
@@ -29,15 +28,14 @@
     widened = jnp.concatenate(
         [framed[:, :, col_off : col_off + side_len] for col_off in range(3)], axis=-1
     )
-    summed = jnp.zeros((frames_out * side_len * side_len, channels), jnp.float32)
-    for time_off in range(3):
-        for row_off in range(3):
-            window = widened[
-                time_off : time_off + frames_out, row_off : row_off + side_len
-            ].reshape(-1, 3 * channels)
-            summed = summed + jnp.dot(
-                window, weight[time_off * 3 + row_off], preferred_element_type=jnp.float32
-            )
+
+    def tap(index, summed):
+        start = (index // 3, index % 3, 0, 0)
+        window = lax.dynamic_slice(widened, start, (frames_out, side_len, side_len, 3 * channels))
+        taps = lax.dynamic_index_in_dim(weight, index, 0, keepdims=False)
+        return summed + jnp.dot(window.reshape(-1, 3 * channels), taps, preferred_element_type=jnp.float32)
+
+    summed = lax.fori_loop(0, 9, tap, jnp.zeros((frames_out * side_len * side_len, channels), jnp.float32))
     return summed.reshape(frames_out, side_len, side_len, channels)
 
 
@@ -135,7 +133,7 @@
     conv2_weight,
     conv2_bias,
 ):
-    frames_dev, tiles_dev, side_len, merged = video_in.shape
+    frames_dev, tiles_dev, side_len, _ = video_in.shape
     channels = norm1_gain.shape[0]
     voxels = video_in.reshape(frames_dev, tiles_dev, side_len, side_len, channels)
     first_frame = lax.axis_index("tm") * frames_dev
@@ -172,13 +170,10 @@
 LANE = 256
 
 
-def silu(a):
-    return a * (0.5 + 0.5 * jnp.tanh(0.5 * a))
-
-
-def normed(v, gain):
+def normed(v, half_gain, mask):
     square = jnp.mean(v * v, axis=-1, keepdims=True)
-    return silu(v * lax.rsqrt(square + epsilon) * gain)
+    u = v * (lax.rsqrt(square + epsilon) * mask) * half_gain
+    return u + u * jnp.tanh(u)
 
 
 def put(buf, x, f0, h):
@@ -186,20 +181,10 @@
     row = lax.broadcasted_iota(jnp.int32, h.shape, 1)
     down = jnp.where(row == 0, 0.0, pltpu.roll(h, 1, 1))
     up = jnp.where(row == side - 1, 0.0, pltpu.roll(h, side - 1, 1))
+    zero = jnp.zeros((n, side, LANE - channels), jnp.bfloat16)
     for q, t in enumerate((down, h, up)):
         buf[x, f0 : f0 + n, :, q * LANE : q * LANE + channels] = t.astype(jnp.bfloat16)
-
-
-def zero_pads(buf, channels):
-    columns, frames, side, _ = buf.shape
-    zero = jnp.zeros((frames, side, LANE - channels), buf.dtype)
-
-    def body(x, _):
-        for q in range(3):
-            buf[x, :, :, q * LANE + channels : (q + 1) * LANE] = zero
-        return 0
-
-    lax.fori_loop(0, columns, body, 0)
+        buf[x, f0 : f0 + n, :, q * LANE + channels : (q + 1) * LANE] = zero
 
 
 def spread_one(flat, weight, p, q):
@@ -240,18 +225,18 @@
     return ((frame >= 0) & (frame < valid)).astype(jnp.float32)
 
 
-def act(buf, pair, f0, valid, x, at, gain):
+def act(buf, pair, mask, x, at, gain):
     channels = gain.shape[1]
-    values = pair.astype(jnp.float32) * there(f0, pair.shape[0], valid)
+    values = pair.astype(jnp.float32)
     for j in range(2):
-        put(buf, x + j, at, normed(values[:, :, j * channels : (j + 1) * channels], gain))
-
-
-def acts(buf, tile, f0, valid, at, gain):
+        put(buf, x + j, at, normed(values[:, :, j * channels : (j + 1) * channels], gain, mask))
+
+
+def acts(buf, tile, mask, at, gain):
     lanes = 2 * gain.shape[1]
 
     def one(k):
-        act(buf, tile[:, :, k * lanes : (k + 1) * lanes], f0, valid, 2 + 2 * k, at, gain)
+        act(buf, tile[:, :, k * lanes : (k + 1) * lanes], mask, 2 + 2 * k, at, gain)
 
     return [partial(one, k) for k in range(tile.shape[2] // lanes)]
 
@@ -260,27 +245,26 @@
     return ref[...].reshape(1, -1)
 
 
-def hides(totals, buf, places, f0, at, bias, gain, valids):
+def hides(totals, buf, places, at, bias, gain, masks):
     def one(g):
         total = totals[g][...]
-        put(buf, places[g], at, normed((total + bias) * there(f0, total.shape[0], valids[g]), gain))
+        put(buf, places[g], at, normed(total + bias, gain, masks[g]))
 
     return [partial(one, g) for g in range(len(places))]
 
 
-def ended(totals, own, lanes, bias, f0, valid):
+def ended(totals, own, lanes, bias, mask):
     parts = [total[...] + bias for total in totals]
-    mask = there(f0, parts[0].shape[0], valid)
     both = jnp.concatenate([part * mask for part in parts], axis=-1)
     return (both + own[:, :, lanes].astype(jnp.float32) * mask).astype(jnp.bfloat16)
 
 
-def finishes(totals, out, own, x0, bias, f0, valid):
+def finishes(totals, out, own, x0, at, bias, mask):
     channels = bias.shape[1]
 
     def one(g):
         lanes = pl.ds((x0 + g) * channels, 2 * channels)
-        out[:, :, lanes] = ended(totals[g : g + 2], own, lanes, bias, f0, valid)
+        out[:, :, pl.ds((at + g) * channels, 2 * channels)] = ended(totals[g : g + 2], own, lanes, bias, mask)
 
     return [partial(one, g) for g in range(0, len(totals), 2)]
 
@@ -290,50 +274,72 @@
         work()
 
 
-def tile_kernel(nb, vf, own, gain1, buf1, buf2, flag):
+def load_kernel(far, own, mine, sem):
+    lanes = mine.shape[3]
+    copies = [
+        pltpu.make_async_copy(far.at[:, :, pl.ds(0, lanes)], mine.at[0], sem.at[0]),
+        pltpu.make_async_copy(far.at[:, :, pl.ds(far.shape[2] - lanes, lanes)], mine.at[1], sem.at[1]),
+        pltpu.make_async_copy(far, own, sem.at[2]),
+    ]
+    for copy in copies:
+        copy.start()
+    for copy in copies:
+        copy.wait()
+
+
+def tile_kernel(nb, vf, own, gain1, far1, far2, buf1, mask, flat1, flat2, sem):
     frames = own.shape[0]
-    channels = gain1.shape[0]
-    tiles = nb.shape[0]
-    beyond = jnp.int32(0)
-    for tile in range(tiles):
-        for k in range(nb.shape[1]):
-            if k not in (LEFT, RIGHT):
-                beyond = jnp.maximum(beyond, tiles - nb[tile, k])
-    flag[0] = beyond
-    zero_pads(buf1, channels)
-    zero_pads(buf2, channels)
-    run(acts(buf1, own, lax.axis_index("tm") * frames, tracks(nb, vf)[0], frames, row_of(gain1)))
-
-
-def late_kernel(nb, vf, buf1, flat1, flat2, bias1, gain2, _, weight1, weight2, buf2, acc):
+    copies = [pltpu.make_async_copy(far1, flat1, sem.at[0]), pltpu.make_async_copy(far2, flat2, sem.at[1])]
+    for copy in copies:
+        copy.start()
+    first, valid = lax.axis_index("tm") * frames, tracks(nb, vf)[0]
+    frame = first - frames + lax.broadcasted_iota(jnp.int32, mask.shape, 0)
+    mask[...] = ((frame >= 0) & (frame < valid)).astype(jnp.float32)
+    run(acts(buf1, own, there(first, frames, valid), frames, 0.5 * row_of(gain1)))
+    for copy in copies:
+        copy.wait()
+
+
+def late_kernel(mask, buf1, flat1, flat2, bias1, gain2, nb, weight1, weight2, buf2, flag, acc):
+    k = lax.broadcasted_iota(jnp.int32, nb.shape, 1)
+    beyond = jnp.where((k < LEFT) | (k > RIGHT), nb.shape[0] - nb[...], 0)
+    flag[0] = jnp.max(beyond)
     frames = buf1.shape[1] // 2
     inner = buf2.shape[0] - 4
-    f0 = lax.axis_index("tm") * frames + 2
-    valid = tracks(nb, vf)[0]
     run(spreads(flat1, weight1))
-    totals = conv(buf1, (2,), inner, frames, frames - 2, weight1, (acc,), spreads(flat2, weight2))
-    run(hides(totals, buf2, range(2, 2 + inner), f0, 4, row_of(bias1), row_of(gain2), [valid] * inner))
-
-
-def main_kernel(nb, vf, own, prev, gain1, weight1, bias1, gain2, weight2, bias2, old1, old2, buf1, buf2, out, *accs):
+    works = spreads(flat2, weight2)
+    totals = conv(buf1, (2,), inner, frames, frames - 2, weight1, (acc,), works)
+    masks = [mask[frames + 2 :, :, :1]] * inner
+    run(hides(totals, buf2, range(2, 2 + inner), 4, row_of(bias1), 0.5 * row_of(gain2), masks))
+
+
+def split_of(columns):
+    half = (columns - 4) // 2
+    return half, half + 2, columns - 4 - half
+
+
+def early_kernel(mask, prev, gain1, weight1, old1, buf1, acc):
     frames = prev.shape[0]
+    _, wide, _ = split_of(prev.shape[2] // gain1.shape[0])
+    before = acts(buf1, prev, mask[:frames, :, :1], 0, 0.5 * row_of(gain1))
+    needed = (wide + 3) // 2
+    run(before[:needed])
+    conv(buf1, (2,), wide, frames - 4, 4, weight1, (acc,), before[needed:])
+
+
+def main_kernel(mask, own, buf1, acc, weight1, bias1, gain2, weight2, bias2, old2, buf2, out, *accs):
+    frames = own.shape[0]
     columns = buf2.shape[0] - 2
-    first = lax.axis_index("tm") * frames
-    valid = tracks(nb, vf)[0]
-    half = (columns - 4) // 2
-    wide, rest = half + 2, columns - 4 - half
-    before = acts(buf1, prev, first - frames, valid, 0, row_of(gain1))
-    needed = (wide + 3) // 2
-    norm = (first - 2, 0, row_of(bias1), row_of(gain2), [valid] * columns)
-    run(before[:needed])
-    totals = conv(buf1, (2,), wide, frames - 4, 4, weight1, accs[0:1], before[needed:])
-    works = hides(totals, buf2, range(2, 2 + wide), *norm)
-    totals = conv(buf1, (2 + wide,), rest, frames - 4, 4, weight1, accs[1:2], works)
+    half, wide, rest = split_of(columns)
+    norm = (0, row_of(bias1), 0.5 * row_of(gain2), [mask[frames - 2 : frames + 2, :, :1]] * columns)
+    present = mask[frames:, :, :1]
+    works = hides([acc.at[g] for g in range(wide)], buf2, range(2, 2 + wide), *norm)
+    totals = conv(buf1, (2 + wide,), rest, frames - 4, 4, weight1, accs[0:1], works)
     works = hides(totals, buf2, range(2 + wide, columns), *norm)
-    totals = conv(buf2, (2,), half, 0, frames, weight2, accs[2:3], works)
-    works = finishes(totals, out, own, 2, row_of(bias2), first, valid)
-    totals = conv(buf2, (2 + half,), rest, 0, frames, weight2, accs[3:4], works)
-    run(finishes(totals, out, own, 2 + half, row_of(bias2), first, valid))
+    totals = conv(buf2, (2,), half, 0, frames, weight2, accs[1:2], works)
+    works = finishes(totals, out, own, 2, 0, row_of(bias2), present)
+    totals = conv(buf2, (2 + half,), rest, 0, frames, weight2, accs[2:3], works)
+    run(finishes(totals, out, own, 2 + half, half, row_of(bias2), present))
 
 
 def rim_kernel(nb, vf, own, rim, prev_rim, gain1, weight1, bias1, gain2, weight2, bias2, old1, old2, inner, buf1, buf2, out, *scratch):
@@ -342,17 +348,20 @@
     columns = buf2.shape[0] - 2
     first = lax.axis_index("tm") * frames
     valid, left, right = tracks(nb, vf)
+    ends = staged.shape[3]
+    copies = [pltpu.make_async_copy(inner, out.at[:, :, pl.ds(ends, merged - 2 * ends)], sem.at[2])]
+    copies[0].start()
     for side, (x, v) in enumerate(((0, left), (columns + 2, right))):
-        act(buf1, prev_rim[side], first - frames, v, x, 0, row_of(gain1))
-        act(buf1, rim[side], first, v, x, frames, row_of(gain1))
+        act(buf1, prev_rim[side], there(first - frames, frames, v), x, 0, 0.5 * row_of(gain1))
+        act(buf1, rim[side], there(first, frames, v), x, frames, 0.5 * row_of(gain1))
     totals = conv(buf1, (0, columns), 2, frames - 4, frames + 2, weight1, accs[0:2])
     places = (0, 1, columns, columns + 1)
-    run(hides(totals, buf2, places, first - 2, 0, row_of(bias1), row_of(gain2), (left, valid, valid, right)))
+    masks = [there(first - 2, frames + 2, v) for v in (left, valid, valid, right)]
+    run(hides(totals, buf2, places, 0, row_of(bias1), 0.5 * row_of(gain2), masks))
     totals = conv(buf2, (0, columns - 2), 2, 0, frames, weight2, accs[2:4])
-    copies = []
-    for side, lane in enumerate((0, merged - staged.shape[3])):
-        lanes = pl.ds(lane, staged.shape[3])
-        staged[side] = ended(totals[2 * side : 2 * side + 2], own, lanes, row_of(bias2), first, valid)
+    for side, lane in enumerate((0, merged - ends)):
+        lanes = pl.ds(lane, ends)
+        staged[side] = ended(totals[2 * side : 2 * side + 2], own, lanes, row_of(bias2), there(first, frames, valid))
         copies.append(pltpu.make_async_copy(staged.at[side], out.at[:, :, lanes], sem.at[side]))
         copies[-1].start()
     for copy in copies:
@@ -414,11 +423,10 @@
                 out[side] = arrived[side]
 
 
-def exchange(own, neighbours, channels):
+def exchange(own, mine, neighbours):
     count = lax.axis_size("space")
     vmem = pl.BlockSpec(memory_space=pltpu.VMEM)
     smem = pl.BlockSpec(memory_space=pltpu.SMEM)
-    mine = jnp.stack([own[:, :, : 2 * channels], own[:, :, -2 * channels :]])
     pair = lax.ppermute(mine, "space", [(i, i ^ 1) for i in range(count)])
     piece = jax.ShapeDtypeStruct(mine.shape, mine.dtype)
     steps = count // 2 - 1
@@ -429,17 +437,18 @@
         out_specs=[vmem] * steps,
         compiler_params=pltpu.CompilerParams(vmem_limit_bytes=8 * 2**20),
     )(neighbours, mine, pair)
-    received = [
-        lax.ppermute(value, "space", [(i, (i + 2 * (s + 1)) % count) for i in range(count)])
-        for s, value in enumerate(sent)
-    ]
-    return pl.pallas_call(
+    received = []
+    for s, value in enumerate(sent):
+        received.append(lax.ppermute(value, "space", [(i, (i + 2 * (s + 1)) % count) for i in range(count)]))
+    prev = shifted(own, "tm", 1)
+    rim = pl.pallas_call(
         rims_kernel,
         out_shape=piece,
         in_specs=[smem] + [vmem] * (2 + steps),
         out_specs=vmem,
         compiler_params=pltpu.CompilerParams(vmem_limit_bytes=8 * 2**20),
     )(neighbours, mine, pair, *received)
+    return prev, rim
 
 
 def call(kernel, cost, outs, ins, args, places=None, **more):
@@ -468,44 +477,60 @@
 
 
 def row_path(video_in, neighbours, valid_frames, gain1, weight1, bias1, gain2, weight2, bias2):
-    own = video_in[:, 0]
-    frames, side, merged = own.shape
+    far = video_in[:, 0]
+    frames, side, merged = far.shape
     channels = gain1.shape[0]
     columns = merged // channels
     tables = (neighbours, valid_frames)
-    prev = shifted(own, "tm", 1)
-    rim = exchange(own, neighbours, channels)
-    prev_rim = shifted(rim, "tm", 1)
     room = rooms(side, channels)
     one = 2 * 27 * channels * channels * side
+    flat = pltpu.VMEM((9, channels, 3 * channels), jnp.bfloat16)
+    own, mine = call(
+        load_kernel,
+        (one, far.size),
+        [pltpu.VMEM(far.shape, far.dtype), pltpu.VMEM((2, frames, side, 2 * channels), far.dtype)],
+        [HB],
+        (far,),
+        scratch_shapes=[pltpu.SemaphoreType.DMA((3,))],
+    )
+    prev, rim = exchange(far, mine, neighbours)
+    prev_rim = shifted(rim, "tm", 1)
     space1 = pltpu.VMEM((columns + 4, 2 * frames, side, 3 * LANE), jnp.bfloat16)
     space2 = pltpu.VMEM((columns + 2, frames + 2, side, 3 * LANE), jnp.bfloat16)
     spaced = pltpu.VMEM((9, 3 * LANE, channels), jnp.bfloat16)
-    buf1, buf2, flag = call(
+    buf1, mask, flat1, flat2 = call(
         tile_kernel,
         (one * 2 * columns, own.size),
-        [space1, space2, jax.ShapeDtypeStruct((1,), jnp.int32)],
-        [SM, SM, VM, VM],
-        (*tables, own, gain1),
-        places=[VM, VM, SM],
-    )
-    wide1, wide2, buf2 = call(
+        [space1, pltpu.VMEM((2 * frames, side, 128), jnp.float32), flat, flat],
+        [SM, SM, VM, VM, HB, HB],
+        (*tables, own, gain1, jnp.swapaxes(weight1, 1, 2), jnp.swapaxes(weight2, 1, 2)),
+        scratch_shapes=[pltpu.SemaphoreType.DMA((2,))],
+    )
+    wide1, wide2, buf2, flag = call(
         late_kernel,
         (one * 4 * columns, own.size),
-        [spaced, spaced, space2],
-        [SM, SM] + [VM] * 6,
-        (*tables, buf1, jnp.swapaxes(weight1, 1, 2), jnp.swapaxes(weight2, 1, 2), bias1, gain2, buf2),
-        input_output_aliases={7: 2},
+        [spaced, spaced, space2, jax.ShapeDtypeStruct((1,), jnp.int32)],
+        [VM] * 7,
+        (mask, buf1, flat1, flat2, bias1, gain2, neighbours),
+        places=[VM] * 3 + [SM],
         scratch_shapes=[room(columns - 2, frames - 2)],
     )
-    buf1, buf2, inner = call(
+    buf1, acc = call(
+        early_kernel,
+        (one * 3 * columns, own.size),
+        [space1, room(split_of(columns)[1], 4)],
+        [VM] * 5,
+        (mask, prev, gain1, wide1, buf1),
+        input_output_aliases={4: 0},
+    )
+    buf2, inner = call(
         main_kernel,
         (one * 8 * columns, own.size),
-        [space1, space2, jax.ShapeDtypeStruct(own.shape, own.dtype)],
-        [SM, SM] + [VM] * 10,
-        (*tables, own, prev, gain1, wide1, bias1, gain2, wide2, bias2, buf1, buf2),
-        input_output_aliases={10: 0, 11: 1},
-        scratch_shapes=[room(columns // 2, 4)] * 2 + [room(columns // 2, frames)] * 2,
+        [space2, pltpu.VMEM((frames, side, (columns - 4) * channels), own.dtype)],
+        [VM] * 10,
+        (mask, own, buf1, acc, wide1, bias1, gain2, wide2, bias2, buf2),
+        input_output_aliases={9: 0},
+        scratch_shapes=[room(columns // 2, 4)] + [room(columns // 2, frames)] * 2,
     )
     return flag, (own, rim, prev_rim, wide1, wide2, buf1, buf2, inner)
 
@@ -518,17 +543,17 @@
         rim_kernel,
         (own.size * 1000, own.size),
         [space1, space2, jax.ShapeDtypeStruct(own.shape, own.dtype)],
-        [SM, SM] + [VM] * 11 + [HB],
+        [SM, SM] + [VM] * 12,
         (*tables, own, rim, prev_rim, gain1, wide1, bias1, gain2, wide2, bias2, buf1, buf2, inner),
         places=[VM, VM, HB],
-        input_output_aliases={11: 0, 12: 1, 13: 2},
-        scratch_shapes=[room(2, own.shape[0] + 2)] * 4 + [pltpu.VMEM(rim.shape, rim.dtype), pltpu.SemaphoreType.DMA((2,))],
+        input_output_aliases={11: 0, 12: 1},
+        scratch_shapes=[room(2, own.shape[0] + 2)] * 4 + [pltpu.VMEM(rim.shape, rim.dtype), pltpu.SemaphoreType.DMA((3,))],
     )
     return out[:, None]
 
 
 def on_device(*args):
-    video_in, neighbours, valid_frames, gain1, weight1, bias1, gain2, weight2, bias2 = args
+    video_in, neighbours, _, gain1, _, bias1, gain2, _, bias2 = args
     frames_dev, tiles_dev = video_in.shape[:2]
     tiles = neighbours.shape[0]
     if tiles_dev != 1 or tiles % 2 or frames_dev != 4:

time: 39.7 us -> 38 us (0.957)
  Pallas kernels: 23.1 us -> 21.1 us
  waiting for transfers between devices: 1.77 us -> 3.05 us
  local copies, waits for them, and re-layouts: 0.88 us -> 0.03 us
    pallas_call x4 -> x6, Pallas kernels: 21.7 us -> 19.7 us  [call(): pl.pallas_call(kernel, out_shape=outs, in_specs=ins, out_specs=[VM] * len...]
    ppermute x3, waiting for transfers between devices: 1.76 us -> 3.04 us  [exchange(): lax.ppermute(value, 'space', [(i, (i + 2 * (s + 1)) % count) for i in ran...]
    another operation x1 -> x0, local copies, waits for them, and re-layouts: 0.84 us -> none  [exchange(): mine = jnp.stack([own[:, :, :2 * channels], own[:, :, -2 * channels:]])]
  transfers between devices with their start and end apart: 6 -> 6, of which waited for: 2 -> 2; matrix products, arithmetic and copies ran while one was open for 2% -> 0% of each run, Pallas kernels for 47% -> 44%
where the time goes in v4:
time: 38 us; the launch traced here: 37.7 us
  Pallas kernels  21.1 us (56%)
  starting transfers between devices  12.4 us (33%)
  waiting for transfers between devices  3.05 us (8%)
  between operations  0.98 us (3%)
    pallas_call x6, Pallas kernels, call(): pl.pallas_call(kernel, out_shape=outs, in_specs=ins, out_specs=[VM] * len...  19.7 us
    ppermute x3, starting transfers between devices, exchange(): lax.ppermute(value, 'space', [(i, (i + 2 * (s + 1)) % count) for i in ran...  5.71 us
    ppermute x2, starting transfers between devices, shifted(): lax.ppermute(value, axis, [(source, source + steps) for source in range(f...  4.29 us
    ppermute x3, waiting for transfers between devices, exchange(): lax.ppermute(value, 'space', [(i, (i + 2 * (s + 1)) % count) for i in ran...  3.04 us
    ppermute x1, starting transfers between devices, exchange(): pair = lax.ppermute(mine, 'space', [(i, i ^ 1) for i in range(count)])  2.4 us
  transfers between devices with their start and end apart: 6, of which 2 were waited for; matrix products, arithmetic and copies ran while one was open for 0% of the time, Pallas kernels for 44%

profile of v4, /device:TPU:0, one launch (start us, length us, event | category | flops | bytes accessed | tf_op | source)
XLA Modules:
  0.0 37.7 jit_solution(5653427107189781254)
XLA Ops:
  0.0 2.4 %collective-permute-start.11 = (bf16[4,16,3072]{2,1,0:T(8,128)(2,1)}, bf16[4,16,3072]{2,1,0:T(8,128)(2,1)S(1)}, u32[]{:S(2)}, u32[]{:S(2)}) collective-permute-start(bf16[4,16,3072]{2,1,0:T(8,128)(2,1)} %bitcast.183), channel_id=1, source_target_pairs={{0,8},{8,16},{16,24},{1,9},{9,17},{17,25},{2,10},{10,18},{18,26},{... | collective-permute-start | bytes 1179656 | tf_op jit(solution)/shard_map/ppermute | solution.py:16
  2.4 1.1 %shard_map.93 = (bf16[4,16,3072]{2,1,0:T(8,128)(2,1)S(1)}, bf16[2,4,16,384]{3,2,1,0:T(8,128)(2,1)S(1)}) custom-call(bf16[4,16,3072]{2,1,0:T(8,128)(2,1)} %bitcast.184), custom_call_target="tpu_custom_call" | custom-call | flops 31850496 | bytes 196608 | tf_op jit(solution)/shard_map/pallas_call | solution.py:456
  3.5 2.4 %collective-permute-start.6 = (bf16[2,4,16,384]{3,2,1,0:T(8,128)(2,1)S(1)}, bf16[2,4,16,384]{3,2,1,0:T(8,128)(2,1)S(1)}, u32[]{:S(2)}, u32[]{:S(2)}) collective-permute-start(bf16[2,4,16,384]{3,2,1,0:T(8,128)(2,1)S(1)} %get-tuple-element.377.mine), channel_id=1, source_target_pairs={{0,1},{1,0},{2,3},{3,2},{4,5},{5,4},{6,7},{7,6},{8,9},{9,8},{10,11... | collective-permute-start | bytes 294920 | tf_op jit(solution)/shard_map/ppermute | solution.py:430
  5.9 0.0 copy-start.2
  5.9 0.0 copy-start.4
  5.9 0.0 copy-start.5
  5.9 3.2 %shard_map.94 = (bf16[20,8,16,768]{3,2,1,0:T(8,128)(2,1)S(1)}, f32[8,16,128]{2,1,0:T(8,128)S(1)}, bf16[9,192,576]{2,1,0:T(8,128)(2,1)S(1)}, bf16[9,192,576]{2,1,0:T(8,128)(2,1)S(1)}) custom-call(s32[8,8]{1,0:T(8,128)} %nb.7, s32[8]{0:T(128)} %vf.1, bf16[4,16,3072]{2,1,0:T(8,128)(2,1)S(1)} %get-tuple-element.371.own, f32[192]{0:T(256)} %gain1.3, ...), custom_call_target="tpu_custom_call" | custom-call | flops 1019215872 | bytes 196608 | tf_op jit(solution)/shard_map/pallas_call | solution.py:456
  9.1 0.0 collective-permute-done.6.pair
  9.1 0.0 copy-done.2
  9.2 0.7 %shard_map.96 = (bf16[2,4,16,384]{3,2,1,0:T(8,128)(2,1)S(1)}, bf16[2,4,16,384]{3,2,1,0:T(8,128)(2,1)S(1)}, bf16[2,4,16,384]{3,2,1,0:T(8,128)(2,1)S(1)}) custom-call(s32[8,8]{1,0:T(8,128)S(1)} %copy-done.2, bf16[2,4,16,384]{3,2,1,0:T(8,128)(2,1)S(1)} %get-tuple-element.377.mine, bf16[2,4,16,384]{3,2,1,0:T(8,128)(2,1)S(1)} %collective-permute-done.6.pair), custom_call_target="tpu_custom_call" | custom-call | tf_op jit(solution)/shard_map/pallas_call | solution.py:433
  9.9 1.8 %collective-permute-start.7 = (bf16[2,4,16,384]{3,2,1,0:T(8,128)(2,1)S(1)}, bf16[2,4,16,384]{3,2,1,0:T(8,128)(2,1)S(1)}, u32[]{:S(2)}, u32[]{:S(2)}) collective-permute-start(bf16[2,4,16,384]{3,2,1,0:T(8,128)(2,1)S(1)} %get-tuple-element.378), channel_id=1, source_target_pairs={{0,2},{1,3},{2,4},{3,5},{4,6},{5,7},{6,0},{7,1},{8,10},{9,11},{10,... | collective-permute-start | bytes 294920 | tf_op jit(solution)/shard_map/ppermute | solution.py:442
  11.6 2.6 %collective-permute-start.8 = (bf16[2,4,16,384]{3,2,1,0:T(8,128)(2,1)S(1)}, bf16[2,4,16,384]{3,2,1,0:T(8,128)(2,1)S(1)}, u32[]{:S(2)}, u32[]{:S(2)}) collective-permute-start(bf16[2,4,16,384]{3,2,1,0:T(8,128)(2,1)S(1)} %get-tuple-element.379), channel_id=1, source_target_pairs={{0,4},{1,5},{2,6},{3,7},{4,0},{5,1},{6,2},{7,3},{8,12},{9,13},{10,... | collective-permute-start | bytes 294920 | tf_op jit(solution)/shard_map/ppermute | solution.py:442
  14.2 1.3 %collective-permute-start.9 = (bf16[2,4,16,384]{3,2,1,0:T(8,128)(2,1)S(1)}, bf16[2,4,16,384]{3,2,1,0:T(8,128)(2,1)S(1)}, u32[]{:S(2)}, u32[]{:S(2)}) collective-permute-start(bf16[2,4,16,384]{3,2,1,0:T(8,128)(2,1)S(1)} %get-tuple-element.380), channel_id=1, source_target_pairs={{0,6},{1,7},{2,0},{3,1},{4,2},{5,3},{6,4},{7,5},{8,14},{9,15},{10,... | collective-permute-start | bytes 294920 | tf_op jit(solution)/shard_map/ppermute | solution.py:442
  15.6 0.0 copy-done.4
  15.6 0.0 copy-done.5
  15.6 0.0 copy-start.3
  15.6 2.5 %shard_map.95 = (bf16[9,768,192]{2,1,0:T(8,128)(2,1)S(1)}, bf16[9,768,192]{2,1,0:T(8,128)(2,1)S(1)}, bf16[18,6,16,768]{3,2,1,0:T(8,128)(2,1)S(1)}, s32[1]{0:T(128)}) custom-call(f32[8,16,128]{2,1,0:T(8,128)S(1)} %get-tuple-element.372.mask, bf16[20,8,16,768]{3,2,1,0:T(8,128)(2,1)S(1)} %get-tuple-element.373.buf1.old1, ...), custom_call_target="tpu_custom_call" | custom-call | flops 2038431744 | bytes 196608 | tf_op jit(solution)/shard_map/pallas_call | solution.py:456
  18.7 0.0 collective-permute-done.7.rest_0_
  18.8 2.9 %collective-permute-done.8.rest_1_ = bf16[2,4,16,384]{3,2,1,0:T(8,128)(2,1)S(1)} collective-permute-done((bf16[2,4,16,384]{3,2,1,0:T(8,128)(2,1)S(1)}, bf16[2,4,16,384]{3,2,1,0:T(8,128)(2,1)S(1)}, u32[]{:S(2)}, u32[]{:S(2)}) %collective-permute-start.8) | collective-permute-done | bytes 98336 | tf_op jit(solution)/shard_map/ppermute | solution.py:442
  21.7 0.1 collective-permute-done.9.rest_2_
  21.8 0.7 %shard_map.97 = bf16[2,4,16,384]{3,2,1,0:T(8,128)(2,1)S(1)} custom-call(s32[8,8]{1,0:T(8,128)S(1)} %copy-done.2, bf16[2,4,16,384]{3,2,1,0:T(8,128)(2,1)S(1)} %get-tuple-element.377.mine, bf16[2,4,16,384]{3,2,1,0:T(8,128)(2,1)S(1)} %collective-permute-done.6.pair, bf16[2,4,16,384]{3,2,1,0:T(8,128)(2,1)S(1)} %collective-permute-done.7.rest_0_, ...), custom_call_target="tpu_custom_call" | custom-call | tf_op jit(solution)/shard_map/pallas_call | solution.py:444
  22.5 1.9 %collective-permute-start.10 = (bf16[2,4,16,384]{3,2,1,0:T(8,128)(2,1)S(1)}, bf16[2,4,16,384]{3,2,1,0:T(8,128)(2,1)S(1)}, u32[]{:S(2)}, u32[]{:S(2)}) collective-permute-start(bf16[2,4,16,384]{3,2,1,0:T(8,128)(2,1)S(1)} %shard_map.97), channel_id=1, source_target_pairs={{0,8},{8,16},{16,24},{1,9},{9,17},{17,25},{2,10},{10,18},{18,26},{... | collective-permute-start | bytes 294920 | tf_op jit(solution)/shard_map/ppermute | solution.py:16
  24.4 0.0 collective-permute-done.11.prev
  24.4 0.0 copy-done.3
  24.4 0.0 copy-start.6
  24.4 3.5 %shard_map.98 = (bf16[20,8,16,768]{3,2,1,0:T(8,128)(2,1)S(1)}, f32[8,4,16,192]{3,2,1,0:T(8,128)S(1)}) custom-call(f32[8,16,128]{2,1,0:T(8,128)S(1)} %get-tuple-element.372.mask, bf16[4,16,3072]{2,1,0:T(8,128)(2,1)S(1)} %collective-permute-done.11.prev, f32[192]{0:T(256)S(1)} %copy-done.3, ...), custom_call_target="tpu_custom_call", output_to_operand_aliasing={{0}: (4, {})} | custom-call | flops 1528823808 | bytes 196608 | tf_op jit(solution)/shard_map/pallas_call | solution.py:456
  27.9 0.0 copy-done.6
  28.0 0.0 copy-start
  28.0 0.0 copy-start.7
  28.0 5.0 %shard_map.99 = (bf16[18,6,16,768]{3,2,1,0:T(8,128)(2,1)S(1)}, bf16[4,16,2304]{2,1,0:T(8,128)(2,1)S(1)}) custom-call(f32[8,16,128]{2,1,0:T(8,128)S(1)} %get-tuple-element.372.mask, bf16[4,16,3072]{2,1,0:T(8,128)(2,1)S(1)} %get-tuple-element.371.own, bf16[20,8,16,768]{3,2,1,0:T(8,128)(2,1)S(1)} %get-tuple-element.383.buf1, ...), custom_call_target="tpu_custom_call", output_to_operand_aliasing={{0}: (9, {})} | custom-call | flops 4076863488 | bytes 196608 | tf_op jit(solution)/shard_map/pallas_call | solution.py:456
  32.9 0.0 collective-permute-done.10
  33.0 0.0 copy-done
  33.0 0.0 copy-done.7
  33.0 4.6 %conditional.3 = ((bf16[4,1,16,3072]{3,2,0,1:T(8,128)(2,1)})) conditional(s32[]{:T(128)} %bitcast.58, (s32[8,8]{1,0:T(8,128)S(1)}, s32[8]{0:T(128)S(1)}, bf16[4,16,3072]{2,1,0:T(8,128)(2,1)S(1)}, bf16[2,4,16,384]{3,2,1,0:T(8,128)(2,1)S(1)}, bf16[2,4,16,384]{3,2,1,0:T(8,128)(2,1)S(1)}, /*index=5*/f32[192]{0:T(256)S(1)}, ...), branch_computations={%region_0.0_spmd, %region_1.12_spmd} | conditional | flops 483940256 | bytes 51179728 | solution.py:562
  33.2 4.4 %branch_0_fun.1 = (bf16[20,8,16,768]{3,2,1,0:T(8,128)(2,1)S(1)}, bf16[18,6,16,768]{3,2,1,0:T(8,128)(2,1)S(1)}, bf16[4,16,3072]{2,1,0:T(8,128)(2,1)}) custom-call(s32[8,8]{1,0:T(8,128)S(1)} %get-tuple-element.305.nb, s32[8]{0:T(128)S(1)} %get-tuple-element.306.vf, ...), custom_call_target="tpu_custom_call", output_to_operand_aliasing={{0}: (11, {}), {1}: (12, {})} | custom-call | flops 196608000 | bytes 196608 | tf_op jit(solution)/shard_map/cond/branch_0_fun/pallas_call | solution.py:456
Async XLA Ops:
  0.0 24.4 %collective-permute-start.11 = (bf16[4,16,3072]{2,1,0:T(8,128)(2,1)}, bf16[4,16,3072]{2,1,0:T(8,128)(2,1)S(1)}, u32[]{:S(2)}, u32[]{:S(2)}) collective-permute-start(bf16[4,16,3072]{2,1,0:T(8,128)(2,1)} %bitcast.183), channel_id=1, source_target_pairs={{0,8},{8,16},{16,24},{1,9},{9,17},{17,25},{2,10},{10,18},{18,26},{... | collective-permute-start | bytes 1179656 | tf_op jit(solution)/shard_map/ppermute | solution.py:16
  3.5 5.6 %collective-permute-start.6 = (bf16[2,4,16,384]{3,2,1,0:T(8,128)(2,1)S(1)}, bf16[2,4,16,384]{3,2,1,0:T(8,128)(2,1)S(1)}, u32[]{:S(2)}, u32[]{:S(2)}) collective-permute-start(bf16[2,4,16,384]{3,2,1,0:T(8,128)(2,1)S(1)} %get-tuple-element.377.mine), channel_id=1, source_target_pairs={{0,1},{1,0},{2,3},{3,2},{4,5},{5,4},{6,7},{7,6},{8,9},{9,8},{10,11... | collective-permute-start | bytes 294920 | tf_op jit(solution)/shard_map/ppermute | solution.py:430
  5.9 3.2 %copy-start.2 = (s32[8,8]{1,0:T(8,128)S(1)}, s32[8,8]{1,0:T(8,128)}, u32[]{:S(2)}) copy-start(s32[8,8]{1,0:T(8,128)} %nb.7) | copy-start | bytes 772
  5.9 9.6 %copy-start.4 = (f32[192]{0:T(256)S(1)}, f32[192]{0:T(256)}, u32[]{:S(2)}) copy-start(f32[192]{0:T(256)} %bias1.3) | copy-start | bytes 2308
  5.9 9.6 %copy-start.5 = (f32[192]{0:T(256)S(1)}, f32[192]{0:T(256)}, u32[]{:S(2)}) copy-start(f32[192]{0:T(256)} %gain2.3) | copy-start | bytes 2308
  9.9 8.9 %collective-permute-start.7 = (bf16[2,4,16,384]{3,2,1,0:T(8,128)(2,1)S(1)}, bf16[2,4,16,384]{3,2,1,0:T(8,128)(2,1)S(1)}, u32[]{:S(2)}, u32[]{:S(2)}) collective-permute-start(bf16[2,4,16,384]{3,2,1,0:T(8,128)(2,1)S(1)} %get-tuple-element.378), channel_id=1, source_target_pairs={{0,2},{1,3},{2,4},{3,5},{4,6},{5,7},{6,0},{7,1},{8,10},{9,11},{10,... | collective-permute-start | bytes 294920 | tf_op jit(solution)/shard_map/ppermute | solution.py:442
  11.6 10.1 %collective-permute-start.8 = (bf16[2,4,16,384]{3,2,1,0:T(8,128)(2,1)S(1)}, bf16[2,4,16,384]{3,2,1,0:T(8,128)(2,1)S(1)}, u32[]{:S(2)}, u32[]{:S(2)}) collective-permute-start(bf16[2,4,16,384]{3,2,1,0:T(8,128)(2,1)S(1)} %get-tuple-element.379), channel_id=1, source_target_pairs={{0,4},{1,5},{2,6},{3,7},{4,0},{5,1},{6,2},{7,3},{8,12},{9,13},{10,... | collective-permute-start | bytes 294920 | tf_op jit(solution)/shard_map/ppermute | solution.py:442
  14.2 7.6 %collective-permute-start.9 = (bf16[2,4,16,384]{3,2,1,0:T(8,128)(2,1)S(1)}, bf16[2,4,16,384]{3,2,1,0:T(8,128)(2,1)S(1)}, u32[]{:S(2)}, u32[]{:S(2)}) collective-permute-start(bf16[2,4,16,384]{3,2,1,0:T(8,128)(2,1)S(1)} %get-tuple-element.380), channel_id=1, source_target_pairs={{0,6},{1,7},{2,0},{3,1},{4,2},{5,3},{6,4},{7,5},{8,14},{9,15},{10,... | collective-permute-start | bytes 294920 | tf_op jit(solution)/shard_map/ppermute | solution.py:442
  15.6 8.8 %copy-start.3 = (f32[192]{0:T(256)S(1)}, f32[192]{0:T(256)}, u32[]{:S(2)}) copy-start(f32[192]{0:T(256)} %gain1.3) | copy-start | bytes 2308
  22.5 10.5 %collective-permute-start.10 = (bf16[2,4,16,384]{3,2,1,0:T(8,128)(2,1)S(1)}, bf16[2,4,16,384]{3,2,1,0:T(8,128)(2,1)S(1)}, u32[]{:S(2)}, u32[]{:S(2)}) collective-permute-start(bf16[2,4,16,384]{3,2,1,0:T(8,128)(2,1)S(1)} %shard_map.97), channel_id=1, source_target_pairs={{0,8},{8,16},{16,24},{1,9},{9,17},{17,25},{2,10},{10,18},{18,26},{... | collective-permute-start | bytes 294920 | tf_op jit(solution)/shard_map/ppermute | solution.py:16
  24.4 3.6 %copy-start.6 = (f32[192]{0:T(256)S(1)}, f32[192]{0:T(256)}, u32[]{:S(2)}) copy-start(f32[192]{0:T(256)} %bias2.1) | copy-start | bytes 2308
  28.0 5.0 %copy-start = (bf16[4,1,16,3072]{3,2,1,0:T(8,128)(2,1)S(1)}, bf16[4,1,16,3072]{3,2,1,0:T(8,128)(2,1)}, u32[]{:S(2)}) copy-start(bf16[4,1,16,3072]{3,2,1,0:T(8,128)(2,1)} %param.19) | copy-start | bytes 1179652
  28.0 5.0 %copy-start.7 = (s32[8]{0:T(128)S(1)}, s32[8]{0:T(128)}, u32[]{:S(2)}) copy-start(s32[8]{0:T(128)} %vf.1) | copy-start | bytes 100

commit v5 on v4

--- a/solution.py
+++ b/solution.py
@@ -287,11 +287,14 @@
         copy.wait()
 
 
-def tile_kernel(nb, vf, own, gain1, far1, far2, buf1, mask, flat1, flat2, sem):
+def tile_kernel(nb, vf, own, gain1, far1, far2, buf1, mask, flat1, flat2, beside, sem):
     frames = own.shape[0]
     copies = [pltpu.make_async_copy(far1, flat1, sem.at[0]), pltpu.make_async_copy(far2, flat2, sem.at[1])]
     for copy in copies:
         copy.start()
+    for tile in range(nb.shape[0]):
+        beside[2 * tile] = nb[tile, LEFT]
+        beside[2 * tile + 1] = nb[tile, RIGHT]
     first, valid = lax.axis_index("tm") * frames, tracks(nb, vf)[0]
     frame = first - frames + lax.broadcasted_iota(jnp.int32, mask.shape, 0)
     mask[...] = ((frame >= 0) & (frame < valid)).astype(jnp.float32)
@@ -381,13 +384,13 @@
     return vf[me], of(nb[me, LEFT]), of(nb[me, RIGHT])
 
 
-def pick_kernel(nb, mine, pair, *outs):
-    tiles = nb.shape[0]
+def pick_kernel(beside, mine, pair, *outs):
+    tiles = beside.shape[0] // 2
     me = lax.axis_index("space")
     for step, out in enumerate(outs):
         there = lax.rem(me + 2 * (step + 1), tiles)
-        for side, column in ((0, LEFT), (1, RIGHT)):
-            source = nb[there, column]
+        for side in range(2):
+            source = beside[2 * there + side]
 
             @pl.when(source == me)
             def _():
@@ -398,13 +401,13 @@
                 out[side] = pair[1 - side]
 
 
-def rims_kernel(nb, mine, pair, *rest):
+def rims_kernel(beside, mine, pair, *rest):
     received, out = rest[:-1], rest[-1]
-    tiles = nb.shape[0]
+    tiles = beside.shape[0] // 2
     half = tiles // 2
     me = lax.axis_index("space")
-    for side, column in ((0, LEFT), (1, RIGHT)):
-        source = nb[me, column]
+    for side in range(2):
+        source = beside[2 * me + side]
         step = lax.rem(me // 2 - source // 2 + tiles, half)
         at_home = (step == 0) | (source >= tiles)
 
@@ -423,7 +426,7 @@
                 out[side] = arrived[side]
 
 
-def exchange(own, mine, neighbours):
+def exchange(own, mine, beside):
     count = lax.axis_size("space")
     vmem = pl.BlockSpec(memory_space=pltpu.VMEM)
     smem = pl.BlockSpec(memory_space=pltpu.SMEM)
@@ -436,7 +439,7 @@
         in_specs=[smem, vmem, vmem],
         out_specs=[vmem] * steps,
         compiler_params=pltpu.CompilerParams(vmem_limit_bytes=8 * 2**20),
-    )(neighbours, mine, pair)
+    )(beside, mine, pair)
     received = []
     for s, value in enumerate(sent):
         received.append(lax.ppermute(value, "space", [(i, (i + 2 * (s + 1)) % count) for i in range(count)]))
@@ -447,7 +450,7 @@
         in_specs=[smem] + [vmem] * (2 + steps),
         out_specs=vmem,
         compiler_params=pltpu.CompilerParams(vmem_limit_bytes=8 * 2**20),
-    )(neighbours, mine, pair, *received)
+    )(beside, mine, pair, *received)
     return prev, rim
 
 
@@ -493,23 +496,24 @@
         (far,),
         scratch_shapes=[pltpu.SemaphoreType.DMA((3,))],
     )
-    prev, rim = exchange(far, mine, neighbours)
-    prev_rim = shifted(rim, "tm", 1)
     space1 = pltpu.VMEM((columns + 4, 2 * frames, side, 3 * LANE), jnp.bfloat16)
     space2 = pltpu.VMEM((columns + 2, frames + 2, side, 3 * LANE), jnp.bfloat16)
     spaced = pltpu.VMEM((9, 3 * LANE, channels), jnp.bfloat16)
-    buf1, mask, flat1, flat2 = call(
+    buf1, mask, flat1, flat2, beside = call(
         tile_kernel,
         (one * 2 * columns, own.size),
-        [space1, pltpu.VMEM((2 * frames, side, 128), jnp.float32), flat, flat],
+        [space1, pltpu.VMEM((2 * frames, side, 128), jnp.float32), flat, flat, pltpu.SMEM((2 * neighbours.shape[0],), jnp.int32)],
         [SM, SM, VM, VM, HB, HB],
         (*tables, own, gain1, jnp.swapaxes(weight1, 1, 2), jnp.swapaxes(weight2, 1, 2)),
+        places=[VM] * 4 + [SM],
         scratch_shapes=[pltpu.SemaphoreType.DMA((2,))],
     )
+    prev, rim = exchange(far, mine, beside)
+    prev_rim = shifted(rim, "tm", 1)
     wide1, wide2, buf2, flag = call(
         late_kernel,
         (one * 4 * columns, own.size),
-        [spaced, spaced, space2, jax.ShapeDtypeStruct((1,), jnp.int32)],
+        [spaced, spaced, space2, pltpu.SMEM((1,), jnp.int32)],
         [VM] * 7,
         (mask, buf1, flat1, flat2, bias1, gain2, neighbours),
         places=[VM] * 3 + [SM],

time: 38 us -> 36.7 us (0.966)
  Pallas kernels: 21.1 us -> 19.6 us
  waiting for transfers between devices: 3.05 us -> 3.9 us
  between operations: 0.98 us -> 0.33 us
    ppermute x3, waiting for transfers between devices: 3.04 us -> 3.89 us  [exchange(): lax.ppermute(value, 'space', [(i, (i + 2 * (s + 1)) % count) for i in ran...]
    pallas_call x1, Pallas kernels: 0.69 us -> 0.01 us  [exchange(): pl.pallas_call(rims_kernel, out_shape=piece, in_specs=[smem] + [vmem] * (...]
    pallas_call x1, Pallas kernels: 0.7 us -> 0.1 us  [exchange(): pl.pallas_call(pick_kernel, out_shape=[piece] * steps, in_specs=[smem, vm...]
  transfers between devices with their start and end apart: 6 -> 6, of which waited for: 2 -> 2; matrix products, arithmetic and copies ran while one was open for 0% -> 0% of each run, Pallas kernels for 44% -> 42%
where the time goes in v5:
time: 36.7 us; the launch traced here: 36.5 us
  Pallas kernels  19.6 us (53%)
  starting transfers between devices  12.4 us (34%)
  waiting for transfers between devices  3.9 us (11%)
    pallas_call x6, Pallas kernels, call(): pl.pallas_call(kernel, out_shape=outs, in_specs=ins, out_specs=[VM] * len...  19.5 us
    ppermute x3, starting transfers between devices, exchange(): lax.ppermute(value, 'space', [(i, (i + 2 * (s + 1)) % count) for i in ran...  5.69 us
    ppermute x2, starting transfers between devices, shifted(): lax.ppermute(value, axis, [(source, source + steps) for source in range(f...  4.35 us
    ppermute x3, waiting for transfers between devices, exchange(): lax.ppermute(value, 'space', [(i, (i + 2 * (s + 1)) % count) for i in ran...  3.89 us
    ppermute x1, starting transfers between devices, exchange(): pair = lax.ppermute(mine, 'space', [(i, i ^ 1) for i in range(count)])  2.4 us
  transfers between devices with their start and end apart: 6, of which 2 were waited for; matrix products, arithmetic and copies ran while one was open for 0% of the time, Pallas kernels for 42%

profile of v5, /device:TPU:0, one launch (start us, length us, event | category | flops | bytes accessed | tf_op | source)
XLA Modules:
  0.0 36.5 jit_solution(2371257681394553028)
XLA Ops:
  0.0 2.4 %collective-permute-start.11 = (bf16[4,16,3072]{2,1,0:T(8,128)(2,1)}, bf16[4,16,3072]{2,1,0:T(8,128)(2,1)S(1)}, u32[]{:S(2)}, u32[]{:S(2)}) collective-permute-start(bf16[4,16,3072]{2,1,0:T(8,128)(2,1)} %bitcast.183), channel_id=1, source_target_pairs={{0,8},{8,16},{16,24},{1,9},{9,17},{17,25},{2,10},{10,18},{18,26},{... | collective-permute-start | bytes 1179656 | tf_op jit(solution)/shard_map/ppermute | solution.py:16
  2.4 1.1 %shard_map.93 = (bf16[4,16,3072]{2,1,0:T(8,128)(2,1)S(1)}, bf16[2,4,16,384]{3,2,1,0:T(8,128)(2,1)S(1)}) custom-call(bf16[4,16,3072]{2,1,0:T(8,128)(2,1)} %bitcast.184), custom_call_target="tpu_custom_call" | custom-call | flops 31850496 | bytes 196608 | tf_op jit(solution)/shard_map/pallas_call | solution.py:459
  3.5 2.4 %collective-permute-start.6 = (bf16[2,4,16,384]{3,2,1,0:T(8,128)(2,1)S(1)}, bf16[2,4,16,384]{3,2,1,0:T(8,128)(2,1)S(1)}, u32[]{:S(2)}, u32[]{:S(2)}) collective-permute-start(bf16[2,4,16,384]{3,2,1,0:T(8,128)(2,1)S(1)} %get-tuple-element.379.mine), channel_id=1, source_target_pairs={{0,1},{1,0},{2,3},{3,2},{4,5},{5,4},{6,7},{7,6},{8,9},{9,8},{10,11... | collective-permute-start | bytes 294920 | tf_op jit(solution)/shard_map/ppermute | solution.py:433
  5.9 0.0 copy-start.2
  5.9 0.0 copy-start.4
  5.9 0.0 copy-start.5
  5.9 3.2 %shard_map.94 = (bf16[20,8,16,768]{3,2,1,0:T(8,128)(2,1)S(1)}, f32[8,16,128]{2,1,0:T(8,128)S(1)}, bf16[9,192,576]{2,1,0:T(8,128)(2,1)S(1)}, bf16[9,192,576]{2,1,0:T(8,128)(2,1)S(1)}, s32[16]{0:T(128)S(4)}) custom-call(s32[8,8]{1,0:T(8,128)} %nb.3, s32[8]{0:T(128)} %vf.1, bf16[4,16,3072]{2,1,0:T(8,128)(2,1)S(1)} %get-tuple-element.372.own, f32[192]{0:T(256)} %gain1.3, ...), custom_call_target="tpu_custom_call" | custom-call | flops 1019215872 | bytes 196608 | tf_op jit(solution)/shard_map/pallas_call | solution.py:459
  9.1 0.0 collective-permute-done.6.pair
  9.1 0.1 shard_map.96
  9.3 1.8 %collective-permute-start.7 = (bf16[2,4,16,384]{3,2,1,0:T(8,128)(2,1)S(1)}, bf16[2,4,16,384]{3,2,1,0:T(8,128)(2,1)S(1)}, u32[]{:S(2)}, u32[]{:S(2)}) collective-permute-start(bf16[2,4,16,384]{3,2,1,0:T(8,128)(2,1)S(1)} %get-tuple-element.380), channel_id=1, source_target_pairs={{0,2},{1,3},{2,4},{3,5},{4,6},{5,7},{6,0},{7,1},{8,10},{9,11},{10,... | collective-permute-start | bytes 294920 | tf_op jit(solution)/shard_map/ppermute | solution.py:445
  11.0 2.6 %collective-permute-start.8 = (bf16[2,4,16,384]{3,2,1,0:T(8,128)(2,1)S(1)}, bf16[2,4,16,384]{3,2,1,0:T(8,128)(2,1)S(1)}, u32[]{:S(2)}, u32[]{:S(2)}) collective-permute-start(bf16[2,4,16,384]{3,2,1,0:T(8,128)(2,1)S(1)} %get-tuple-element.381), channel_id=1, source_target_pairs={{0,4},{1,5},{2,6},{3,7},{4,0},{5,1},{6,2},{7,3},{8,12},{9,13},{10,... | collective-permute-start | bytes 294920 | tf_op jit(solution)/shard_map/ppermute | solution.py:445
  13.6 1.3 %collective-permute-start.9 = (bf16[2,4,16,384]{3,2,1,0:T(8,128)(2,1)S(1)}, bf16[2,4,16,384]{3,2,1,0:T(8,128)(2,1)S(1)}, u32[]{:S(2)}, u32[]{:S(2)}) collective-permute-start(bf16[2,4,16,384]{3,2,1,0:T(8,128)(2,1)S(1)} %get-tuple-element.382), channel_id=1, source_target_pairs={{0,6},{1,7},{2,0},{3,1},{4,2},{5,3},{6,4},{7,5},{8,14},{9,15},{10,... | collective-permute-start | bytes 294920 | tf_op jit(solution)/shard_map/ppermute | solution.py:445
  14.9 0.0 copy-done.2
  14.9 0.0 copy-done.4
  15.0 0.0 copy-done.5
  15.0 0.0 copy-start.3
  15.0 2.3 %shard_map.95 = (bf16[9,768,192]{2,1,0:T(8,128)(2,1)S(1)}, bf16[9,768,192]{2,1,0:T(8,128)(2,1)S(1)}, bf16[18,6,16,768]{3,2,1,0:T(8,128)(2,1)S(1)}, s32[1]{0:T(128)S(4)}) custom-call(f32[8,16,128]{2,1,0:T(8,128)S(1)} %get-tuple-element.373.mask, bf16[20,8,16,768]{3,2,1,0:T(8,128)(2,1)S(1)} %get-tuple-element.374.buf1.old1, ...), custom_call_target="tpu_custom_call" | custom-call | flops 2038431744 | bytes 196608 | tf_op jit(solution)/shard_map/pallas_call | solution.py:459
  17.3 0.0 collective-permute-done.7.rest_0_
  17.3 3.8 %collective-permute-done.8.rest_1_ = bf16[2,4,16,384]{3,2,1,0:T(8,128)(2,1)S(1)} collective-permute-done((bf16[2,4,16,384]{3,2,1,0:T(8,128)(2,1)S(1)}, bf16[2,4,16,384]{3,2,1,0:T(8,128)(2,1)S(1)}, u32[]{:S(2)}, u32[]{:S(2)}) %collective-permute-start.8) | collective-permute-done | bytes 98336 | tf_op jit(solution)/shard_map/ppermute | solution.py:445
  21.1 0.1 collective-permute-done.9.rest_2_
  21.2 1.9 %collective-permute-start.10 = (bf16[2,4,16,384]{3,2,1,0:T(8,128)(2,1)S(1)}, bf16[2,4,16,384]{3,2,1,0:T(8,128)(2,1)S(1)}, u32[]{:S(2)}, u32[]{:S(2)}) collective-permute-start(bf16[2,4,16,384]{3,2,1,0:T(8,128)(2,1)S(1)} %shard_map.97), channel_id=1, source_target_pairs={{0,8},{8,16},{16,24},{1,9},{9,17},{17,25},{2,10},{10,18},{18,26},{... | collective-permute-start | bytes 294920 | tf_op jit(solution)/shard_map/ppermute | solution.py:16
  23.2 0.0 collective-permute-done.11.prev
  23.2 0.0 copy-done.3
  23.2 0.0 copy-start.6
  23.2 3.5 %shard_map.98 = (bf16[20,8,16,768]{3,2,1,0:T(8,128)(2,1)S(1)}, f32[8,4,16,192]{3,2,1,0:T(8,128)S(1)}) custom-call(f32[8,16,128]{2,1,0:T(8,128)S(1)} %get-tuple-element.373.mask, bf16[4,16,3072]{2,1,0:T(8,128)(2,1)S(1)} %collective-permute-done.11.prev, f32[192]{0:T(256)S(1)} %copy-done.3, ...), custom_call_target="tpu_custom_call", output_to_operand_aliasing={{0}: (4, {})} | custom-call | flops 1528823808 | bytes 196608 | tf_op jit(solution)/shard_map/pallas_call | solution.py:459
  26.7 0.0 copy-done.6
  26.7 0.0 copy-start
  26.8 0.0 copy-start.7
  26.8 5.0 %shard_map.99 = (bf16[18,6,16,768]{3,2,1,0:T(8,128)(2,1)S(1)}, bf16[4,16,2304]{2,1,0:T(8,128)(2,1)S(1)}) custom-call(f32[8,16,128]{2,1,0:T(8,128)S(1)} %get-tuple-element.373.mask, bf16[4,16,3072]{2,1,0:T(8,128)(2,1)S(1)} %get-tuple-element.372.own, bf16[20,8,16,768]{3,2,1,0:T(8,128)(2,1)S(1)} %get-tuple-element.385.buf1, ...), custom_call_target="tpu_custom_call", output_to_operand_aliasing={{0}: (9, {})} | custom-call | flops 4076863488 | bytes 196608 | tf_op jit(solution)/shard_map/pallas_call | solution.py:459
  31.7 0.0 collective-permute-done.10
  31.7 0.0 copy-done
  31.8 0.0 copy-done.7
  31.8 4.6 %conditional.3 = ((bf16[4,1,16,3072]{3,2,0,1:T(8,128)(2,1)})) conditional(s32[]{:T(128)} %bitcast.58, (s32[8,8]{1,0:T(8,128)S(1)}, s32[8]{0:T(128)S(1)}, bf16[4,16,3072]{2,1,0:T(8,128)(2,1)S(1)}, bf16[2,4,16,384]{3,2,1,0:T(8,128)(2,1)S(1)}, bf16[2,4,16,384]{3,2,1,0:T(8,128)(2,1)S(1)}, /*index=5*/f32[192]{0:T(256)S(1)}, ...), branch_computations={%region_0.0_spmd, %region_1.12_spmd} | conditional | flops 483940256 | bytes 51179728 | solution.py:566
  32.0 4.4 %branch_0_fun.1 = (bf16[20,8,16,768]{3,2,1,0:T(8,128)(2,1)S(1)}, bf16[18,6,16,768]{3,2,1,0:T(8,128)(2,1)S(1)}, bf16[4,16,3072]{2,1,0:T(8,128)(2,1)}) custom-call(s32[8,8]{1,0:T(8,128)S(1)} %get-tuple-element.305.nb, s32[8]{0:T(128)S(1)} %get-tuple-element.306.vf, ...), custom_call_target="tpu_custom_call", output_to_operand_aliasing={{0}: (11, {}), {1}: (12, {})} | custom-call | flops 196608000 | bytes 196608 | tf_op jit(solution)/shard_map/cond/branch_0_fun/pallas_call | solution.py:459
  (1 shorter events, 0.0 us)
Async XLA Ops:
  0.0 23.2 %collective-permute-start.11 = (bf16[4,16,3072]{2,1,0:T(8,128)(2,1)}, bf16[4,16,3072]{2,1,0:T(8,128)(2,1)S(1)}, u32[]{:S(2)}, u32[]{:S(2)}) collective-permute-start(bf16[4,16,3072]{2,1,0:T(8,128)(2,1)} %bitcast.183), channel_id=1, source_target_pairs={{0,8},{8,16},{16,24},{1,9},{9,17},{17,25},{2,10},{10,18},{18,26},{... | collective-permute-start | bytes 1179656 | tf_op jit(solution)/shard_map/ppermute | solution.py:16
  3.5 5.6 %collective-permute-start.6 = (bf16[2,4,16,384]{3,2,1,0:T(8,128)(2,1)S(1)}, bf16[2,4,16,384]{3,2,1,0:T(8,128)(2,1)S(1)}, u32[]{:S(2)}, u32[]{:S(2)}) collective-permute-start(bf16[2,4,16,384]{3,2,1,0:T(8,128)(2,1)S(1)} %get-tuple-element.379.mine), channel_id=1, source_target_pairs={{0,1},{1,0},{2,3},{3,2},{4,5},{5,4},{6,7},{7,6},{8,9},{9,8},{10,11... | collective-permute-start | bytes 294920 | tf_op jit(solution)/shard_map/ppermute | solution.py:433
  5.9 9.0 %copy-start.2 = (s32[8,8]{1,0:T(8,128)S(1)}, s32[8,8]{1,0:T(8,128)}, u32[]{:S(2)}) copy-start(s32[8,8]{1,0:T(8,128)} %nb.3) | copy-start | bytes 772
  5.9 9.0 %copy-start.4 = (f32[192]{0:T(256)S(1)}, f32[192]{0:T(256)}, u32[]{:S(2)}) copy-start(f32[192]{0:T(256)} %bias1.3) | copy-start | bytes 2308
  5.9 9.0 %copy-start.5 = (f32[192]{0:T(256)S(1)}, f32[192]{0:T(256)}, u32[]{:S(2)}) copy-start(f32[192]{0:T(256)} %gain2.3) | copy-start | bytes 2308
  9.3 8.0 %collective-permute-start.7 = (bf16[2,4,16,384]{3,2,1,0:T(8,128)(2,1)S(1)}, bf16[2,4,16,384]{3,2,1,0:T(8,128)(2,1)S(1)}, u32[]{:S(2)}, u32[]{:S(2)}) collective-permute-start(bf16[2,4,16,384]{3,2,1,0:T(8,128)(2,1)S(1)} %get-tuple-element.380), channel_id=1, source_target_pairs={{0,2},{1,3},{2,4},{3,5},{4,6},{5,7},{6,0},{7,1},{8,10},{9,11},{10,... | collective-permute-start | bytes 294920 | tf_op jit(solution)/shard_map/ppermute | solution.py:445
  11.0 10.1 %collective-permute-start.8 = (bf16[2,4,16,384]{3,2,1,0:T(8,128)(2,1)S(1)}, bf16[2,4,16,384]{3,2,1,0:T(8,128)(2,1)S(1)}, u32[]{:S(2)}, u32[]{:S(2)}) collective-permute-start(bf16[2,4,16,384]{3,2,1,0:T(8,128)(2,1)S(1)} %get-tuple-element.381), channel_id=1, source_target_pairs={{0,4},{1,5},{2,6},{3,7},{4,0},{5,1},{6,2},{7,3},{8,12},{9,13},{10,... | collective-permute-start | bytes 294920 | tf_op jit(solution)/shard_map/ppermute | solution.py:445
  13.6 7.6 %collective-permute-start.9 = (bf16[2,4,16,384]{3,2,1,0:T(8,128)(2,1)S(1)}, bf16[2,4,16,384]{3,2,1,0:T(8,128)(2,1)S(1)}, u32[]{:S(2)}, u32[]{:S(2)}) collective-permute-start(bf16[2,4,16,384]{3,2,1,0:T(8,128)(2,1)S(1)} %get-tuple-element.382), channel_id=1, source_target_pairs={{0,6},{1,7},{2,0},{3,1},{4,2},{5,3},{6,4},{7,5},{8,14},{9,15},{10,... | collective-permute-start | bytes 294920 | tf_op jit(solution)/shard_map/ppermute | solution.py:445
  15.0 8.2 %copy-start.3 = (f32[192]{0:T(256)S(1)}, f32[192]{0:T(256)}, u32[]{:S(2)}) copy-start(f32[192]{0:T(256)} %gain1.3) | copy-start | bytes 2308
  21.2 10.5 %collective-permute-start.10 = (bf16[2,4,16,384]{3,2,1,0:T(8,128)(2,1)S(1)}, bf16[2,4,16,384]{3,2,1,0:T(8,128)(2,1)S(1)}, u32[]{:S(2)}, u32[]{:S(2)}) collective-permute-start(bf16[2,4,16,384]{3,2,1,0:T(8,128)(2,1)S(1)} %shard_map.97), channel_id=1, source_target_pairs={{0,8},{8,16},{16,24},{1,9},{9,17},{17,25},{2,10},{10,18},{18,26},{... | collective-permute-start | bytes 294920 | tf_op jit(solution)/shard_map/ppermute | solution.py:16
  23.2 3.6 %copy-start.6 = (f32[192]{0:T(256)S(1)}, f32[192]{0:T(256)}, u32[]{:S(2)}) copy-start(f32[192]{0:T(256)} %bias2.1) | copy-start | bytes 2308
  26.7 5.0 %copy-start = (bf16[4,1,16,3072]{3,2,1,0:T(8,128)(2,1)S(1)}, bf16[4,1,16,3072]{3,2,1,0:T(8,128)(2,1)}, u32[]{:S(2)}) copy-start(bf16[4,1,16,3072]{3,2,1,0:T(8,128)(2,1)} %param.19) | copy-start | bytes 1179652
  26.8 5.0 %copy-start.7 = (s32[8]{0:T(128)S(1)}, s32[8]{0:T(128)}, u32[]{:S(2)}) copy-start(s32[8]{0:T(128)} %vf.1) | copy-start | bytes 100

commit v6 on v5

--- a/solution.py
+++ b/solution.py
@@ -295,7 +295,9 @@
     for tile in range(nb.shape[0]):
         beside[2 * tile] = nb[tile, LEFT]
         beside[2 * tile + 1] = nb[tile, RIGHT]
-    first, valid = lax.axis_index("tm") * frames, tracks(nb, vf)[0]
+    for k, value in enumerate(tracks(nb, vf)):
+        beside[2 * nb.shape[0] + k] = value
+    first, valid = lax.axis_index("tm") * frames, beside[2 * nb.shape[0]]
     frame = first - frames + lax.broadcasted_iota(jnp.int32, mask.shape, 0)
     mask[...] = ((frame >= 0) & (frame < valid)).astype(jnp.float32)
     run(acts(buf1, own, there(first, frames, valid), frames, 0.5 * row_of(gain1)))
@@ -345,12 +347,12 @@
     run(finishes(totals, out, own, 2 + half, half, row_of(bias2), present))
 
 
-def rim_kernel(nb, vf, own, rim, prev_rim, gain1, weight1, bias1, gain2, weight2, bias2, old1, old2, inner, buf1, buf2, out, *scratch):
+def rim_kernel(beside, own, rim, prev_rim, gain1, weight1, bias1, gain2, weight2, bias2, old1, old2, inner, buf1, buf2, out, *scratch):
     *accs, staged, sem = scratch
     frames, _, merged = own.shape
     columns = buf2.shape[0] - 2
     first = lax.axis_index("tm") * frames
-    valid, left, right = tracks(nb, vf)
+    valid, left, right = (beside[beside.shape[0] - 3 + k] for k in range(3))
     ends = staged.shape[3]
     copies = [pltpu.make_async_copy(inner, out.at[:, :, pl.ds(ends, merged - 2 * ends)], sem.at[2])]
     copies[0].start()
@@ -385,7 +387,7 @@
 
 
 def pick_kernel(beside, mine, pair, *outs):
-    tiles = beside.shape[0] // 2
+    tiles = (beside.shape[0] - 3) // 2
     me = lax.axis_index("space")
     for step, out in enumerate(outs):
         there = lax.rem(me + 2 * (step + 1), tiles)
@@ -403,7 +405,7 @@
 
 def rims_kernel(beside, mine, pair, *rest):
     received, out = rest[:-1], rest[-1]
-    tiles = beside.shape[0] // 2
+    tiles = (beside.shape[0] - 3) // 2
     half = tiles // 2
     me = lax.axis_index("space")
     for side in range(2):
@@ -502,7 +504,7 @@
     buf1, mask, flat1, flat2, beside = call(
         tile_kernel,
         (one * 2 * columns, own.size),
-        [space1, pltpu.VMEM((2 * frames, side, 128), jnp.float32), flat, flat, pltpu.SMEM((2 * neighbours.shape[0],), jnp.int32)],
+        [space1, pltpu.VMEM((2 * frames, side, 128), jnp.float32), flat, flat, pltpu.SMEM((2 * neighbours.shape[0] + 3,), jnp.int32)],
         [SM, SM, VM, VM, HB, HB],
         (*tables, own, gain1, jnp.swapaxes(weight1, 1, 2), jnp.swapaxes(weight2, 1, 2)),
         places=[VM] * 4 + [SM],
@@ -536,21 +538,21 @@
         input_output_aliases={9: 0},
         scratch_shapes=[room(columns // 2, 4)] + [room(columns // 2, frames)] * 2,
     )
-    return flag, (own, rim, prev_rim, wide1, wide2, buf1, buf2, inner)
-
-
-def row_end(state, tables, gain1, bias1, gain2, bias2):
-    own, rim, prev_rim, wide1, wide2, buf1, buf2, inner = state
+    return flag, (beside, own, rim, prev_rim, wide1, wide2, buf1, buf2, inner)
+
+
+def row_end(state, gain1, bias1, gain2, bias2):
+    beside, own, rim, prev_rim, wide1, wide2, buf1, buf2, inner = state
     space1, space2 = pltpu.VMEM(buf1.shape, buf1.dtype), pltpu.VMEM(buf2.shape, buf2.dtype)
     room = rooms(own.shape[1], gain1.shape[0])
     _, _, out = call(
         rim_kernel,
         (own.size * 1000, own.size),
         [space1, space2, jax.ShapeDtypeStruct(own.shape, own.dtype)],
-        [SM, SM] + [VM] * 12,
-        (*tables, own, rim, prev_rim, gain1, wide1, bias1, gain2, wide2, bias2, buf1, buf2, inner),
+        [SM] + [VM] * 12,
+        (beside, own, rim, prev_rim, gain1, wide1, bias1, gain2, wide2, bias2, buf1, buf2, inner),
         places=[VM, VM, HB],
-        input_output_aliases={11: 0, 12: 1},
+        input_output_aliases={10: 0, 11: 1},
         scratch_shapes=[room(2, own.shape[0] + 2)] * 4 + [pltpu.VMEM(rim.shape, rim.dtype), pltpu.SemaphoreType.DMA((3,))],
     )
     return out[:, None]
@@ -566,7 +568,7 @@
     return lax.cond(
         flag[0] > 0,
         lambda state, args: general_path(*args),
-        lambda state, args: row_end(state, args[1:3], gain1, bias1, gain2, bias2),
+        lambda state, args: row_end(state, gain1, bias1, gain2, bias2),
         state,
         args,
     )

time: 36.7 us -> 36.2 us (0.986)
  Pallas kernels: 19.6 us -> 19 us
    pallas_call x6, Pallas kernels: 19.5 us -> 18.9 us  [call(): pl.pallas_call(kernel, out_shape=outs, in_specs=ins, out_specs=[VM] * len...]
where the time goes in v6:
time: 36.2 us; the launch traced here: 36 us
  Pallas kernels  19 us (52%)
  starting transfers between devices  12.4 us (34%)
  waiting for transfers between devices  3.92 us (11%)
    pallas_call x6, Pallas kernels, call(): pl.pallas_call(kernel, out_shape=outs, in_specs=ins, out_specs=[VM] * len...  18.9 us
    ppermute x3, starting transfers between devices, exchange(): lax.ppermute(value, 'space', [(i, (i + 2 * (s + 1)) % count) for i in ran...  5.67 us
    ppermute x2, starting transfers between devices, shifted(): lax.ppermute(value, axis, [(source, source + steps) for source in range(f...  4.35 us
    ppermute x3, waiting for transfers between devices, exchange(): lax.ppermute(value, 'space', [(i, (i + 2 * (s + 1)) % count) for i in ran...  3.91 us
    ppermute x1, starting transfers between devices, exchange(): pair = lax.ppermute(mine, 'space', [(i, i ^ 1) for i in range(count)])  2.4 us
  transfers between devices with their start and end apart: 6, of which 2 were waited for; matrix products, arithmetic and copies ran while one was open for 0% of the time, Pallas kernels for 42%

profile of v6, /device:TPU:0, one launch (start us, length us, event | category | flops | bytes accessed | tf_op | source)
XLA Modules:
  0.0 36.0 jit_solution(17046172507079602431)
XLA Ops:
  0.0 2.4 %collective-permute-start.11 = (bf16[4,16,3072]{2,1,0:T(8,128)(2,1)}, bf16[4,16,3072]{2,1,0:T(8,128)(2,1)S(1)}, u32[]{:S(2)}, u32[]{:S(2)}) collective-permute-start(bf16[4,16,3072]{2,1,0:T(8,128)(2,1)} %bitcast.183), channel_id=1, source_target_pairs={{0,8},{8,16},{16,24},{1,9},{9,17},{17,25},{2,10},{10,18},{18,26},{... | collective-permute-start | bytes 1179656 | tf_op jit(solution)/shard_map/ppermute | solution.py:16
  2.4 1.1 %shard_map.93 = (bf16[4,16,3072]{2,1,0:T(8,128)(2,1)S(1)}, bf16[2,4,16,384]{3,2,1,0:T(8,128)(2,1)S(1)}) custom-call(bf16[4,16,3072]{2,1,0:T(8,128)(2,1)} %bitcast.184), custom_call_target="tpu_custom_call" | custom-call | flops 31850496 | bytes 196608 | tf_op jit(solution)/shard_map/pallas_call | solution.py:461
  3.5 2.4 %collective-permute-start.6 = (bf16[2,4,16,384]{3,2,1,0:T(8,128)(2,1)S(1)}, bf16[2,4,16,384]{3,2,1,0:T(8,128)(2,1)S(1)}, u32[]{:S(2)}, u32[]{:S(2)}) collective-permute-start(bf16[2,4,16,384]{3,2,1,0:T(8,128)(2,1)S(1)} %get-tuple-element.376.mine), channel_id=1, source_target_pairs={{0,1},{1,0},{2,3},{3,2},{4,5},{5,4},{6,7},{7,6},{8,9},{9,8},{10,11... | collective-permute-start | bytes 294920 | tf_op jit(solution)/shard_map/ppermute | solution.py:435
  5.9 0.0 copy-start.2
  5.9 0.0 copy-start.4
  5.9 0.0 copy-start.5
  5.9 3.2 %shard_map.94 = (bf16[20,8,16,768]{3,2,1,0:T(8,128)(2,1)S(1)}, f32[8,16,128]{2,1,0:T(8,128)S(1)}, bf16[9,192,576]{2,1,0:T(8,128)(2,1)S(1)}, bf16[9,192,576]{2,1,0:T(8,128)(2,1)S(1)}, s32[19]{0:T(128)S(4)}) custom-call(s32[8,8]{1,0:T(8,128)} %nb.3, s32[8]{0:T(128)} %vf.1, bf16[4,16,3072]{2,1,0:T(8,128)(2,1)S(1)} %get-tuple-element.369.own, f32[192]{0:T(256)} %gain1.3, ...), custom_call_target="tpu_custom_call" | custom-call | flops 1019215872 | bytes 196608 | tf_op jit(solution)/shard_map/pallas_call | solution.py:461
  9.2 0.0 collective-permute-done.6.pair
  9.2 0.1 shard_map.96
  9.3 1.7 %collective-permute-start.7 = (bf16[2,4,16,384]{3,2,1,0:T(8,128)(2,1)S(1)}, bf16[2,4,16,384]{3,2,1,0:T(8,128)(2,1)S(1)}, u32[]{:S(2)}, u32[]{:S(2)}) collective-permute-start(bf16[2,4,16,384]{3,2,1,0:T(8,128)(2,1)S(1)} %get-tuple-element.377), channel_id=1, source_target_pairs={{0,2},{1,3},{2,4},{3,5},{4,6},{5,7},{6,0},{7,1},{8,10},{9,11},{10,... | collective-permute-start | bytes 294920 | tf_op jit(solution)/shard_map/ppermute | solution.py:447
  11.0 2.6 %collective-permute-start.8 = (bf16[2,4,16,384]{3,2,1,0:T(8,128)(2,1)S(1)}, bf16[2,4,16,384]{3,2,1,0:T(8,128)(2,1)S(1)}, u32[]{:S(2)}, u32[]{:S(2)}) collective-permute-start(bf16[2,4,16,384]{3,2,1,0:T(8,128)(2,1)S(1)} %get-tuple-element.378), channel_id=1, source_target_pairs={{0,4},{1,5},{2,6},{3,7},{4,0},{5,1},{6,2},{7,3},{8,12},{9,13},{10,... | collective-permute-start | bytes 294920 | tf_op jit(solution)/shard_map/ppermute | solution.py:447
  13.6 1.3 %collective-permute-start.9 = (bf16[2,4,16,384]{3,2,1,0:T(8,128)(2,1)S(1)}, bf16[2,4,16,384]{3,2,1,0:T(8,128)(2,1)S(1)}, u32[]{:S(2)}, u32[]{:S(2)}) collective-permute-start(bf16[2,4,16,384]{3,2,1,0:T(8,128)(2,1)S(1)} %get-tuple-element.379), channel_id=1, source_target_pairs={{0,6},{1,7},{2,0},{3,1},{4,2},{5,3},{6,4},{7,5},{8,14},{9,15},{10,... | collective-permute-start | bytes 294920 | tf_op jit(solution)/shard_map/ppermute | solution.py:447
  14.9 0.0 copy-done.2
  14.9 0.0 copy-done.4
  15.0 0.0 copy-done.5
  15.0 0.0 copy-start.3
  15.0 2.3 %shard_map.95 = (bf16[9,768,192]{2,1,0:T(8,128)(2,1)S(1)}, bf16[9,768,192]{2,1,0:T(8,128)(2,1)S(1)}, bf16[18,6,16,768]{3,2,1,0:T(8,128)(2,1)S(1)}, s32[1]{0:T(128)S(4)}) custom-call(f32[8,16,128]{2,1,0:T(8,128)S(1)} %get-tuple-element.370.mask, bf16[20,8,16,768]{3,2,1,0:T(8,128)(2,1)S(1)} %get-tuple-element.371.buf1.old1, ...), custom_call_target="tpu_custom_call" | custom-call | flops 2038431744 | bytes 196608 | tf_op jit(solution)/shard_map/pallas_call | solution.py:461
  17.3 0.0 collective-permute-done.7.rest_0_
  17.3 3.8 %collective-permute-done.8.rest_1_ = bf16[2,4,16,384]{3,2,1,0:T(8,128)(2,1)S(1)} collective-permute-done((bf16[2,4,16,384]{3,2,1,0:T(8,128)(2,1)S(1)}, bf16[2,4,16,384]{3,2,1,0:T(8,128)(2,1)S(1)}, u32[]{:S(2)}, u32[]{:S(2)}) %collective-permute-start.8) | collective-permute-done | bytes 98336 | tf_op jit(solution)/shard_map/ppermute | solution.py:447
  21.1 0.1 collective-permute-done.9.rest_2_
  21.2 1.9 %collective-permute-start.10 = (bf16[2,4,16,384]{3,2,1,0:T(8,128)(2,1)S(1)}, bf16[2,4,16,384]{3,2,1,0:T(8,128)(2,1)S(1)}, u32[]{:S(2)}, u32[]{:S(2)}) collective-permute-start(bf16[2,4,16,384]{3,2,1,0:T(8,128)(2,1)S(1)} %shard_map.97), channel_id=1, source_target_pairs={{0,8},{8,16},{16,24},{1,9},{9,17},{17,25},{2,10},{10,18},{18,26},{... | collective-permute-start | bytes 294920 | tf_op jit(solution)/shard_map/ppermute | solution.py:16
  23.2 0.0 collective-permute-done.11.prev
  23.2 0.0 copy-done.3
  23.2 0.0 copy-start.6
  23.2 3.5 %shard_map.98 = (bf16[20,8,16,768]{3,2,1,0:T(8,128)(2,1)S(1)}, f32[8,4,16,192]{3,2,1,0:T(8,128)S(1)}) custom-call(f32[8,16,128]{2,1,0:T(8,128)S(1)} %get-tuple-element.370.mask, bf16[4,16,3072]{2,1,0:T(8,128)(2,1)S(1)} %collective-permute-done.11.prev, f32[192]{0:T(256)S(1)} %copy-done.3, ...), custom_call_target="tpu_custom_call", output_to_operand_aliasing={{0}: (4, {})} | custom-call | flops 1528823808 | bytes 196608 | tf_op jit(solution)/shard_map/pallas_call | solution.py:461
  26.8 0.0 copy-done.6
  26.8 0.0 copy-start
  26.8 0.0 copy-start.7
  26.8 5.0 %shard_map.99 = (bf16[18,6,16,768]{3,2,1,0:T(8,128)(2,1)S(1)}, bf16[4,16,2304]{2,1,0:T(8,128)(2,1)S(1)}) custom-call(f32[8,16,128]{2,1,0:T(8,128)S(1)} %get-tuple-element.370.mask, bf16[4,16,3072]{2,1,0:T(8,128)(2,1)S(1)} %get-tuple-element.369.own, bf16[20,8,16,768]{3,2,1,0:T(8,128)(2,1)S(1)} %get-tuple-element.382.buf1, ...), custom_call_target="tpu_custom_call", output_to_operand_aliasing={{0}: (9, {})} | custom-call | flops 4076863488 | bytes 196608 | tf_op jit(solution)/shard_map/pallas_call | solution.py:461
  31.8 0.0 collective-permute-done.10
  31.8 0.0 copy-done
  31.8 0.0 copy-done.7
  31.8 4.0 %conditional.3 = ((bf16[4,1,16,3072]{3,2,0,1:T(8,128)(2,1)})) conditional(s32[]{:T(128)} %bitcast.58, (s32[19]{0:T(128)S(4)}, bf16[4,16,3072]{2,1,0:T(8,128)(2,1)S(1)}, bf16[2,4,16,384]{3,2,1,0:T(8,128)(2,1)S(1)}, bf16[2,4,16,384]{3,2,1,0:T(8,128)(2,1)S(1)}, f32[192]{0:T(256)S(1)}, /*index=5*/bf16[9,768,192]{2,1,0:T(8,128)(2,1)S(1)}, ...), branch_computations={%region_0.0_spmd, %region_1.12_spmd} | conditional | flops 483940256 | bytes 51179728 | solution.py:568
  32.0 3.8 %branch_0_fun.1 = (bf16[20,8,16,768]{3,2,1,0:T(8,128)(2,1)S(1)}, bf16[18,6,16,768]{3,2,1,0:T(8,128)(2,1)S(1)}, bf16[4,16,3072]{2,1,0:T(8,128)(2,1)}) custom-call(s32[19]{0:T(128)S(4)} %get-tuple-element.303.beside, bf16[4,16,3072]{2,1,0:T(8,128)(2,1)S(1)} %get-tuple-element.304.own, ...), custom_call_target="tpu_custom_call", output_to_operand_aliasing={{0}: (10, {}), {1}: (11, {})} | custom-call | flops 196608000 | bytes 196608 | tf_op jit(solution)/shard_map/cond/branch_0_fun/pallas_call | solution.py:461
  (1 shorter events, 0.0 us)
Async XLA Ops:
  0.0 23.2 %collective-permute-start.11 = (bf16[4,16,3072]{2,1,0:T(8,128)(2,1)}, bf16[4,16,3072]{2,1,0:T(8,128)(2,1)S(1)}, u32[]{:S(2)}, u32[]{:S(2)}) collective-permute-start(bf16[4,16,3072]{2,1,0:T(8,128)(2,1)} %bitcast.183), channel_id=1, source_target_pairs={{0,8},{8,16},{16,24},{1,9},{9,17},{17,25},{2,10},{10,18},{18,26},{... | collective-permute-start | bytes 1179656 | tf_op jit(solution)/shard_map/ppermute | solution.py:16
  3.5 5.6 %collective-permute-start.6 = (bf16[2,4,16,384]{3,2,1,0:T(8,128)(2,1)S(1)}, bf16[2,4,16,384]{3,2,1,0:T(8,128)(2,1)S(1)}, u32[]{:S(2)}, u32[]{:S(2)}) collective-permute-start(bf16[2,4,16,384]{3,2,1,0:T(8,128)(2,1)S(1)} %get-tuple-element.376.mine), channel_id=1, source_target_pairs={{0,1},{1,0},{2,3},{3,2},{4,5},{5,4},{6,7},{7,6},{8,9},{9,8},{10,11... | collective-permute-start | bytes 294920 | tf_op jit(solution)/shard_map/ppermute | solution.py:435
  5.9 9.0 %copy-start.2 = (s32[8,8]{1,0:T(8,128)S(1)}, s32[8,8]{1,0:T(8,128)}, u32[]{:S(2)}) copy-start(s32[8,8]{1,0:T(8,128)} %nb.3) | copy-start | bytes 772
  5.9 9.0 %copy-start.4 = (f32[192]{0:T(256)S(1)}, f32[192]{0:T(256)}, u32[]{:S(2)}) copy-start(f32[192]{0:T(256)} %bias1.3) | copy-start | bytes 2308
  5.9 9.0 %copy-start.5 = (f32[192]{0:T(256)S(1)}, f32[192]{0:T(256)}, u32[]{:S(2)}) copy-start(f32[192]{0:T(256)} %gain2.3) | copy-start | bytes 2308
  9.3 8.0 %collective-permute-start.7 = (bf16[2,4,16,384]{3,2,1,0:T(8,128)(2,1)S(1)}, bf16[2,4,16,384]{3,2,1,0:T(8,128)(2,1)S(1)}, u32[]{:S(2)}, u32[]{:S(2)}) collective-permute-start(bf16[2,4,16,384]{3,2,1,0:T(8,128)(2,1)S(1)} %get-tuple-element.377), channel_id=1, source_target_pairs={{0,2},{1,3},{2,4},{3,5},{4,6},{5,7},{6,0},{7,1},{8,10},{9,11},{10,... | collective-permute-start | bytes 294920 | tf_op jit(solution)/shard_map/ppermute | solution.py:447
  11.0 10.1 %collective-permute-start.8 = (bf16[2,4,16,384]{3,2,1,0:T(8,128)(2,1)S(1)}, bf16[2,4,16,384]{3,2,1,0:T(8,128)(2,1)S(1)}, u32[]{:S(2)}, u32[]{:S(2)}) collective-permute-start(bf16[2,4,16,384]{3,2,1,0:T(8,128)(2,1)S(1)} %get-tuple-element.378), channel_id=1, source_target_pairs={{0,4},{1,5},{2,6},{3,7},{4,0},{5,1},{6,2},{7,3},{8,12},{9,13},{10,... | collective-permute-start | bytes 294920 | tf_op jit(solution)/shard_map/ppermute | solution.py:447
  13.6 7.6 %collective-permute-start.9 = (bf16[2,4,16,384]{3,2,1,0:T(8,128)(2,1)S(1)}, bf16[2,4,16,384]{3,2,1,0:T(8,128)(2,1)S(1)}, u32[]{:S(2)}, u32[]{:S(2)}) collective-permute-start(bf16[2,4,16,384]{3,2,1,0:T(8,128)(2,1)S(1)} %get-tuple-element.379), channel_id=1, source_target_pairs={{0,6},{1,7},{2,0},{3,1},{4,2},{5,3},{6,4},{7,5},{8,14},{9,15},{10,... | collective-permute-start | bytes 294920 | tf_op jit(solution)/shard_map/ppermute | solution.py:447
  15.0 8.2 %copy-start.3 = (f32[192]{0:T(256)S(1)}, f32[192]{0:T(256)}, u32[]{:S(2)}) copy-start(f32[192]{0:T(256)} %gain1.3) | copy-start | bytes 2308
  21.2 10.5 %collective-permute-start.10 = (bf16[2,4,16,384]{3,2,1,0:T(8,128)(2,1)S(1)}, bf16[2,4,16,384]{3,2,1,0:T(8,128)(2,1)S(1)}, u32[]{:S(2)}, u32[]{:S(2)}) collective-permute-start(bf16[2,4,16,384]{3,2,1,0:T(8,128)(2,1)S(1)} %shard_map.97), channel_id=1, source_target_pairs={{0,8},{8,16},{16,24},{1,9},{9,17},{17,25},{2,10},{10,18},{18,26},{... | collective-permute-start | bytes 294920 | tf_op jit(solution)/shard_map/ppermute | solution.py:16
  23.2 3.6 %copy-start.6 = (f32[192]{0:T(256)S(1)}, f32[192]{0:T(256)}, u32[]{:S(2)}) copy-start(f32[192]{0:T(256)} %bias2.1) | copy-start | bytes 2308
  26.8 5.0 %copy-start = (bf16[4,1,16,3072]{3,2,1,0:T(8,128)(2,1)S(1)}, bf16[4,1,16,3072]{3,2,1,0:T(8,128)(2,1)}, u32[]{:S(2)}) copy-start(bf16[4,1,16,3072]{3,2,1,0:T(8,128)(2,1)} %param.19) | copy-start | bytes 1179652
  26.8 5.0 %copy-start.7 = (s32[8]{0:T(128)S(1)}, s32[8]{0:T(128)}, u32[]{:S(2)}) copy-start(s32[8]{0:T(128)} %vf.1) | copy-start | bytes 100

commit v7 on v6

--- a/solution.py
+++ b/solution.py
@@ -274,12 +274,14 @@
         work()
 
 
-def load_kernel(far, own, mine, sem):
+def load_kernel(far, far_nb, far_vf, own, mine, nb, vf, sem):
     lanes = mine.shape[3]
     copies = [
         pltpu.make_async_copy(far.at[:, :, pl.ds(0, lanes)], mine.at[0], sem.at[0]),
         pltpu.make_async_copy(far.at[:, :, pl.ds(far.shape[2] - lanes, lanes)], mine.at[1], sem.at[1]),
         pltpu.make_async_copy(far, own, sem.at[2]),
+        pltpu.make_async_copy(far_nb, nb, sem.at[3]),
+        pltpu.make_async_copy(far_vf, vf, sem.at[4]),
     ]
     for copy in copies:
         copy.start()
@@ -490,13 +492,15 @@
     room = rooms(side, channels)
     one = 2 * 27 * channels * channels * side
     flat = pltpu.VMEM((9, channels, 3 * channels), jnp.bfloat16)
-    own, mine = call(
+    own, mine, *near = call(
         load_kernel,
         (one, far.size),
-        [pltpu.VMEM(far.shape, far.dtype), pltpu.VMEM((2, frames, side, 2 * channels), far.dtype)],
-        [HB],
-        (far,),
-        scratch_shapes=[pltpu.SemaphoreType.DMA((3,))],
+        [pltpu.VMEM(far.shape, far.dtype), pltpu.VMEM((2, frames, side, 2 * channels), far.dtype)]
+        + [pltpu.SMEM(table.shape, table.dtype) for table in tables],
+        [HB] * 3,
+        (far, *tables),
+        places=[VM, VM, SM, SM],
+        scratch_shapes=[pltpu.SemaphoreType.DMA((5,))],
     )
     space1 = pltpu.VMEM((columns + 4, 2 * frames, side, 3 * LANE), jnp.bfloat16)
     space2 = pltpu.VMEM((columns + 2, frames + 2, side, 3 * LANE), jnp.bfloat16)
@@ -506,7 +510,7 @@
         (one * 2 * columns, own.size),
         [space1, pltpu.VMEM((2 * frames, side, 128), jnp.float32), flat, flat, pltpu.SMEM((2 * neighbours.shape[0] + 3,), jnp.int32)],
         [SM, SM, VM, VM, HB, HB],
-        (*tables, own, gain1, jnp.swapaxes(weight1, 1, 2), jnp.swapaxes(weight2, 1, 2)),
+        (*near, own, gain1, jnp.swapaxes(weight1, 1, 2), jnp.swapaxes(weight2, 1, 2)),
         places=[VM] * 4 + [SM],
         scratch_shapes=[pltpu.SemaphoreType.DMA((2,))],
     )

time: 36.2 us -> 36.1 us (level)
  transfers between devices with their start and end apart: 6 -> 6, of which waited for: 2 -> 1; matrix products, arithmetic and copies ran while one was open for 0% -> 0% of each run, Pallas kernels for 42% -> 42%
where the time goes in v7:
time: 36.1 us; the launch traced here: 35.9 us
  Pallas kernels  19 us (53%)
  starting transfers between devices  12.6 us (35%)
  waiting for transfers between devices  3.74 us (10%)
    pallas_call x6, Pallas kernels, call(): pl.pallas_call(kernel, out_shape=outs, in_specs=ins, out_specs=[VM] * len...  18.9 us
    ppermute x3, starting transfers between devices, exchange(): lax.ppermute(value, 'space', [(i, (i + 2 * (s + 1)) % count) for i in ran...  5.81 us
    ppermute x2, starting transfers between devices, shifted(): lax.ppermute(value, axis, [(source, source + steps) for source in range(f...  4.38 us
    ppermute x3, waiting for transfers between devices, exchange(): lax.ppermute(value, 'space', [(i, (i + 2 * (s + 1)) % count) for i in ran...  3.73 us
    ppermute x1, starting transfers between devices, exchange(): pair = lax.ppermute(mine, 'space', [(i, i ^ 1) for i in range(count)])  2.4 us
  transfers between devices with their start and end apart: 6, of which 1 were waited for; matrix products, arithmetic and copies ran while one was open for 0% of the time, Pallas kernels for 42%

profile of v7, /device:TPU:0, one launch (start us, length us, event | category | flops | bytes accessed | tf_op | source)
XLA Modules:
  0.0 35.9 jit_solution(3152192584988780011)
XLA Ops:
  0.0 2.4 %collective-permute-start.11 = (bf16[4,16,3072]{2,1,0:T(8,128)(2,1)}, bf16[4,16,3072]{2,1,0:T(8,128)(2,1)S(1)}, u32[]{:S(2)}, u32[]{:S(2)}) collective-permute-start(bf16[4,16,3072]{2,1,0:T(8,128)(2,1)} %bitcast.183), channel_id=1, source_target_pairs={{0,8},{8,16},{16,24},{1,9},{9,17},{17,25},{2,10},{10,18},{18,26},{... | collective-permute-start | bytes 1179656 | tf_op jit(solution)/shard_map/ppermute | solution.py:16
  2.4 1.1 %shard_map.93 = (bf16[4,16,3072]{2,1,0:T(8,128)(2,1)S(1)}, bf16[2,4,16,384]{3,2,1,0:T(8,128)(2,1)S(1)}, s32[8,8]{1,0:T(8,128)S(4)}, s32[8]{0:T(128)S(4)}) custom-call(bf16[4,16,3072]{2,1,0:T(8,128)(2,1)} %bitcast.184, s32[8,8]{1,0:T(8,128)} %nb.1, s32[8]{0:T(128)} %far_vf.1), custom_call_target="tpu_custom_call" | custom-call | flops 31850496 | bytes 196608 | tf_op jit(solution)/shard_map/pallas_call | solution.py:463
  3.6 2.4 %collective-permute-start.6 = (bf16[2,4,16,384]{3,2,1,0:T(8,128)(2,1)S(1)}, bf16[2,4,16,384]{3,2,1,0:T(8,128)(2,1)S(1)}, u32[]{:S(2)}, u32[]{:S(2)}) collective-permute-start(bf16[2,4,16,384]{3,2,1,0:T(8,128)(2,1)S(1)} %get-tuple-element.380.mine), channel_id=1, source_target_pairs={{0,1},{1,0},{2,3},{3,2},{4,5},{5,4},{6,7},{7,6},{8,9},{9,8},{10,11... | collective-permute-start | bytes 294920 | tf_op jit(solution)/shard_map/ppermute | solution.py:437
  6.0 0.0 copy-start.2
  6.0 0.0 copy-start.4
  6.0 0.0 copy-start.5
  6.0 3.1 %shard_map.94 = (bf16[20,8,16,768]{3,2,1,0:T(8,128)(2,1)S(1)}, f32[8,16,128]{2,1,0:T(8,128)S(1)}, bf16[9,192,576]{2,1,0:T(8,128)(2,1)S(1)}, bf16[9,192,576]{2,1,0:T(8,128)(2,1)S(1)}, s32[19]{0:T(128)S(4)}) custom-call(s32[8,8]{1,0:T(8,128)S(4)} %get-tuple-element.371.nb, s32[8]{0:T(128)S(4)} %get-tuple-element.372.vf, ...), custom_call_target="tpu_custom_call" | custom-call | flops 1019215872 | bytes 196608 | tf_op jit(solution)/shard_map/pallas_call | solution.py:463
  9.1 0.0 collective-permute-done.6.pair
  9.1 0.1 shard_map.96
  9.2 1.9 %collective-permute-start.7 = (bf16[2,4,16,384]{3,2,1,0:T(8,128)(2,1)S(1)}, bf16[2,4,16,384]{3,2,1,0:T(8,128)(2,1)S(1)}, u32[]{:S(2)}, u32[]{:S(2)}) collective-permute-start(bf16[2,4,16,384]{3,2,1,0:T(8,128)(2,1)S(1)} %get-tuple-element.381), channel_id=1, source_target_pairs={{0,2},{1,3},{2,4},{3,5},{4,6},{5,7},{6,0},{7,1},{8,10},{9,11},{10,... | collective-permute-start | bytes 294920 | tf_op jit(solution)/shard_map/ppermute | solution.py:449
  11.0 2.6 %collective-permute-start.8 = (bf16[2,4,16,384]{3,2,1,0:T(8,128)(2,1)S(1)}, bf16[2,4,16,384]{3,2,1,0:T(8,128)(2,1)S(1)}, u32[]{:S(2)}, u32[]{:S(2)}) collective-permute-start(bf16[2,4,16,384]{3,2,1,0:T(8,128)(2,1)S(1)} %get-tuple-element.382), channel_id=1, source_target_pairs={{0,4},{1,5},{2,6},{3,7},{4,0},{5,1},{6,2},{7,3},{8,12},{9,13},{10,... | collective-permute-start | bytes 294920 | tf_op jit(solution)/shard_map/ppermute | solution.py:449
  13.6 1.3 %collective-permute-start.9 = (bf16[2,4,16,384]{3,2,1,0:T(8,128)(2,1)S(1)}, bf16[2,4,16,384]{3,2,1,0:T(8,128)(2,1)S(1)}, u32[]{:S(2)}, u32[]{:S(2)}) collective-permute-start(bf16[2,4,16,384]{3,2,1,0:T(8,128)(2,1)S(1)} %get-tuple-element.383), channel_id=1, source_target_pairs={{0,6},{1,7},{2,0},{3,1},{4,2},{5,3},{6,4},{7,5},{8,14},{9,15},{10,... | collective-permute-start | bytes 294920 | tf_op jit(solution)/shard_map/ppermute | solution.py:449
  15.0 0.0 copy-done.2
  15.0 0.0 copy-done.4
  15.0 0.0 copy-done.5
  15.0 0.0 copy-start.3
  15.0 2.3 %shard_map.95 = (bf16[9,768,192]{2,1,0:T(8,128)(2,1)S(1)}, bf16[9,768,192]{2,1,0:T(8,128)(2,1)S(1)}, bf16[18,6,16,768]{3,2,1,0:T(8,128)(2,1)S(1)}, s32[1]{0:T(128)S(4)}) custom-call(f32[8,16,128]{2,1,0:T(8,128)S(1)} %get-tuple-element.374.mask, bf16[20,8,16,768]{3,2,1,0:T(8,128)(2,1)S(1)} %get-tuple-element.375.buf1.old1, ...), custom_call_target="tpu_custom_call" | custom-call | flops 2038431744 | bytes 196608 | tf_op jit(solution)/shard_map/pallas_call | solution.py:463
  17.3 0.0 collective-permute-done.7.rest_0_
  17.3 3.7 %collective-permute-done.8.rest_1_ = bf16[2,4,16,384]{3,2,1,0:T(8,128)(2,1)S(1)} collective-permute-done((bf16[2,4,16,384]{3,2,1,0:T(8,128)(2,1)S(1)}, bf16[2,4,16,384]{3,2,1,0:T(8,128)(2,1)S(1)}, u32[]{:S(2)}, u32[]{:S(2)}) %collective-permute-start.8) | collective-permute-done | bytes 98336 | tf_op jit(solution)/shard_map/ppermute | solution.py:449
  21.0 0.0 collective-permute-done.9.rest_2_
  21.1 2.0 %collective-permute-start.10 = (bf16[2,4,16,384]{3,2,1,0:T(8,128)(2,1)S(1)}, bf16[2,4,16,384]{3,2,1,0:T(8,128)(2,1)S(1)}, u32[]{:S(2)}, u32[]{:S(2)}) collective-permute-start(bf16[2,4,16,384]{3,2,1,0:T(8,128)(2,1)S(1)} %shard_map.97), channel_id=1, source_target_pairs={{0,8},{8,16},{16,24},{1,9},{9,17},{17,25},{2,10},{10,18},{18,26},{... | collective-permute-start | bytes 294920 | tf_op jit(solution)/shard_map/ppermute | solution.py:16
  23.1 0.0 collective-permute-done.11.prev
  23.1 0.0 copy-done.3
  23.1 0.0 copy-start.6
  23.1 3.5 %shard_map.98 = (bf16[20,8,16,768]{3,2,1,0:T(8,128)(2,1)S(1)}, f32[8,4,16,192]{3,2,1,0:T(8,128)S(1)}) custom-call(f32[8,16,128]{2,1,0:T(8,128)S(1)} %get-tuple-element.374.mask, bf16[4,16,3072]{2,1,0:T(8,128)(2,1)S(1)} %collective-permute-done.11.prev, f32[192]{0:T(256)S(1)} %copy-done.3, ...), custom_call_target="tpu_custom_call", output_to_operand_aliasing={{0}: (4, {})} | custom-call | flops 1528823808 | bytes 196608 | tf_op jit(solution)/shard_map/pallas_call | solution.py:463
  26.6 0.0 copy-done.6
  26.7 0.0 copy-start
  26.7 0.0 copy-start.7
  26.7 5.0 %shard_map.99 = (bf16[18,6,16,768]{3,2,1,0:T(8,128)(2,1)S(1)}, bf16[4,16,2304]{2,1,0:T(8,128)(2,1)S(1)}) custom-call(f32[8,16,128]{2,1,0:T(8,128)S(1)} %get-tuple-element.374.mask, bf16[4,16,3072]{2,1,0:T(8,128)(2,1)S(1)} %get-tuple-element.373.own, bf16[20,8,16,768]{3,2,1,0:T(8,128)(2,1)S(1)} %get-tuple-element.386.buf1, ...), custom_call_target="tpu_custom_call", output_to_operand_aliasing={{0}: (9, {})} | custom-call | flops 4076863488 | bytes 196608 | tf_op jit(solution)/shard_map/pallas_call | solution.py:463
  31.6 0.0 collective-permute-done.10
  31.7 0.0 copy-done
  31.7 0.0 copy-done.7
  31.7 4.0 %conditional.3 = ((bf16[4,1,16,3072]{3,2,0,1:T(8,128)(2,1)})) conditional(s32[]{:T(128)} %bitcast.58, (s32[19]{0:T(128)S(4)}, bf16[4,16,3072]{2,1,0:T(8,128)(2,1)S(1)}, bf16[2,4,16,384]{3,2,1,0:T(8,128)(2,1)S(1)}, bf16[2,4,16,384]{3,2,1,0:T(8,128)(2,1)S(1)}, f32[192]{0:T(256)S(1)}, /*index=5*/bf16[9,768,192]{2,1,0:T(8,128)(2,1)S(1)}, ...), branch_computations={%region_0.0_spmd, %region_1.12_spmd} | conditional | flops 483940256 | bytes 51179728 | solution.py:572
  31.9 3.8 %branch_0_fun.1 = (bf16[20,8,16,768]{3,2,1,0:T(8,128)(2,1)S(1)}, bf16[18,6,16,768]{3,2,1,0:T(8,128)(2,1)S(1)}, bf16[4,16,3072]{2,1,0:T(8,128)(2,1)}) custom-call(s32[19]{0:T(128)S(4)} %get-tuple-element.303.beside, bf16[4,16,3072]{2,1,0:T(8,128)(2,1)S(1)} %get-tuple-element.304.own, ...), custom_call_target="tpu_custom_call", output_to_operand_aliasing={{0}: (10, {}), {1}: (11, {})} | custom-call | flops 196608000 | bytes 196608 | tf_op jit(solution)/shard_map/cond/branch_0_fun/pallas_call | solution.py:463
  (1 shorter events, 0.0 us)
Async XLA Ops:
  0.0 23.1 %collective-permute-start.11 = (bf16[4,16,3072]{2,1,0:T(8,128)(2,1)}, bf16[4,16,3072]{2,1,0:T(8,128)(2,1)S(1)}, u32[]{:S(2)}, u32[]{:S(2)}) collective-permute-start(bf16[4,16,3072]{2,1,0:T(8,128)(2,1)} %bitcast.183), channel_id=1, source_target_pairs={{0,8},{8,16},{16,24},{1,9},{9,17},{17,25},{2,10},{10,18},{18,26},{... | collective-permute-start | bytes 1179656 | tf_op jit(solution)/shard_map/ppermute | solution.py:16
  3.6 5.5 %collective-permute-start.6 = (bf16[2,4,16,384]{3,2,1,0:T(8,128)(2,1)S(1)}, bf16[2,4,16,384]{3,2,1,0:T(8,128)(2,1)S(1)}, u32[]{:S(2)}, u32[]{:S(2)}) collective-permute-start(bf16[2,4,16,384]{3,2,1,0:T(8,128)(2,1)S(1)} %get-tuple-element.380.mine), channel_id=1, source_target_pairs={{0,1},{1,0},{2,3},{3,2},{4,5},{5,4},{6,7},{7,6},{8,9},{9,8},{10,11... | collective-permute-start | bytes 294920 | tf_op jit(solution)/shard_map/ppermute | solution.py:437
  6.0 9.0 %copy-start.2 = (s32[8,8]{1,0:T(8,128)S(1)}, s32[8,8]{1,0:T(8,128)}, u32[]{:S(2)}) copy-start(s32[8,8]{1,0:T(8,128)} %nb.1) | copy-start | bytes 772
  6.0 9.0 %copy-start.4 = (f32[192]{0:T(256)S(1)}, f32[192]{0:T(256)}, u32[]{:S(2)}) copy-start(f32[192]{0:T(256)} %bias1.3) | copy-start | bytes 2308
  6.0 9.0 %copy-start.5 = (f32[192]{0:T(256)S(1)}, f32[192]{0:T(256)}, u32[]{:S(2)}) copy-start(f32[192]{0:T(256)} %gain2.3) | copy-start | bytes 2308
  9.2 8.2 %collective-permute-start.7 = (bf16[2,4,16,384]{3,2,1,0:T(8,128)(2,1)S(1)}, bf16[2,4,16,384]{3,2,1,0:T(8,128)(2,1)S(1)}, u32[]{:S(2)}, u32[]{:S(2)}) collective-permute-start(bf16[2,4,16,384]{3,2,1,0:T(8,128)(2,1)S(1)} %get-tuple-element.381), channel_id=1, source_target_pairs={{0,2},{1,3},{2,4},{3,5},{4,6},{5,7},{6,0},{7,1},{8,10},{9,11},{10,... | collective-permute-start | bytes 294920 | tf_op jit(solution)/shard_map/ppermute | solution.py:449
  11.0 10.0 %collective-permute-start.8 = (bf16[2,4,16,384]{3,2,1,0:T(8,128)(2,1)S(1)}, bf16[2,4,16,384]{3,2,1,0:T(8,128)(2,1)S(1)}, u32[]{:S(2)}, u32[]{:S(2)}) collective-permute-start(bf16[2,4,16,384]{3,2,1,0:T(8,128)(2,1)S(1)} %get-tuple-element.382), channel_id=1, source_target_pairs={{0,4},{1,5},{2,6},{3,7},{4,0},{5,1},{6,2},{7,3},{8,12},{9,13},{10,... | collective-permute-start | bytes 294920 | tf_op jit(solution)/shard_map/ppermute | solution.py:449
  13.6 7.4 %collective-permute-start.9 = (bf16[2,4,16,384]{3,2,1,0:T(8,128)(2,1)S(1)}, bf16[2,4,16,384]{3,2,1,0:T(8,128)(2,1)S(1)}, u32[]{:S(2)}, u32[]{:S(2)}) collective-permute-start(bf16[2,4,16,384]{3,2,1,0:T(8,128)(2,1)S(1)} %get-tuple-element.383), channel_id=1, source_target_pairs={{0,6},{1,7},{2,0},{3,1},{4,2},{5,3},{6,4},{7,5},{8,14},{9,15},{10,... | collective-permute-start | bytes 294920 | tf_op jit(solution)/shard_map/ppermute | solution.py:449
  15.0 8.1 %copy-start.3 = (f32[192]{0:T(256)S(1)}, f32[192]{0:T(256)}, u32[]{:S(2)}) copy-start(f32[192]{0:T(256)} %gain1.3) | copy-start | bytes 2308
  21.1 10.6 %collective-permute-start.10 = (bf16[2,4,16,384]{3,2,1,0:T(8,128)(2,1)S(1)}, bf16[2,4,16,384]{3,2,1,0:T(8,128)(2,1)S(1)}, u32[]{:S(2)}, u32[]{:S(2)}) collective-permute-start(bf16[2,4,16,384]{3,2,1,0:T(8,128)(2,1)S(1)} %shard_map.97), channel_id=1, source_target_pairs={{0,8},{8,16},{16,24},{1,9},{9,17},{17,25},{2,10},{10,18},{18,26},{... | collective-permute-start | bytes 294920 | tf_op jit(solution)/shard_map/ppermute | solution.py:16
  23.1 3.6 %copy-start.6 = (f32[192]{0:T(256)S(1)}, f32[192]{0:T(256)}, u32[]{:S(2)}) copy-start(f32[192]{0:T(256)} %bias2.1) | copy-start | bytes 2308
  26.7 5.0 %copy-start = (bf16[4,1,16,3072]{3,2,1,0:T(8,128)(2,1)S(1)}, bf16[4,1,16,3072]{3,2,1,0:T(8,128)(2,1)}, u32[]{:S(2)}) copy-start(bf16[4,1,16,3072]{3,2,1,0:T(8,128)(2,1)} %param.19) | copy-start | bytes 1179652
  26.7 5.0 %copy-start.7 = (s32[8]{0:T(128)S(1)}, s32[8]{0:T(128)}, u32[]{:S(2)}) copy-start(s32[8]{0:T(128)} %far_vf.1) | copy-start | bytes 100
